TPU v7x, 128 devices: a whole 4x4x4 slice. The times are simulated.
128 devices in a mesh: lat: 8 (over x, core), lon: 16 (over z, y).
Axes of the slice: x: 4, y: 4, z: 4, core: 2. Of those that a mesh axis runs over, the one named last changes fastest.
Arguments:
- background: float32 [12, 256, 2048], P(None, 'lat', 'lon'), may hold values from -6 to 6
- wind_lon: float32 [12, 256, 2048], P(None, 'lat', 'lon'), may hold values from -0.4 to 0.4
- wind_lat: float32 [12, 256, 2048], P(None, 'lat', 'lon'), may hold values from -0.3 to 0.3
- obs_value: float32 [262144], P(('lat', 'lon')), may hold values from -6 to 6
- obs_weight: float32 [262144], P(('lat', 'lon')), may hold values from 0.25 to 4
- obs_tile: int32 [262144, 1], P(('lat', 'lon')), may hold values from 0 to 127; in each aligned block of 2048 rows (0 to 2047, 2048 to 4095, ...) at most 32 rows name the same one
- obs_cell: int32 [262144], P(('lat', 'lon')), may hold values from 0 to 49151
- obs_step: int32 [262144], P(('lat', 'lon')), may hold values from 1 to 4
- obs_count: int32 [128], P(('lat', 'lon')), may hold values from 512 to 2048, as said below
Outputs:
- increment: float32 [12, 256, 2048], P(None, 'lat', 'lon')
- residual: float32 [12, 256, 2048], P(None, 'lat', 'lon')
Inputs may be any that keep to these rules, and one draw needn't show every extreme that they name: `obs_tile`: counted with lat slowest. Among the 2048 slots of one device at most 32 name the same tile, and in every draw some tile is named by exactly 32 slots of one device. `obs_cell`: level slowest, then latitude row, then longitude column within the tile. `obs_count`: slots of a device at or beyond its count are unused; in every draw some device has all 2048 slots live.
All inputs are finite; a program needn't handle non-finite values.
Results may differ from a plain program's by a relative error of at most 0.0012.
Values sent between devices are 32-bit elements; how exact they have to be, the bound alone decides.
No kernel may reach another device: no remote copies, remote signals or barrier semaphores. Data moves between devices by JAX's collectives and lax.ppermute only.
A program may use at most 64 MiB of HBM per device.

v0:
```python
import jax
import jax.numpy as jnp
from jax import lax
from jax.sharding import PartitionSpec as P

STEPS = 4
ITERS = 2


shear_rate = 0.2
diffusion = 0.08


def with_halo(array, sides, width, wrap):
    for axis, dim in sides:
        size, length = (lax.axis_size(axis), array.shape[dim])
        up = [(i, (i + 1) % size) for i in range(size if wrap else size - 1)]
        down = [(j, i) for i, j in up]
        last = lax.slice_in_dim(array, length - width, length, axis=dim)
        initial = lax.slice_in_dim(array, 0, width, axis=dim)
        before = lax.ppermute(last, axis, up)
        after = lax.ppermute(initial, axis, down)
        array = jnp.concatenate([before, array, after], axis=dim)
    return array


def extend(source):
    banded = with_halo(source, (("lat", 1),), 1, False)
    return with_halo(banded, (("lon", 2),), 1, True)


def along_lon(padded):
    return 0.5 * (padded[:, 1:-1, 2:] - padded[:, 1:-1, :-2])


def along_lat(padded):
    return 0.5 * (padded[:, 2:, 1:-1] - padded[:, :-2, 1:-1])


def spread(padded):
    return (
        padded[:, 2:, 1:-1]
        + padded[:, :-2, 1:-1]
        + padded[:, 1:-1, 2:]
        + padded[:, 1:-1, :-2]
        - 4.0 * padded[:, 1:-1, 1:-1]
    )


def squares(residual):
    return lax.psum(jnp.sum(residual * residual), ("lat", "lon"))


def on_device(
    background, wind_lon, wind_lat, obs_value, obs_weight, obs_tile, obs_cell, obs_step, obs_count
):
    levels = background.shape[0]
    devices = lax.axis_size(("lat", "lon"))
    per_device = obs_value.shape[0]
    room = max(2, 2 * per_device // devices)
    live = jnp.arange(per_device, dtype=jnp.int32) < obs_count[0]
    target = obs_tile[:, 0]
    member = (target[:, None] == jnp.arange(devices, dtype=jnp.int32)[None, :]).astype(jnp.int32)
    place = jnp.sum(jnp.cumsum(member, axis=0) * member, axis=1) - 1
    where_to = target * room + place
    packed = jnp.stack(
        [
            obs_cell.astype(jnp.float32),
            obs_step.astype(jnp.float32),
            obs_value,
            jnp.where(live, obs_weight, 0.0),
        ]
    )
    outgoing = jnp.zeros((4, devices * room), jnp.float32).at[:, where_to].set(packed)
    arrived = lax.all_to_all(
        outgoing.reshape(4, devices, room), ("lat", "lon"), split_axis=1, concat_axis=1, tiled=True
    )
    arrived = arrived.reshape(4, devices * room)
    cells = arrived[0].astype(jnp.int32)
    steps_seen = arrived[1].astype(jnp.int32)
    values = arrived[2]
    weights = arrived[3]
    drifts = []
    gains = []
    state = background
    observed = jnp.zeros_like(values)
    for moment in range(STEPS):
        padded = extend(state)
        drift = wind_lon + shear_rate * state
        drifts.append(drift)
        gains.append(1.0 - shear_rate * along_lon(padded))
        state = (
            state
            - drift * along_lon(padded)
            - wind_lat * along_lat(padded)
            + diffusion * spread(padded)
        )
        observed = observed + jnp.where(steps_seen == moment + 1, state.reshape(-1)[cells], 0.0)
    departures = values - observed

    def backward_adjoint(amounts):
        adjoint = jnp.zeros_like(background)
        for moment in reversed(range(STEPS)):
            adjoint = (
                adjoint.reshape(-1)
                .at[cells]
                .add(jnp.where(steps_seen == moment + 1, amounts, 0.0))
                .reshape(background.shape)
            )
            stacked = extend(
                jnp.concatenate([adjoint, drifts[moment] * adjoint, wind_lat * adjoint], axis=0)
            )
            plain_pad = stacked[:levels]
            drift_pad = stacked[levels : 2 * levels]
            merid_pad = stacked[2 * levels :]
            adjoint = (
                gains[moment] * adjoint
                + along_lon(drift_pad)
                + along_lat(merid_pad)
                + diffusion * spread(plain_pad)
            )
        return adjoint

    gradient = backward_adjoint(weights * departures)
    increment = jnp.zeros_like(background)
    residual = gradient
    direction = gradient
    norm_now = squares(residual)
    for repeat in range(ITERS):
        moving = direction
        seen = jnp.zeros_like(values)
        for forward_moment in range(STEPS):
            forward_padded = extend(moving)
            moving = (
                gains[forward_moment] * moving
                - drifts[forward_moment] * along_lon(forward_padded)
                - wind_lat * along_lat(forward_padded)
                + diffusion * spread(forward_padded)
            )
            seen = seen + jnp.where(
                steps_seen == forward_moment + 1, moving.reshape(-1)[cells], 0.0
            )
        image = direction + backward_adjoint(weights * seen)
        alpha = norm_now / lax.psum(jnp.sum(direction * image), ("lat", "lon"))
        increment = increment + alpha * direction
        residual = residual - alpha * image
        norm_next = squares(residual)
        direction = residual + norm_next / norm_now * direction
        norm_now = norm_next
    return (increment, residual)


def solution(mesh):
    return jax.shard_map(
        on_device,
        mesh=mesh,
        in_specs=(
            P(None, "lat", "lon"),
            P(None, "lat", "lon"),
            P(None, "lat", "lon"),
            P(("lat", "lon")),
            P(("lat", "lon")),
            P(("lat", "lon"), None),
            P(("lat", "lon")),
            P(("lat", "lon")),
            P(("lat", "lon")),
        ),
        out_specs=(P(None, "lat", "lon"), P(None, "lat", "lon")),
        check_vma=False,
    )
```

profile of v0, /device:TPU:1, one launch (start us, length us, event | category | flops | bytes accessed | tf_op | source)
XLA Modules:
  0.0 1283.7 jit_solution(1401726688508193071)
XLA Ops:
  110.2 23.0 %gather_fusion.3 = f32[4096]{0:T(1024)S(1)} fusion(f32[49152]{0:T(1024)S(1)} %bitcast.111, s32[4096]{0:T(1024)S(1)} %broadcast_clamp_fusion), kind=kCustom, calls=%fused_computation.3 | custom fusion | bytes 49152 | tf_op jit(solution)/shard_map/gather | solution.py:98
  133.2 23.0 %gather_fusion.2 = f32[4096]{0:T(1024)S(1)} fusion(f32[49152]{0:T(1024)S(1)} %bitcast.104, s32[4096]{0:T(1024)S(1)} %broadcast_clamp_fusion), kind=kCustom, calls=%fused_computation.2 | custom fusion | bytes 49152 | tf_op jit(solution)/shard_map/gather | solution.py:98
  156.3 23.0 %gather_fusion.1 = f32[4096]{0:T(1024)S(1)} fusion(f32[49152]{0:T(1024)S(1)} %bitcast.103, s32[4096]{0:T(1024)S(1)} %broadcast_clamp_fusion), kind=kCustom, calls=%fused_computation.1 | custom fusion | bytes 49152 | tf_op jit(solution)/shard_map/gather | solution.py:98
  179.3 23.0 %gather_fusion = f32[4096]{0:T(1024)S(1)} fusion(f32[49152]{0:T(1024)S(1)} %bitcast.102, s32[4096]{0:T(1024)S(1)} %broadcast_clamp_fusion), kind=kCustom, calls=%fused_computation | custom fusion | bytes 49152 | tf_op jit(solution)/shard_map/gather | solution.py:98
  202.9 23.4 %scatter_custom_fusion.1 = f32[49152]{0:T(1024)S(1)} fusion(s32[4096]{0:T(1024)S(1)} %bitcast.128, f32[4096]{0:T(1024)S(1)} %get-tuple-element.165, f32[]{:T(128)} %constant.10.clone.1), kind=kCustom, calls=%fused_computation.529 | custom fusion | flops 4096 | bytes 196612 | tf_op jit(solution)/shard_map/scatter-add | solution.py:107
  248.3 24.1 %scatter_fusion = f32[49152]{0:T(1024)S(1)} fusion(f32[49152]{0:T(1024)S(1)} %bitcast.92, s32[4096]{0:T(1024)S(1)} %bitcast.129, f32[4096]{0:T(1024)S(1)} %get-tuple-element.164), kind=kCustom, calls=%fused_computation.14 | custom fusion | flops 4096 | bytes 65536 | tf_op jit(solution)/shard_map/scatter-add | solution.py:107
  294.8 24.3 %scatter_fusion.1 = f32[49152]{0:T(1024)S(1)} fusion(f32[49152]{0:T(1024)S(1)} %bitcast.67, s32[4096]{0:T(1024)S(1)} %bitcast.130, f32[4096]{0:T(1024)S(1)} %get-tuple-element.163), kind=kCustom, calls=%fused_computation.15 | custom fusion | flops 4096 | bytes 65536 | tf_op jit(solution)/shard_map/scatter-add | solution.py:107
  341.7 24.1 %scatter_fusion.2 = f32[49152]{0:T(1024)S(1)} fusion(f32[49152]{0:T(1024)S(1)} %bitcast.72, s32[4096]{0:T(1024)S(1)} %bitcast.131, f32[4096]{0:T(1024)S(1)} %get-tuple-element.21), kind=kCustom, calls=%fused_computation.16 | custom fusion | flops 4096 | bytes 65536 | tf_op jit(solution)/shard_map/scatter-add | solution.py:107
  478.7 23.0 %gather_fusion.5 = f32[4096]{0:T(1024)S(1)} fusion(f32[49152]{0:T(1024)S(1)} %bitcast.107, s32[4096]{0:T(1024)S(1)} %broadcast_clamp_fusion), kind=kCustom, calls=%fused_computation.5 | custom fusion | bytes 49152 | tf_op jit(solution)/shard_map/gather | solution.py:141
  501.8 23.0 %gather_fusion.6 = f32[4096]{0:T(1024)S(1)} fusion(f32[49152]{0:T(1024)S(1)} %bitcast.109, s32[4096]{0:T(1024)S(1)} %broadcast_clamp_fusion), kind=kCustom, calls=%fused_computation.6 | custom fusion | bytes 49152 | tf_op jit(solution)/shard_map/gather | solution.py:141
  525.1 23.0 %gather_fusion.7 = f32[4096]{0:T(1024)S(1)} fusion(f32[49152]{0:T(1024)S(1)} %bitcast.113, s32[4096]{0:T(1024)S(1)} %broadcast_clamp_fusion), kind=kCustom, calls=%fused_computation.7 | custom fusion | bytes 49152 | tf_op jit(solution)/shard_map/gather | solution.py:141
  548.2 23.4 %scatter_custom_fusion.5 = f32[49152]{0:T(1024)S(1)} fusion(s32[4096]{0:T(1024)S(1)} %bitcast.132, f32[4096]{0:T(1024)S(1)} %get-tuple-element.162, f32[]{:T(128)} %constant.10.clone.1), kind=kCustom, calls=%fused_computation.527 | custom fusion | flops 4096 | bytes 196612 | tf_op jit(solution)/shard_map/scatter-add | solution.py:107
  595.5 24.1 %scatter_fusion.3 = f32[49152]{0:T(1024)S(1)} fusion(f32[49152]{0:T(1024)S(1)} %bitcast.97, s32[4096]{0:T(1024)S(1)} %bitcast.133, f32[4096]{0:T(1024)S(1)} %get-tuple-element.161), kind=kCustom, calls=%fused_computation.18 | custom fusion | flops 4096 | bytes 65536 | tf_op jit(solution)/shard_map/scatter-add | solution.py:107
  642.1 24.1 %scatter_fusion.4 = f32[49152]{0:T(1024)S(1)} fusion(f32[49152]{0:T(1024)S(1)} %bitcast.77, s32[4096]{0:T(1024)S(1)} %bitcast.134, f32[4096]{0:T(1024)S(1)} %get-tuple-element.160), kind=kCustom, calls=%fused_computation.19 | custom fusion | flops 4096 | bytes 65536 | tf_op jit(solution)/shard_map/scatter-add | solution.py:107
  689.3 24.1 %scatter_fusion.5 = f32[49152]{0:T(1024)S(1)} fusion(f32[49152]{0:T(1024)S(1)} %bitcast.82, s32[4096]{0:T(1024)S(1)} %bitcast.135, f32[4096]{0:T(1024)S(1)} %get-tuple-element.19), kind=kCustom, calls=%fused_computation.20 | custom fusion | flops 4096 | bytes 65536 | tf_op jit(solution)/shard_map/scatter-add | solution.py:107
  737.0 63.1 %all-reduce = (f32[]{:T(128)}, f32[]{:T(128)}) all-reduce(f32[]{:T(128)} %get-tuple-element.11, f32[]{:T(128)} %get-tuple-element.10), channel_id=1, replica_groups=mesh['lat'=8,'lon'=16] {'lat','lon'}, use_global_device_ids=true, to_apply=%region_9.10 | all-reduce | flops 2 | bytes 16 | tf_op jit(solution)/shard_map/psum | solution.py:51
  802.0 63.0 %psum.30 = f32[]{:T(128)} all-reduce(f32[]{:T(128)} %multiply_reduce_fusion.1), channel_id=1, replica_groups=mesh['lat'=8,'lon'=16] {'lat','lon'}, use_global_device_ids=true, to_apply=%region_17.18 | all-reduce | flops 1 | bytes 8 | tf_op jit(solution)/shard_map/psum | solution.py:51
  982.8 23.0 %gather_fusion.10 = f32[4096]{0:T(1024)S(1)} fusion(f32[49152]{0:T(1024)S(1)} %bitcast.110, s32[4096]{0:T(1024)S(1)} %broadcast_clamp_fusion), kind=kCustom, calls=%fused_computation.10 | custom fusion | bytes 49152 | tf_op jit(solution)/shard_map/gather | solution.py:141
  1006.1 23.0 %gather_fusion.11 = f32[4096]{0:T(1024)S(1)} fusion(f32[49152]{0:T(1024)S(1)} %bitcast.112, s32[4096]{0:T(1024)S(1)} %broadcast_clamp_fusion), kind=kCustom, calls=%fused_computation.11 | custom fusion | bytes 49152 | tf_op jit(solution)/shard_map/gather | solution.py:141
  1029.2 23.4 %scatter_custom_fusion.9 = f32[49152]{0:T(1024)S(1)} fusion(s32[4096]{0:T(1024)S(1)} %bitcast.136, f32[4096]{0:T(1024)S(1)} %get-tuple-element.159, f32[]{:T(128)} %constant.10.clone.1), kind=kCustom, calls=%fused_computation.525 | custom fusion | flops 4096 | bytes 196612 | tf_op jit(solution)/shard_map/scatter-add | solution.py:107
  1076.5 24.1 %scatter_fusion.6 = f32[49152]{0:T(1024)S(1)} fusion(f32[49152]{0:T(1024)S(1)} %bitcast.87, s32[4096]{0:T(1024)S(1)} %bitcast.137, f32[4096]{0:T(1024)S(1)} %get-tuple-element.158), kind=kCustom, calls=%fused_computation.22 | custom fusion | flops 4096 | bytes 65536 | tf_op jit(solution)/shard_map/scatter-add | solution.py:107
  1122.5 24.1 %scatter_fusion.7 = f32[49152]{0:T(1024)S(1)} fusion(f32[49152]{0:T(1024)S(1)} %bitcast.62, s32[4096]{0:T(1024)S(1)} %bitcast.138, f32[4096]{0:T(1024)S(1)} %get-tuple-element.157), kind=kCustom, calls=%fused_computation.23 | custom fusion | flops 4096 | bytes 65536 | tf_op jit(solution)/shard_map/scatter-add | solution.py:107
  1173.6 24.1 %scatter_fusion.8 = f32[49152]{0:T(1024)S(1)} fusion(f32[49152]{0:T(1024)S(1)} %bitcast.57, s32[4096]{0:T(1024)S(1)} %bitcast.139, f32[4096]{0:T(1024)S(1)} %get-tuple-element.16), kind=kCustom, calls=%fused_computation.24 | custom fusion | flops 4096 | bytes 65536 | tf_op jit(solution)/shard_map/scatter-add | solution.py:107
  1218.2 63.1 %psum.31 = f32[]{:T(128)} all-reduce(f32[]{:T(128)} %get-tuple-element.14), channel_id=1, replica_groups=mesh['lat'=8,'lon'=16] {'lat','lon'}, use_global_device_ids=true, to_apply=%region_23.24 | all-reduce | flops 1 | bytes 8 | tf_op jit(solution)/shard_map/psum | solution.py:144
  (443 shorter events, 592.4 us)
Async XLA Ops:
  1.6 7.6 collective-permute-start
  12.1 10.6 collective-permute-start.2
  18.4 9.9 collective-permute-start.3
  38.5 6.6 collective-permute-start.6
  38.6 9.7 collective-permute-start.7
  57.9 6.6 collective-permute-start.10
  58.0 9.7 collective-permute-start.11
  78.2 19.2 %collective-permute-start.14 = (f32[12,34,1]{2,1,0:T(8,128)}, f32[12,34,1]{2,1,0:T(8,128)}, u32[]{:S(2)}, u32[]{:S(2)}) collective-permute-start(f32[12,34,1]{2,1,0:T(8,128)} %get-tuple-element.100), channel_id=1, source_target_pairs={{1,0},{2,1},{3,2},{4,3},{5,4},{6,5},{7,6},{8,7},{9,8},{10,9},{11,1... | collective-permute-start | bytes 4904 | tf_op jit(solution)/shard_map/ppermute | solution.py:22
  78.2 19.2 %collective-permute-start.15 = (f32[12,34,1]{2,1,0:T(8,128)}, f32[12,34,1]{2,1,0:T(8,128)}, u32[]{:S(2)}, u32[]{:S(2)}) collective-permute-start(f32[12,34,1]{2,1,0:T(8,128)} %get-tuple-element.99), channel_id=1, source_target_pairs={{0,1},{1,2},{2,3},{3,4},{4,5},{5,6},{6,7},{7,8},{8,9},{9,10},{10,1... | collective-permute-start | bytes 4904 | tf_op jit(solution)/shard_map/ppermute | solution.py:21
  90.8 16.4 %all-to-all-start = ((f32[128,1,128]{2,1,0:T(1,128)}), f32[128,1,128]{2,1,0:T(1,128)S(1)}, u32[]{:S(2)}, u32[]{:S(2)}) async-start(f32[128,1,128]{2,1,0:T(1,128)} %reshape.435), calls=%async_computation | async-start | bytes 131072 | tf_op jit(solution)/shard_map/all_to_all | solution.py:75
  396.8 6.6 collective-permute-start.34
  396.9 9.7 collective-permute-start.35
  415.2 6.6 collective-permute-start.38
  415.3 9.7 collective-permute-start.39
  434.5 9.7 collective-permute-start.43
  454.0 70.8 %collective-permute-start.46 = (f32[12,34,1]{2,1,0:T(8,128)}, f32[12,34,1]{2,1,0:T(8,128)S(1)}, u32[]{:S(2)}, u32[]{:S(2)}) collective-permute-start(f32[12,34,1]{2,1,0:T(8,128)} %get-tuple-element.92), channel_id=1, source_target_pairs={{1,0},{2,1},{3,2},{4,3},{5,4},{6,5},{7,6},{8,7},{9,8},{10,9},{11,1... | collective-permute-start | bytes 4904 | tf_op jit(solution)/shard_map/ppermute | solution.py:22
  454.0 70.8 %collective-permute-start.47 = (f32[12,34,1]{2,1,0:T(8,128)S(1)}, f32[12,34,1]{2,1,0:T(8,128)S(1)}, u32[]{:S(2)}, u32[]{:S(2)}) collective-permute-start(f32[12,34,1]{2,1,0:T(8,128)S(1)} %get-tuple-element.91), channel_id=1, source_target_pairs={{0,1},{1,2},{2,3},{3,4},{4,5},{5,6},{6,7},{7,8},{8,9},{9,10},{10,1... | collective-permute-start | bytes 4904 | tf_op jit(solution)/shard_map/ppermute | solution.py:21
  876.9 9.9 collective-permute-start.67
  895.7 9.9 collective-permute-start.71
  915.4 6.6 collective-permute-start.74
  915.5 9.7 collective-permute-start.75
  935.1 70.7 %collective-permute-start.78 = (f32[12,34,1]{2,1,0:T(8,128)}, f32[12,34,1]{2,1,0:T(8,128)S(1)}, u32[]{:S(2)}, u32[]{:S(2)}) collective-permute-start(f32[12,34,1]{2,1,0:T(8,128)} %get-tuple-element.84), channel_id=1, source_target_pairs={{1,0},{2,1},{3,2},{4,3},{5,4},{6,5},{7,6},{8,7},{9,8},{10,9},{11,1... | collective-permute-start | bytes 4904 | tf_op jit(solution)/shard_map/ppermute | solution.py:22
  935.1 70.7 %collective-permute-start.79 = (f32[12,34,1]{2,1,0:T(8,128)}, f32[12,34,1]{2,1,0:T(8,128)S(1)}, u32[]{:S(2)}, u32[]{:S(2)}) collective-permute-start(f32[12,34,1]{2,1,0:T(8,128)} %get-tuple-element.83), channel_id=1, source_target_pairs={{0,1},{1,2},{2,3},{3,4},{4,5},{5,6},{6,7},{7,8},{8,9},{9,10},{10,1... | collective-permute-start | bytes 4904 | tf_op jit(solution)/shard_map/ppermute | solution.py:21
  1158.2 6.8 collective-permute-start.90
  (97 other events, 995.2 us)
where the time goes:
time: 1290 us; the launch traced here: 1280 us
  local copies, waits for them, and re-layouts  368 us (29%)
  other arithmetic  321 us (25%)
  waiting for transfers between devices  205 us (16%)
  starting transfers between devices  192 us (15%)
  blocking collectives  189 us (15%)
    scatter-add x12, other arithmetic, backward_adjoint(): adjoint = adjoint.reshape(-1).at[cells].add(jnp.where(steps_seen == momen...  287 us
    gather x8, local copies, waits for them, and re-layouts, on_device(): moving.reshape(-1)[cells]  184 us
    psum x2, blocking collectives, squares(): return lax.psum(jnp.sum(residual * residual), ('lat', 'lon'))  126 us
    ppermute x48, waiting for transfers between devices, with_halo(): after = lax.ppermute(initial, axis, down)  119 us
    ppermute x48, starting transfers between devices, with_halo(): before = lax.ppermute(last, axis, up)  115 us
    gather x4, local copies, waits for them, and re-layouts, on_device(): state.reshape(-1)[cells]  92.1 us
    ppermute x48, waiting for transfers between devices, with_halo(): before = lax.ppermute(last, axis, up)  77.6 us
    ppermute x48, starting transfers between devices, with_halo(): after = lax.ppermute(initial, axis, down)  70.9 us
  transfers between devices with their start and end apart: 97, of which 56 were waited for; matrix products, arithmetic and copies ran while one was open for 14% of the time, Pallas kernels for 0%

commit v1 on v0

v1 whole, which is shorter than its diff:
```python
import jax
import jax.numpy as jnp
from jax import lax
from jax.experimental import pallas as pl
from jax.experimental.pallas import tpu as pltpu
from jax.sharding import PartitionSpec as P

LAT = 8
LON = 16
ALL = 128
STEPS = 4
LV = 3
COL = 64
EDGE = 8
EXT = COL + 2 * EDGE
ROOM = 256
ROWS = STEPS * LV * COL
F32 = jnp.float32
BF16 = jnp.bfloat16
I32 = jnp.int32


def lanes(shape):
    return lax.broadcasted_iota(I32, shape, len(shape) - 1)


def sublanes(shape):
    return lax.broadcasted_iota(I32, shape, len(shape) - 2)


def half():
    return lax.rem(lax.axis_index("lat"), 2)


def prep_kernel(bg, wl, wt, out):
    low = lanes((16, 128)) < 64
    for f, ref in enumerate((bg, wl, wt)):
        for level in range(12):
            q, l = level // 3, level % 3
            even = ref[level, pl.ds(0, 16, stride=2), :]
            odd = ref[level, pl.ds(1, 16, stride=2), :]
            out[2 * q, f * 3 + l] = jnp.where(low, even, pltpu.roll(odd, 64, 1))
            out[2 * q + 1, f * 3 + l] = jnp.where(low, pltpu.roll(even, 64, 1), odd)


def put_edges(sa, sb, index, lo, hi, h):
    @pl.when(h == 0)
    def _():
        sa[index] = hi
        sb[index] = lo

    @pl.when(h != 0)
    def _():
        sa[index] = lo
        sb[index] = hi


def get_edges(ra, rb, index, h):
    a, b = ra[index], rb[index]
    first = jnp.full(a.shape, h, I32) == 0
    return jnp.where(first, b, a), jnp.where(first, a, b)


def recv_kernel(x, center, sa, sb):
    h = half()
    for f in range(9):
        t = x[:, f].reshape(128, 128).T
        for u in range(2):
            center[f, u] = t[u * 64 : u * 64 + 64]
            put_edges(sa, sb, (f, u), t[u * 64 : u * 64 + 8], t[u * 64 + 56 : u * 64 + 64], h)


def up(x):
    return pltpu.roll(x, EXT - 1, 0)


def down(x):
    return pltpu.roll(x, 1, 0)


def north(e, o):
    return pltpu.roll(o, 1, 1), e


def south(e, o):
    return o, pltpu.roll(e, 127, 1)


def forward_kernel(center, ra, rb, states, gains, drifts, cn, cs):
    h = half()
    lane = lanes((EXT, 128))

    def ext(f, u):
        left, right = get_edges(ra, rb, (f, u), h)
        return jnp.concatenate([left, center[f, u], right], axis=0)

    for l in range(LV):
        s = [ext(l, u) for u in range(2)]
        wl = [ext(3 + l, u) for u in range(2)]
        wt = [ext(6 + l, u) for u in range(2)]
        n = [0.08 + 0.5 * wt[u] for u in range(2)]
        d = [0.08 - 0.5 * wt[u] for u in range(2)]
        n[0] = jnp.where(lane == 0, 0.0, n[0])
        d[1] = jnp.where(lane == 127, 0.0, d[1])
        for u in range(2):
            cn[l, u] = n[u]
            cs[l, u] = d[u]
        for k in range(STEPS):
            no, so = north(*s), south(*s)
            new = []
            for u in range(2):
                hi, lo = up(s[u]), down(s[u])
                drift = 0.5 * wl[u] + 0.1 * s[u]
                gains[k, l, u] = 0.68 - 0.1 * (hi - lo)
                drifts[k, l, u] = drift
                new.append(
                    0.68 * s[u] + 0.08 * (hi + lo) - drift * (hi - lo) + n[u] * no[u] + d[u] * so[u]
                )
            s = new
            for u in range(2):
                states[k, l, u] = s[u]


def tangent(e, g, d, n, s):
    no, so = north(*e), south(*e)
    out = []
    for u in range(2):
        hi, lo = up(e[u]), down(e[u])
        out.append(g[u] * e[u] + 0.08 * (hi + lo) - d[u] * (hi - lo) + n[u] * no[u] + s[u] * so[u])
    return out


def adjoint(x, g, d, n, s):
    no = north(s[0] * x[0], s[1] * x[1])
    so = south(n[0] * x[0], n[1] * x[1])
    out = []
    for u in range(2):
        flow = d[u] * x[u]
        wide = 0.08 * x[u]
        out.append(g[u] * x[u] + up(wide + flow) + down(wide - flow) + no[u] + so[u])
    return out


def pack_kernel(count, tile, cell, step, value, weight, out, rows, base, acc, bt):
    shape = (16, 128)
    live = sublanes(shape) * 128 + lanes(shape) < count[0]
    c, t = cell[...], tile[...]
    level = c >> 12
    q = (level >= 3).astype(I32) + (level >= 6).astype(I32) + (level >= 9).astype(I32)
    row = (c & 4095) >> 7
    col = c & 127
    lat = (t >> 4) * 32 + row
    dest = (2 * q + (col >> 6)) * LON + (t & 15)
    w = jnp.where(live, weight[...], 0.0)
    w0 = w.astype(BF16).astype(F32)
    w1 = (w - w0).astype(BF16).astype(F32)
    wv = (w0 + w1) * value[...]
    v0 = wv.astype(BF16).astype(F32)
    v1 = (wv - v0).astype(BF16).astype(F32)
    v2 = wv - v0 - v1
    zero = jnp.zeros(shape, F32)
    rows[0] = jnp.where(live, dest, -1).astype(F32)
    rows[1] = (((level - 3 * q) * 64 + (col & 63)) * 256).astype(F32)
    rows[2] = step[...].astype(F32)
    rows[3] = w0
    rows[4] = v0
    rows[5] = ((lat & 1) * 128 + (lat >> 1)).astype(F32)
    rows[6] = zero
    rows[7] = w1
    rows[8] = v1
    rows[9] = zero
    rows[10] = zero
    rows[11] = zero
    rows[12] = v2
    base[...] = jnp.zeros_like(base)
    acc[...] = jnp.zeros_like(acc)
    square = (128, 256)
    before = ((sublanes(square) < lanes(square)) | (lanes(square) >= 128)).astype(F32).astype(BF16)
    ids = sublanes((128, 128)).astype(F32)
    places = sublanes((ROOM, 128)).astype(F32)

    def block(b, carry):
        def line(i):
            return rows[i, pl.ds(b, 1), :]

        member = jnp.where(ids == line(0), 1.0, 0.0)
        member16 = member.astype(BF16)
        counted = jnp.dot(member16, before, preferred_element_type=F32)
        rank = jnp.sum(member * (counted[:, :128] + base[...]), axis=0, keepdims=True)
        base[...] += counted[:, 128:]
        here = places == rank
        for p in range(3):
            for ch in range(4):
                piece = jnp.where(here, line(1 + 4 * p + ch), 0.0).astype(BF16)
                for m in range(8):
                    at = m * 128 + ch * 32
                    bt[at : at + 32, p * 128 : p * 128 + 128] = piece[m * 32 : m * 32 + 32]
        three = jnp.concatenate([member16, member16, member16], axis=1)
        acc[...] += lax.dot_general(
            three, bt[...], (((1,), (1,)), ((), ())), preferred_element_type=F32
        )
        return carry

    lax.fori_loop(0, 16, block, 0)
    for m in range(8):
        out[:, m, :] = acc[:, m * 128 : m * 128 + 128]


def scatter_kernel(x, wsum, vsum, sa, sb, xt, at, bt, acc):
    h = half()
    most = jnp.max(x[...], axis=0)
    lane = lanes((8, 128))
    used = jnp.where((lane >= 32) & (lane < 64) & (most > 0.5), 1.0, 0.0)
    total = jnp.sum(used).astype(I32)
    acc[...] = jnp.zeros_like(acc)
    for m in range(8):

        @pl.when(total > 32 * m)
        def _():
            xt[m * 128 : m * 128 + 128, :] = x[:, m, :].T

    row_ids = sublanes((ROWS, 128))
    lat_ids = sublanes((256, 128))

    def group(g, carry):
        start = (g // 4) * 128 + (g % 4) * 8

        def part(ch):
            return xt[pl.ds(pl.multiple_of(start + ch * 32, 8), 8), :]

        cell = part(0).astype(I32)
        row = (part(1).astype(I32) - 1) * (LV * COL) + (cell >> 8)
        lat = cell & 255
        w = part(2)
        v = part(3)
        w0 = w.astype(BF16).astype(F32)
        w1 = w - w0
        v0 = v.astype(BF16).astype(F32)
        v1 = (v - v0).astype(BF16).astype(F32)
        v2 = v - v0 - v1
        for r in range(8):
            cols = slice(r * 128, r * 128 + 128)
            at[:, cols] = jnp.where(row_ids == row[r : r + 1], 1.0, 0.0).astype(BF16)
            here = lat_ids == lat[r : r + 1]
            for p, piece in enumerate((w0, w1, v0, v1, v2)):
                bt[p * 256 : p * 256 + 256, cols] = jnp.where(here, piece[r : r + 1], 0.0).astype(BF16)
        acc[...] += lax.dot_general(
            at[...], bt[...], (((1,), (1,)), ((), ())), preferred_element_type=F32
        )
        return carry

    lax.fori_loop(0, (total + 7) // 8, group, 0)
    low = sublanes((8, 128)) < 4
    for k in range(STEPS):
        for l in range(LV):
            for u in range(2):
                rows = slice((k * LV + l) * COL, (k * LV + l + 1) * COL)
                take = lambda p: acc[rows, p * 256 + u * 128 : p * 256 + u * 128 + 128]
                w = take(0) + take(1)
                v = take(2) + take(3) + take(4)
                wsum[k, l, u] = w
                vsum[k, l, u] = v
                lo = jnp.where(low, w[:8], pltpu.roll(v[:8], 4, 0))
                hi = jnp.where(low, pltpu.roll(v[56:], 4, 0), w[56:])
                put_edges(sa, sb, (k, l, u), lo, hi, h)


def keep(x, out, sa, sb, l, h):
    for u in range(2):
        out[l, u] = x[u][EDGE : EDGE + COL]
        put_edges(sa, sb, (l, u), x[u][EDGE : 2 * EDGE], x[u][COL : COL + EDGE], h)


def gradient_kernel(wsum, vsum, ra, rb, states, gains, drifts, cn, cs, wide, out, sa, sb):
    h = half()
    for l in range(LV):
        n = [cn[l, u] for u in range(2)]
        s = [cs[l, u] for u in range(2)]
        x = None
        for k in reversed(range(STEPS)):
            m = []
            for u in range(2):
                left, right = get_edges(ra, rb, (k, l, u), h)
                w = jnp.concatenate([left, wsum[k, l, u], right], axis=0)
                v = jnp.concatenate(
                    [pltpu.roll(left, 4, 0), vsum[k, l, u], pltpu.roll(right, 4, 0)], axis=0
                )
                wide[k, l, u] = w
                m.append(v - w * states[k, l, u])
            x = m if x is None else [x[u] + m[u] for u in range(2)]
            x = adjoint(
                x, [gains[k, l, u] for u in range(2)], [drifts[k, l, u] for u in range(2)], n, s
            )
        keep(x, out, sa, sb, l, h)


def hessian(l, p, wide, gains, drifts, cn, cs):
    n = [cn[l, u] for u in range(2)]
    s = [cs[l, u] for u in range(2)]
    g = lambda k: [gains[k, l, u] for u in range(2)]
    d = lambda k: [drifts[k, l, u] for u in range(2)]
    e, seen = p, []
    for k in range(STEPS):
        e = tangent(e, g(k), d(k), n, s)
        seen.append([wide[k, l, u] * e[u] for u in range(2)])
    x = None
    for k in reversed(range(STEPS)):
        x = seen[k] if x is None else [x[u] + seen[k][u] for u in range(2)]
        x = adjoint(x, g(k), d(k), n, s)
    return [p[u] + x[u] for u in range(2)]


def extended(center, ra, rb, l, h):
    out = []
    for u in range(2):
        left, right = get_edges(ra, rb, (l, u), h)
        out.append(jnp.concatenate([left, center[l, u], right], axis=0))
    return out


def hessian_kernel(center, ra, rb, wide, gains, drifts, cn, cs, out, sa, sb):
    h = half()
    for l in range(LV):
        p = extended(center, ra, rb, l, h)
        keep(hessian(l, p, wide, gains, drifts, cn, cs), out, sa, sb, l, h)


def last_kernel(g, center, ra, rb, wide, gains, drifts, cn, cs, out):
    h = half()
    sums = [jnp.zeros((8, 128), F32) for _ in range(5)]

    def fold(a, b):
        prod = a * b
        return jnp.sum(prod.reshape(8, 8, 128), axis=0)

    for l in range(LV):
        p = extended(center, ra, rb, l, h)
        y = hessian(l, p, wide, gains, drifts, cn, cs)
        v = [
            [g[l, u] for u in range(2)],
            [center[l, u] for u in range(2)],
            [y[u][EDGE : EDGE + COL] for u in range(2)],
        ]
        for i, (a, b) in enumerate(((0, 0), (0, 1), (1, 1), (0, 2), (1, 2))):
            for u in range(2):
                sums[i] = sums[i] + fold(v[a][u], v[b][u])
        for i in range(3):
            t = jnp.concatenate(v[i], axis=0).T.reshape(LAT, 16, 128)
            out[:, i * 3 + l] = t
    row = sublanes((16, 128))
    table = jnp.zeros((16, 128), F32)
    for i in range(5):
        table = jnp.where(row == i, jnp.sum(sums[i], axis=0, keepdims=True), table)
    for b in range(LAT):
        out[b, 9] = table


def final_kernel(x, parts, increment, residual):
    total = jnp.sum(parts[...], axis=0)
    total = jnp.broadcast_to(jnp.sum(total, axis=1, keepdims=True), (8, 128))
    a00, a01, a11, a02, a12 = [total[i : i + 1] for i in range(5)]
    alpha = a00 / a01
    new = a00 - 2.0 * alpha * a01 + alpha * alpha * a11
    keep1 = 1.0 + new / a00
    curve = keep1 * (keep1 * a01 - alpha * (a02 + a11)) + alpha * alpha * a12
    second = new / curve
    a = alpha + second * keep1
    b = alpha * second
    low = lanes((16, 128)) < 64
    for level in range(12):
        q, l = level // 3, level % 3
        got = []
        for h in range(2):
            v0, v1, v2 = [x[2 * q + h, i * 3 + l] for i in range(3)]
            got.append((a * v0 - b * v1, v0 - a * v1 + b * v2))
        for i, ref in enumerate((increment, residual)):
            x0, x1 = got[0][i], got[1][i]
            ref[level, pl.ds(0, 16, stride=2), :] = jnp.where(low, x0, pltpu.roll(x1, 64, 1))
            ref[level, pl.ds(1, 16, stride=2), :] = jnp.where(low, pltpu.roll(x0, 64, 1), x1)


VM = pl.BlockSpec(memory_space=pltpu.VMEM)
SM = pl.BlockSpec(memory_space=pltpu.SMEM)


def call(kernel, outs, *args, scratch=(), scalars=0, flops=1000000):
    shapes = tuple(jax.ShapeDtypeStruct(s, F32) for s in outs)
    return pl.pallas_call(
        kernel,
        out_shape=shapes if len(shapes) > 1 else shapes[0],
        in_specs=[SM] * scalars + [VM] * (len(args) - scalars),
        out_specs=(VM,) * len(shapes) if len(shapes) > 1 else VM,
        scratch_shapes=list(scratch),
        name=kernel.__name__,
    )(*args)


def swap(sa, sb):
    near, far = [], []
    for i in range(LAT):
        for j in range(LON):
            me = i * LON + j
            near.append((me, (i ^ 1) * LON + j))
            other = (j + 1) % LON if i % 2 else (j - 1) % LON
            far.append((me, (i ^ 1) * LON + other))
    rb = lax.ppermute(sb, ("lat", "lon"), far)
    ra = lax.ppermute(sa, ("lat", "lon"), near)
    return ra, rb


def on_device(
    background, wind_lon, wind_lat, obs_value, obs_weight, obs_tile, obs_cell, obs_step, obs_count
):
    both = ("lat", "lon")
    plane = (LV, 2, EXT, 128)
    edge = (LV, 2, EDGE, 128)
    middle = (LV, 2, COL, 128)

    sent = call(prep_kernel, [(LAT, 9, 16, 128)], background, wind_lon, wind_lat)
    moved = lax.all_to_all(sent, "lat", 0, 0, tiled=True)
    fold = lambda a: a.reshape(16, 128)
    packed = call(
        pack_kernel,
        [(ALL, 8, 128)],
        obs_count,
        fold(obs_tile),
        fold(obs_cell),
        fold(obs_step),
        fold(obs_value),
        fold(obs_weight),
        scalars=1,
        scratch=[
            pltpu.VMEM((13, 16, 128), F32),
            pltpu.VMEM((128, 128), F32),
            pltpu.VMEM((128, 1024), F32),
            pltpu.VMEM((1024, 384), BF16),
        ],
    )
    fields, sa, sb = call(recv_kernel, [(9, 2, COL, 128)] + [(9, 2, EDGE, 128)] * 2, moved)
    ra, rb = swap(sa, sb)
    arrived = lax.all_to_all(packed, both, 0, 0, tiled=True)
    wsum, vsum, sa, sb = call(
        scatter_kernel,
        [(STEPS,) + middle] * 2 + [(STEPS,) + edge] * 2,
        arrived,
        scratch=[
            pltpu.VMEM((1024, 128), F32),
            pltpu.VMEM((ROWS, 1024), BF16),
            pltpu.VMEM((1280, 1024), BF16),
            pltpu.VMEM((ROWS, 1280), F32),
        ],
    )
    wa, wb = swap(sa, sb)
    states, gains, drifts, cn, cs = call(
        forward_kernel, [(STEPS,) + plane] * 3 + [plane] * 2, fields, ra, rb
    )
    wide, g, sa, sb = call(
        gradient_kernel,
        [(STEPS,) + plane, middle, edge, edge],
        wsum,
        vsum,
        wa,
        wb,
        states,
        gains,
        drifts,
        cn,
        cs,
    )
    ra, rb = swap(sa, sb)
    hg, sa, sb = call(
        hessian_kernel, [middle, edge, edge], g, ra, rb, wide, gains, drifts, cn, cs
    )
    ra, rb = swap(sa, sb)
    sent = call(
        last_kernel, [(LAT, 10, 16, 128)], g, hg, ra, rb, wide, gains, drifts, cn, cs
    )
    moved = lax.all_to_all(sent, "lat", 0, 0, tiled=True)
    mine = jnp.sum(moved[:, 9, :8], axis=0)
    parts = lax.all_to_all(
        jnp.broadcast_to(mine[None], (LON, 8, 128)), "lon", 0, 0, tiled=True
    )
    return call(final_kernel, [(12, 32, 128)] * 2, moved, parts)


def solution(mesh):
    grid = P(None, "lat", "lon")
    flat = P(("lat", "lon"))
    return jax.shard_map(
        on_device,
        mesh=mesh,
        in_specs=(grid, grid, grid, flat, flat, P(("lat", "lon"), None), flat, flat, flat),
        out_specs=(grid, grid),
        check_vma=False,
    )
```

time: 1290 us -> 133 us (0.10)
  local copies, waits for them, and re-layouts: 368 us -> 4.12 us
  other arithmetic: 321 us -> 0.01 us
  waiting for transfers between devices: 205 us -> 22.8 us
  starting transfers between devices: 192 us -> 29.5 us
  blocking collectives: 189 us -> 27.4 us
  Pallas kernels: 0 us -> 47.2 us
    scatter-add x12 -> x0, other arithmetic: 287 us -> none  [backward_adjoint(): adjoint = adjoint.reshape(-1).at[cells].add(jnp.where(steps_seen == momen...]
    gather x12 -> x0, local copies, waits for them, and re-layouts: 276 us -> none  [the longest x8 184 us: on_device(): moving.reshape(-1)[cells]]
    psum x3 -> x0, blocking collectives: 189 us -> none  [the longest x2 126 us: squares(): return lax.psum(jnp.sum(residual * residual), ('lat', 'lon'))]
    ppermute x96 -> x8, waiting for transfers between devices: 197 us -> 10.9 us  [the longest x4 7.67 us: swap(): rb = lax.ppermute(sb, ('lat', 'lon'), far)]
    ppermute x96 -> x8, starting transfers between devices: 186 us -> 14 us  [the longest x4 13.5 us: swap(): ra = lax.ppermute(sa, ('lat', 'lon'), near)]
    slice x61 -> x0, local copies, waits for them, and re-layouts: 55.5 us -> none  [the longest x24 33.8 us: with_halo(): initial = lax.slice_in_dim(array, 0, width, axis=dim)]
    pallas_call x0 -> x9, Pallas kernels: none -> 47.2 us  [call(): pl.pallas_call(kernel, out_shape=shapes if len(shapes) > 1 else shapes[0]...]
    all_to_all x0 -> x2, blocking collectives: none -> 27.4 us  [the longest x1 17.7 us: on_device(): moved = lax.all_to_all(sent, 'lat', 0, 0, tiled=True)]
  transfers between devices with their start and end apart: 97 -> 10, of which waited for: 56 -> 7; matrix products, arithmetic and copies ran while one was open for 14% -> 0% of each run, Pallas kernels for 0% -> 15%
where the time goes in v1:
time: 133 us; the launch traced here: 132 us
  Pallas kernels  47.2 us (35%)
  starting transfers between devices  29.5 us (22%)
  blocking collectives  27.4 us (21%)
  waiting for transfers between devices  22.8 us (17%)
  local copies, waits for them, and re-layouts  4.12 us (3%)
  between operations  1.34 us (1%)
    pallas_call x9, Pallas kernels, call(): pl.pallas_call(kernel, out_shape=shapes if len(shapes) > 1 else shapes[0]...  47.2 us
    all_to_all x1, blocking collectives, on_device(): moved = lax.all_to_all(sent, 'lat', 0, 0, tiled=True)  17.7 us
    ppermute x4, starting transfers between devices, swap(): ra = lax.ppermute(sa, ('lat', 'lon'), near)  13.5 us
    all_to_all x1, waiting for transfers between devices, on_device(): arrived = lax.all_to_all(packed, both, 0, 0, tiled=True)  11.9 us
    all_to_all x1, starting transfers between devices, on_device(): arrived = lax.all_to_all(packed, both, 0, 0, tiled=True)  11.5 us
    all_to_all x1, blocking collectives, on_device(): lax.all_to_all(jnp.broadcast_to(mine[None], (LON, 8, 128)), 'lon', 0, 0,...  9.78 us
    ppermute x4, waiting for transfers between devices, swap(): rb = lax.ppermute(sb, ('lat', 'lon'), far)  7.67 us
    unnamed x22, local copies, waits for them, and re-layouts  4.11 us
  transfers between devices with their start and end apart: 10, of which 7 were waited for; matrix products, arithmetic and copies ran while one was open for 0% of the time, Pallas kernels for 15%

profile of v1, /device:TPU:1, one launch (start us, length us, event | category | flops | bytes accessed | tf_op | source)
XLA Modules:
  0.0 132.4 jit_solution(12205336100848858495)
XLA Ops:
  1.3 11.5 %pack_kernel.1 = f32[128,8,128]{2,1,0:T(8,128)} custom-call(s32[1]{0:T(128)S(6)} %copy.11.count, s32[16,128]{1,0:T(8,128)} %bitcast.5, s32[16,128]{1,0:T(8,128)} %bitcast.6, s32[16,128]{1,0:T(8,128)} %bitcast.7, f32[16,128]{1,0:T(8,128)} %bitcast.8, f32[16,128]{1,0:T(8,128)} %bitcast.9), custom_call_target="tpu_custom_call" | custom-call | tf_op jit(solution)/shard_map/pack_kernel/pallas_call | solution.py:388
  12.8 11.5 %all-to-all-start = ((f32[128,8,128]{2,1,0:T(8,128)}), f32[128,8,128]{2,1,0:T(8,128)S(1)}, u32[]{:S(2)}, u32[]{:S(2)}) async-start(f32[128,8,128]{2,1,0:T(8,128)} %pack_kernel.1), calls=%async_computation | async-start | bytes 1048576 | tf_op jit(solution)/shard_map/all_to_all | solution.py:441
  24.3 2.2 %prep_kernel.1 = f32[8,9,16,128]{3,2,1,0:T(8,128)} custom-call(f32[12,32,128]{2,1,0:T(8,128)} %bg.1, f32[12,32,128]{2,1,0:T(8,128)} %wl.1, f32[12,32,128]{2,1,0:T(8,128)} %wt.1), custom_call_target="tpu_custom_call" | custom-call | tf_op jit(solution)/shard_map/prep_kernel/pallas_call | solution.py:388
  26.4 11.9 %all-to-all-done.x = f32[128,8,128]{2,1,0:T(8,128)S(1)} async-done(((f32[128,8,128]{2,1,0:T(8,128)}), f32[128,8,128]{2,1,0:T(8,128)S(1)}, u32[]{:S(2)}, u32[]{:S(2)}) %all-to-all-start) | async-done | bytes 524320 | tf_op jit(solution)/shard_map/all_to_all | solution.py:441
  39.1 4.0 %all-to-all-start.1 = ((f32[8,9,16,128]{3,2,1,0:T(8,128)}), f32[8,9,16,128]{3,2,1,0:T(8,128)S(1)}, u32[]{:S(2)}, u32[]{:S(2)}) async-start(f32[8,9,16,128]{3,2,1,0:T(8,128)} %prep_kernel.1), calls=%async_computation.1 | async-start | bytes 1179648 | tf_op jit(solution)/shard_map/all_to_all | solution.py:420
  43.2 12.0 %scatter_kernel.1 = (f32[4,3,2,64,128]{4,3,2,1,0:T(8,128)}, f32[4,3,2,64,128]{4,3,2,1,0:T(8,128)}, f32[4,3,2,8,128]{4,3,2,1,0:T(8,128)}, f32[4,3,2,8,128]{4,3,2,1,0:T(8,128)}) custom-call(f32[128,8,128]{2,1,0:T(8,128)} %copy-done.2), custom_call_target="tpu_custom_call" | custom-call | tf_op jit(solution)/shard_map/scatter_kernel/pallas_call | solution.py:388
  56.0 0.8 copy-done.1
  56.8 2.9 %recv_kernel.1 = (f32[9,2,64,128]{3,2,1,0:T(8,128)}, f32[9,2,8,128]{3,2,1,0:T(8,128)}, f32[9,2,8,128]{3,2,1,0:T(8,128)}) custom-call(f32[8,9,16,128]{3,2,1,0:T(8,128)} %copy-done.1), custom_call_target="tpu_custom_call" | custom-call | tf_op jit(solution)/shard_map/recv_kernel/pallas_call | solution.py:388
  59.6 6.5 %collective-permute-start.2 = (f32[9,2,8,128]{3,2,1,0:T(8,128)}, f32[9,2,8,128]{3,2,1,0:T(8,128)S(1)}, u32[]{:S(2)}, u32[]{:S(2)}) collective-permute-start(f32[9,2,8,128]{3,2,1,0:T(8,128)} %get-tuple-element.26), channel_id=1, source_target_pairs={{0,16},{1,17},{2,18},{3,19},{4,20},{5,21},{6,22},{7,23},{8,24},{9,... | collective-permute-start | bytes 221192 | tf_op jit(solution)/shard_map/ppermute | solution.py:407
  66.2 1.1 collective-permute-done.2.ra
  67.3 2.9 %collective-permute-done.3.rb = f32[9,2,8,128]{3,2,1,0:T(8,128)S(1)} collective-permute-done((f32[9,2,8,128]{3,2,1,0:T(8,128)}, f32[9,2,8,128]{3,2,1,0:T(8,128)S(1)}, u32[]{:S(2)}, u32[]{:S(2)}) %collective-permute-start.3) | collective-permute-done | bytes 73760 | tf_op jit(solution)/shard_map/ppermute | solution.py:406
  70.8 3.4 %forward_kernel.1 = (f32[4,3,2,80,128]{4,3,2,1,0:T(8,128)}, f32[4,3,2,80,128]{4,3,2,1,0:T(8,128)}, f32[4,3,2,80,128]{4,3,2,1,0:T(8,128)}, f32[3,2,80,128]{3,2,1,0:T(8,128)}, f32[3,2,80,128]{3,2,1,0:T(8,128)}) custom-call(f32[9,2,64,128]{3,2,1,0:T(8,128)} %get-tuple-element.25.center, f32[9,2,8,128]{3,2,1,0:T(8,128)} %copy-done.5, f32[9,2,8,128]{3,2,1,0:T(8,128)} %copy-done.6), custom_call_target="tpu_custom_call" | custom-call | tf_op jit(solution)/shard_map/forward_kernel/pallas_call | solution.py:388
  74.9 4.4 %gradient_kernel.1 = (f32[4,3,2,80,128]{4,3,2,1,0:T(8,128)}, f32[3,2,64,128]{3,2,1,0:T(8,128)}, f32[3,2,8,128]{3,2,1,0:T(8,128)}, f32[3,2,8,128]{3,2,1,0:T(8,128)}) custom-call(f32[4,3,2,64,128]{4,3,2,1,0:T(8,128)} %get-tuple-element.21.wsum, f32[4,3,2,64,128]{4,3,2,1,0:T(8,128)} %get-tuple-element.22.vsum, f32[4,3,2,8,128]{4,3,2,1,0:T(8,128)} %copy-done.3, ...), custom_call_target="tpu_custom_call" | custom-call | tf_op jit(solution)/shard_map/gradient_kernel/pallas_call | solution.py:388
  79.2 3.3 %collective-permute-start.4 = (f32[3,2,8,128]{3,2,1,0:T(8,128)}, f32[3,2,8,128]{3,2,1,0:T(8,128)S(1)}, u32[]{:S(2)}, u32[]{:S(2)}) collective-permute-start(f32[3,2,8,128]{3,2,1,0:T(8,128)} %get-tuple-element.34), channel_id=1, source_target_pairs={{0,16},{1,17},{2,18},{3,19},{4,20},{5,21},{6,22},{7,23},{8,24},{9,... | collective-permute-start | bytes 73736 | tf_op jit(solution)/shard_map/ppermute | solution.py:407
  82.6 1.1 collective-permute-done.4.ra
  83.6 2.4 %collective-permute-done.5.rb = f32[3,2,8,128]{3,2,1,0:T(8,128)S(1)} collective-permute-done((f32[3,2,8,128]{3,2,1,0:T(8,128)}, f32[3,2,8,128]{3,2,1,0:T(8,128)S(1)}, u32[]{:S(2)}, u32[]{:S(2)}) %collective-permute-start.5) | collective-permute-done | bytes 24608 | tf_op jit(solution)/shard_map/ppermute | solution.py:406
  86.6 4.4 %hessian_kernel.1 = (f32[3,2,64,128]{3,2,1,0:T(8,128)}, f32[3,2,8,128]{3,2,1,0:T(8,128)}, f32[3,2,8,128]{3,2,1,0:T(8,128)}) custom-call(f32[3,2,64,128]{3,2,1,0:T(8,128)} %get-tuple-element.33.center.g, f32[3,2,8,128]{3,2,1,0:T(8,128)} %copy-done.9, f32[3,2,8,128]{3,2,1,0:T(8,128)} %copy-done.10, f32[4,3,2,80,128]{4,3,2,1,0:T(8,128)} %get-tuple-element.36.wide, ...), custom_call_target="tpu_custom_call" | custom-call | tf_op jit(solution)/shard_map/hessian_kernel/pallas_call | solution.py:388
  91.1 3.4 %collective-permute-start.6 = (f32[3,2,8,128]{3,2,1,0:T(8,128)}, f32[3,2,8,128]{3,2,1,0:T(8,128)S(1)}, u32[]{:S(2)}, u32[]{:S(2)}) collective-permute-start(f32[3,2,8,128]{3,2,1,0:T(8,128)} %get-tuple-element.38), channel_id=1, source_target_pairs={{0,16},{1,17},{2,18},{3,19},{4,20},{5,21},{6,22},{7,23},{8,24},{9,... | collective-permute-start | bytes 73736 | tf_op jit(solution)/shard_map/ppermute | solution.py:407
  94.5 1.1 collective-permute-done.6.ra
  95.6 2.4 %collective-permute-done.7.rb = f32[3,2,8,128]{3,2,1,0:T(8,128)S(1)} collective-permute-done((f32[3,2,8,128]{3,2,1,0:T(8,128)}, f32[3,2,8,128]{3,2,1,0:T(8,128)S(1)}, u32[]{:S(2)}, u32[]{:S(2)}) %collective-permute-start.7) | collective-permute-done | bytes 24608 | tf_op jit(solution)/shard_map/ppermute | solution.py:406
  98.5 4.3 %last_kernel.1 = f32[8,10,16,128]{3,2,1,0:T(8,128)} custom-call(f32[3,2,64,128]{3,2,1,0:T(8,128)} %get-tuple-element.33.center.g, f32[3,2,64,128]{3,2,1,0:T(8,128)} %get-tuple-element.37.center, f32[3,2,8,128]{3,2,1,0:T(8,128)} %copy-done.7, f32[3,2,8,128]{3,2,1,0:T(8,128)} %copy-done.8, f32[4,3,2,80,128]{4,3,2,1,0:T(8,128)} %get-tuple-element.36.wide, ...), custom_call_target="tpu_custom_call" | custom-call | tf_op jit(solution)/shard_map/last_kernel/pallas_call | solution.py:388
  102.9 17.7 %all_to_all.20.x = f32[8,10,16,128]{3,2,1,0:T(8,128)S(1)} all-to-all(f32[8,10,16,128]{3,2,1,0:T(8,128)} %last_kernel.1), channel_id=1, replica_groups=mesh['lat'=8,'lon'=16] {'lat'}, dimensions={0} | all-to-all | bytes 1310720 | tf_op jit(solution)/shard_map/all_to_all | solution.py:478
  120.6 9.8 %all_to_all.21.parts = f32[16,8,128]{2,1,0:T(8,128)} all-to-all(f32[16,8,128]{2,1,0:T(8,128)S(1)} %broadcast_in_dim.2), channel_id=1, replica_groups=mesh['lat'=8,'lon'=16] {'lon'}, dimensions={0} | all-to-all | bytes 131072 | tf_op jit(solution)/shard_map/all_to_all | solution.py:480
  130.3 2.1 %final_kernel.1 = (f32[12,32,128]{2,1,0:T(8,128)}, f32[12,32,128]{2,1,0:T(8,128)}) custom-call(f32[8,10,16,128]{3,2,1,0:T(8,128)} %copy-done, f32[16,8,128]{2,1,0:T(8,128)} %all_to_all.21.parts), custom_call_target="tpu_custom_call" | custom-call | tf_op jit(solution)/shard_map/final_kernel/pallas_call | solution.py:388
  (31 shorter events, 4.1 us)
Async XLA Ops:
  12.8 25.5 %all-to-all-start = ((f32[128,8,128]{2,1,0:T(8,128)}), f32[128,8,128]{2,1,0:T(8,128)S(1)}, u32[]{:S(2)}, u32[]{:S(2)}) async-start(f32[128,8,128]{2,1,0:T(8,128)} %pack_kernel.1), calls=%async_computation | async-start | bytes 1048576 | tf_op jit(solution)/shard_map/all_to_all | solution.py:441
  38.3 0.8 copy-start.2
  39.1 16.8 %all-to-all-start.1 = ((f32[8,9,16,128]{3,2,1,0:T(8,128)}), f32[8,9,16,128]{3,2,1,0:T(8,128)S(1)}, u32[]{:S(2)}, u32[]{:S(2)}) async-start(f32[8,9,16,128]{3,2,1,0:T(8,128)} %prep_kernel.1), calls=%async_computation.1 | async-start | bytes 1179648 | tf_op jit(solution)/shard_map/all_to_all | solution.py:420
  55.2 19.0 %collective-permute-start = (f32[4,3,2,8,128]{4,3,2,1,0:T(8,128)}, f32[4,3,2,8,128]{4,3,2,1,0:T(8,128)S(1)}, u32[]{:S(2)}, u32[]{:S(2)}) collective-permute-start(f32[4,3,2,8,128]{4,3,2,1,0:T(8,128)} %get-tuple-element.23), channel_id=1, source_target_pairs={{0,16},{1,17},{2,18},{3,19},{4,20},{5,21},{6,22},{7,23},{8,24},{9,... | collective-permute-start | bytes 294920 | tf_op jit(solution)/shard_map/ppermute | solution.py:407
  55.4 18.8 %collective-permute-start.1 = (f32[4,3,2,8,128]{4,3,2,1,0:T(8,128)}, f32[4,3,2,8,128]{4,3,2,1,0:T(8,128)S(1)}, u32[]{:S(2)}, u32[]{:S(2)}) collective-permute-start(f32[4,3,2,8,128]{4,3,2,1,0:T(8,128)} %get-tuple-element.24), channel_id=1, source_target_pairs={{0,31},{1,16},{2,17},{3,18},{4,19},{5,20},{6,21},{7,22},{8,23},{9,... | collective-permute-start | bytes 294920 | tf_op jit(solution)/shard_map/ppermute | solution.py:406
  56.0 0.8 copy-start.1
  59.6 7.7 %collective-permute-start.2 = (f32[9,2,8,128]{3,2,1,0:T(8,128)}, f32[9,2,8,128]{3,2,1,0:T(8,128)S(1)}, u32[]{:S(2)}, u32[]{:S(2)}) collective-permute-start(f32[9,2,8,128]{3,2,1,0:T(8,128)} %get-tuple-element.26), channel_id=1, source_target_pairs={{0,16},{1,17},{2,18},{3,19},{4,20},{5,21},{6,22},{7,23},{8,24},{9,... | collective-permute-start | bytes 221192 | tf_op jit(solution)/shard_map/ppermute | solution.py:407
  66.2 4.0 %collective-permute-start.3 = (f32[9,2,8,128]{3,2,1,0:T(8,128)}, f32[9,2,8,128]{3,2,1,0:T(8,128)S(1)}, u32[]{:S(2)}, u32[]{:S(2)}) collective-permute-start(f32[9,2,8,128]{3,2,1,0:T(8,128)} %get-tuple-element.27), channel_id=1, source_target_pairs={{0,31},{1,16},{2,17},{3,18},{4,19},{5,20},{6,21},{7,22},{8,23},{9,... | collective-permute-start | bytes 221192 | tf_op jit(solution)/shard_map/ppermute | solution.py:406
  67.3 2.9 %copy-start.5 = (f32[9,2,8,128]{3,2,1,0:T(8,128)}, f32[9,2,8,128]{3,2,1,0:T(8,128)S(1)}, u32[]{:S(2)}) copy-start(f32[9,2,8,128]{3,2,1,0:T(8,128)S(1)} %collective-permute-done.2.ra) | copy-start | bytes 221188
  70.2 0.6 copy-start.6
  74.2 0.6 copy-start.3
  74.2 0.7 copy-start.4
  79.2 4.4 %collective-permute-start.4 = (f32[3,2,8,128]{3,2,1,0:T(8,128)}, f32[3,2,8,128]{3,2,1,0:T(8,128)S(1)}, u32[]{:S(2)}, u32[]{:S(2)}) collective-permute-start(f32[3,2,8,128]{3,2,1,0:T(8,128)} %get-tuple-element.34), channel_id=1, source_target_pairs={{0,16},{1,17},{2,18},{3,19},{4,20},{5,21},{6,22},{7,23},{8,24},{9,... | collective-permute-start | bytes 73736 | tf_op jit(solution)/shard_map/ppermute | solution.py:407
  82.6 3.5 %collective-permute-start.5 = (f32[3,2,8,128]{3,2,1,0:T(8,128)}, f32[3,2,8,128]{3,2,1,0:T(8,128)S(1)}, u32[]{:S(2)}, u32[]{:S(2)}) collective-permute-start(f32[3,2,8,128]{3,2,1,0:T(8,128)} %get-tuple-element.35), channel_id=1, source_target_pairs={{0,31},{1,16},{2,17},{3,18},{4,19},{5,20},{6,21},{7,22},{8,23},{9,... | collective-permute-start | bytes 73736 | tf_op jit(solution)/shard_map/ppermute | solution.py:406
  83.6 2.4 %copy-start.9 = (f32[3,2,8,128]{3,2,1,0:T(8,128)}, f32[3,2,8,128]{3,2,1,0:T(8,128)S(1)}, u32[]{:S(2)}) copy-start(f32[3,2,8,128]{3,2,1,0:T(8,128)S(1)} %collective-permute-done.4.ra) | copy-start | bytes 73732
  86.0 0.6 copy-start.10
  91.1 4.5 %collective-permute-start.6 = (f32[3,2,8,128]{3,2,1,0:T(8,128)}, f32[3,2,8,128]{3,2,1,0:T(8,128)S(1)}, u32[]{:S(2)}, u32[]{:S(2)}) collective-permute-start(f32[3,2,8,128]{3,2,1,0:T(8,128)} %get-tuple-element.38), channel_id=1, source_target_pairs={{0,16},{1,17},{2,18},{3,19},{4,20},{5,21},{6,22},{7,23},{8,24},{9,... | collective-permute-start | bytes 73736 | tf_op jit(solution)/shard_map/ppermute | solution.py:407
  94.5 3.5 %collective-permute-start.7 = (f32[3,2,8,128]{3,2,1,0:T(8,128)}, f32[3,2,8,128]{3,2,1,0:T(8,128)S(1)}, u32[]{:S(2)}, u32[]{:S(2)}) collective-permute-start(f32[3,2,8,128]{3,2,1,0:T(8,128)} %get-tuple-element.39), channel_id=1, source_target_pairs={{0,31},{1,16},{2,17},{3,18},{4,19},{5,20},{6,21},{7,22},{8,23},{9,... | collective-permute-start | bytes 73736 | tf_op jit(solution)/shard_map/ppermute | solution.py:406
  95.5 2.4 %copy-start.7 = (f32[3,2,8,128]{3,2,1,0:T(8,128)}, f32[3,2,8,128]{3,2,1,0:T(8,128)S(1)}, u32[]{:S(2)}) copy-start(f32[3,2,8,128]{3,2,1,0:T(8,128)S(1)} %collective-permute-done.6.ra) | copy-start | bytes 73732
  98.0 0.6 copy-start.8
  120.5 9.8 %copy-start = (f32[8,10,16,128]{3,2,1,0:T(8,128)}, f32[8,10,16,128]{3,2,1,0:T(8,128)S(1)}, u32[]{:S(2)}) copy-start(f32[8,10,16,128]{3,2,1,0:T(8,128)S(1)} %all_to_all.20.x) | copy-start | bytes 1966084

commit v2 on v1

--- a/solution.py
+++ b/solution.py
@@ -141,7 +141,7 @@
     return out
 
 
-def pack_kernel(count, tile, cell, step, value, weight, out, rows, base, acc, bt):
+def pack_kernel(count, tile, cell, step, value, weight, out, rows, base, acc, left, right):
     shape = (16, 128)
     live = sublanes(shape) * 128 + lanes(shape) < count[0]
     c, t = cell[...], tile[...]
@@ -157,21 +157,15 @@
     wv = (w0 + w1) * value[...]
     v0 = wv.astype(BF16).astype(F32)
     v1 = (wv - v0).astype(BF16).astype(F32)
-    v2 = wv - v0 - v1
-    zero = jnp.zeros(shape, F32)
     rows[0] = jnp.where(live, dest, -1).astype(F32)
     rows[1] = (((level - 3 * q) * 64 + (col & 63)) * 256).astype(F32)
-    rows[2] = step[...].astype(F32)
-    rows[3] = w0
-    rows[4] = v0
-    rows[5] = ((lat & 1) * 128 + (lat >> 1)).astype(F32)
-    rows[6] = zero
-    rows[7] = w1
-    rows[8] = v1
-    rows[9] = zero
-    rows[10] = zero
-    rows[11] = zero
-    rows[12] = v2
+    rows[2] = ((lat & 1) * 128 + (lat >> 1)).astype(F32)
+    rows[3] = step[...].astype(F32)
+    rows[4] = w0
+    rows[5] = w1
+    rows[6] = v0
+    rows[7] = v1
+    rows[8] = wv - v0 - v1
     base[...] = jnp.zeros_like(base)
     acc[...] = jnp.zeros_like(acc)
     square = (128, 256)
@@ -179,54 +173,49 @@
     ids = sublanes((128, 128)).astype(F32)
     places = sublanes((ROOM, 128)).astype(F32)
 
-    def block(b, carry):
-        def line(i):
-            return rows[i, pl.ds(b, 1), :]
-
-        member = jnp.where(ids == line(0), 1.0, 0.0)
-        member16 = member.astype(BF16)
-        counted = jnp.dot(member16, before, preferred_element_type=F32)
-        rank = jnp.sum(member * (counted[:, :128] + base[...]), axis=0, keepdims=True)
-        base[...] += counted[:, 128:]
-        here = places == rank
-        for p in range(3):
-            for ch in range(4):
-                piece = jnp.where(here, line(1 + 4 * p + ch), 0.0).astype(BF16)
-                for m in range(8):
-                    at = m * 128 + ch * 32
-                    bt[at : at + 32, p * 128 : p * 128 + 128] = piece[m * 32 : m * 32 + 32]
-        three = jnp.concatenate([member16, member16, member16], axis=1)
+    def block(i, carry):
+        for j in range(2):
+            line = lambda n: rows[n, pl.ds(2 * i + j, 1), :]
+            at = slice(j * 128, j * 128 + 128)
+            mine = ids == line(0)
+            member = jnp.where(mine, 1.0, 0.0)
+            counted = jnp.dot(member.astype(BF16), before, preferred_element_type=F32)
+            rank = jnp.sum(member * (counted[:, :128] + base[...]), axis=0, keepdims=True)
+            base[...] += counted[:, 128:]
+            right[:, at] = jnp.where(places == rank, 1.0, 0.0).astype(BF16)
+            for p in range(8):
+                left[p * 128 : p * 128 + 128, at] = jnp.where(mine, line(1 + p), 0.0).astype(BF16)
         acc[...] += lax.dot_general(
-            three, bt[...], (((1,), (1,)), ((), ())), preferred_element_type=F32
+            left[...], right[...], (((1,), (1,)), ((), ())), preferred_element_type=F32
         )
         return carry
 
-    lax.fori_loop(0, 16, block, 0)
-    for m in range(8):
-        out[:, m, :] = acc[:, m * 128 : m * 128 + 128]
-
-
-def scatter_kernel(x, wsum, vsum, sa, sb, xt, at, bt, acc):
+    lax.fori_loop(0, 8, block, 0)
+    for ch, pieces in enumerate(((0, 1), (2,), (3, 4), (5, 6, 7))):
+        for hf in range(2):
+            at = slice(hf * 128, hf * 128 + 128)
+            out[:, 2 * ch + hf, :] = sum(acc[p * 128 : p * 128 + 128, at] for p in pieces)
+
+
+def scatter_kernel(x, after, wsum, vsum, sa, sb, xt, at, bt, acc):
     h = half()
-    most = jnp.max(x[...], axis=0)
-    lane = lanes((8, 128))
-    used = jnp.where((lane >= 32) & (lane < 64) & (most > 0.5), 1.0, 0.0)
-    total = jnp.sum(used).astype(I32)
+    most = jnp.max(x[:, 2:4, :], axis=0)
+    total = jnp.sum(jnp.where(most > 0.5, 1.0, 0.0)).astype(I32)
     acc[...] = jnp.zeros_like(acc)
-    for m in range(8):
-
-        @pl.when(total > 32 * m)
-        def _():
-            xt[m * 128 : m * 128 + 128, :] = x[:, m, :].T
+    for ch in range(4):
+        xt[ch, :128] = x[:, 2 * ch, :].T
+
+    @pl.when(total > 128)
+    def _():
+        for ch in range(4):
+            xt[ch, 128:] = x[:, 2 * ch + 1, :].T
 
     row_ids = sublanes((ROWS, 128))
     lat_ids = sublanes((256, 128))
 
     def group(g, carry):
-        start = (g // 4) * 128 + (g % 4) * 8
-
         def part(ch):
-            return xt[pl.ds(pl.multiple_of(start + ch * 32, 8), 8), :]
+            return xt[ch, pl.ds(pl.multiple_of(g * 8, 8), 8), :]
 
         cell = part(0).astype(I32)
         row = (part(1).astype(I32) - 1) * (LV * COL) + (cell >> 8)
@@ -271,9 +260,29 @@
         put_edges(sa, sb, (l, u), x[u][EDGE : 2 * EDGE], x[u][COL : COL + EDGE], h)
 
 
-def gradient_kernel(wsum, vsum, ra, rb, states, gains, drifts, cn, cs, wide, out, sa, sb):
+def fetch(sources, buffers, sems):
+    levels = []
+    for l in range(LV):
+        copies = []
+        for i, (src, dst) in enumerate(zip(sources, buffers)):
+            at = (slice(None), l) if len(src.shape) == 5 else l
+            copies.append(pltpu.make_async_copy(src.at[at], dst.at[at], sems.at[l, i]))
+        levels.append(copies)
+        for copy in copies:
+            copy.start()
+    return levels
+
+
+def gradient_kernel(
+    wsum, vsum, ra, rb, states_in, gains_in, drifts_in, cn_in, cs_in, out, sa, sb, *scratch
+):
+    *buffers, sems = scratch
     h = half()
+    levels = fetch((states_in, gains_in, drifts_in, cn_in, cs_in), buffers, sems)
+    states, gains, drifts, cn, cs = buffers
     for l in range(LV):
+        for copy in levels[l]:
+            copy.wait()
         n = [cn[l, u] for u in range(2)]
         s = [cs[l, u] for u in range(2)]
         x = None
@@ -285,7 +294,6 @@
                 v = jnp.concatenate(
                     [pltpu.roll(left, 4, 0), vsum[k, l, u], pltpu.roll(right, 4, 0)], axis=0
                 )
-                wide[k, l, u] = w
                 m.append(v - w * states[k, l, u])
             x = m if x is None else [x[u] + m[u] for u in range(2)]
             x = adjoint(
@@ -302,7 +310,8 @@
     e, seen = p, []
     for k in range(STEPS):
         e = tangent(e, g(k), d(k), n, s)
-        seen.append([wide[k, l, u] * e[u] for u in range(2)])
+        w = wide(k)
+        seen.append([w[u] * e[u] for u in range(2)])
     x = None
     for k in reversed(range(STEPS)):
         x = seen[k] if x is None else [x[u] + seen[k][u] for u in range(2)]
@@ -310,23 +319,34 @@
     return [p[u] + x[u] for u in range(2)]
 
 
-def extended(center, ra, rb, l, h):
+def extended(center, ra, rb, index, h):
     out = []
     for u in range(2):
-        left, right = get_edges(ra, rb, (l, u), h)
-        out.append(jnp.concatenate([left, center[l, u], right], axis=0))
+        left, right = get_edges(ra, rb, index + (u,), h)
+        out.append(jnp.concatenate([left, center[index + (u,)], right], axis=0))
     return out
 
 
-def hessian_kernel(center, ra, rb, wide, gains, drifts, cn, cs, out, sa, sb):
+def hessian_kernel(
+    center, ra, rb, wsum, wa, wb, gains_in, drifts_in, cn_in, cs_in, out, sa, sb, *scratch
+):
+    *buffers, sems = scratch
     h = half()
+    levels = fetch((gains_in, drifts_in, cn_in, cs_in), buffers, sems)
     for l in range(LV):
-        p = extended(center, ra, rb, l, h)
-        keep(hessian(l, p, wide, gains, drifts, cn, cs), out, sa, sb, l, h)
-
-
-def last_kernel(g, center, ra, rb, wide, gains, drifts, cn, cs, out):
+        p = extended(center, ra, rb, (l,), h)
+        for copy in levels[l]:
+            copy.wait()
+        wide = lambda k: extended(wsum, wa, wb, (k, l), h)
+        keep(hessian(l, p, wide, *buffers), out, sa, sb, l, h)
+
+
+def last_kernel(
+    g, center, ra, rb, wsum, wa, wb, gains_in, drifts_in, cn_in, cs_in, out, table_ref, *scratch
+):
+    *buffers, sems = scratch
     h = half()
+    levels = fetch((gains_in, drifts_in, cn_in, cs_in), buffers, sems)
     sums = [jnp.zeros((8, 128), F32) for _ in range(5)]
 
     def fold(a, b):
@@ -334,8 +354,11 @@
         return jnp.sum(prod.reshape(8, 8, 128), axis=0)
 
     for l in range(LV):
-        p = extended(center, ra, rb, l, h)
-        y = hessian(l, p, wide, gains, drifts, cn, cs)
+        p = extended(center, ra, rb, (l,), h)
+        for copy in levels[l]:
+            copy.wait()
+        wide = lambda k: extended(wsum, wa, wb, (k, l), h)
+        y = hessian(l, p, wide, *buffers)
         v = [
             [g[l, u] for u in range(2)],
             [center[l, u] for u in range(2)],
@@ -347,18 +370,19 @@
         for i in range(3):
             t = jnp.concatenate(v[i], axis=0).T.reshape(LAT, 16, 128)
             out[:, i * 3 + l] = t
-    row = sublanes((16, 128))
-    table = jnp.zeros((16, 128), F32)
+    lane = lanes((1, 128))
+    table = jnp.zeros((1, 128), F32)
     for i in range(5):
-        table = jnp.where(row == i, jnp.sum(sums[i], axis=0, keepdims=True), table)
-    for b in range(LAT):
-        out[b, 9] = table
+        whole = jnp.sum(jnp.sum(sums[i], axis=0, keepdims=True), axis=1, keepdims=True)
+        table = jnp.where(lane == i, whole, table)
+    table_ref[...] = jnp.broadcast_to(table, (ALL, 128))
 
 
 def final_kernel(x, parts, increment, residual):
-    total = jnp.sum(parts[...], axis=0)
-    total = jnp.broadcast_to(jnp.sum(total, axis=1, keepdims=True), (8, 128))
-    a00, a01, a11, a02, a12 = [total[i : i + 1] for i in range(5)]
+    total = jnp.sum(parts[...], axis=0, keepdims=True)
+    lane = lanes((1, 128))
+    pick = lambda i: jnp.sum(jnp.where(lane == i, total, 0.0), axis=1, keepdims=True)
+    a00, a01, a11, a02, a12 = [jnp.broadcast_to(pick(i), (1, 128)) for i in range(5)]
     alpha = a00 / a01
     new = a00 - 2.0 * alpha * a01 + alpha * alpha * a11
     keep1 = 1.0 + new / a00
@@ -381,14 +405,23 @@
 
 VM = pl.BlockSpec(memory_space=pltpu.VMEM)
 SM = pl.BlockSpec(memory_space=pltpu.SMEM)
-
-
-def call(kernel, outs, *args, scratch=(), scalars=0, flops=1000000):
-    shapes = tuple(jax.ShapeDtypeStruct(s, F32) for s in outs)
+AN = pl.BlockSpec(memory_space=pl.ANY)
+
+
+def call(kernel, outs, *args, scratch=(), space="v", ins=None):
+    shapes = tuple(
+        pltpu.VMEM(s, F32) if where == "v" else jax.ShapeDtypeStruct(s, F32)
+        for s, where in zip(outs, space * len(outs) if len(space) == 1 else space)
+    )
+    ins = ins or "v" * len(args)
+    args = [
+        pltpu.with_memory_space_constraint(a, pltpu.VMEM) if i == "v" else a
+        for a, i in zip(args, ins)
+    ]
     return pl.pallas_call(
         kernel,
         out_shape=shapes if len(shapes) > 1 else shapes[0],
-        in_specs=[SM] * scalars + [VM] * (len(args) - scalars),
+        in_specs=[{"s": SM, "a": AN}.get(i, VM) for i in ins],
         out_specs=(VM,) * len(shapes) if len(shapes) > 1 else VM,
         scratch_shapes=list(scratch),
         name=kernel.__name__,
@@ -416,7 +449,9 @@
     edge = (LV, 2, EDGE, 128)
     middle = (LV, 2, COL, 128)
 
-    sent = call(prep_kernel, [(LAT, 9, 16, 128)], background, wind_lon, wind_lat)
+    sent = call(
+        prep_kernel, [(LAT, 9, 16, 128)], background, wind_lon, wind_lat, ins="hhh"
+    )
     moved = lax.all_to_all(sent, "lat", 0, 0, tiled=True)
     fold = lambda a: a.reshape(16, 128)
     packed = call(
@@ -428,35 +463,42 @@
         fold(obs_step),
         fold(obs_value),
         fold(obs_weight),
-        scalars=1,
+        ins="shhhhh",
         scratch=[
-            pltpu.VMEM((13, 16, 128), F32),
+            pltpu.VMEM((9, 16, 128), F32),
             pltpu.VMEM((128, 128), F32),
-            pltpu.VMEM((128, 1024), F32),
-            pltpu.VMEM((1024, 384), BF16),
+            pltpu.VMEM((1024, 256), F32),
+            pltpu.VMEM((1024, 256), BF16),
+            pltpu.VMEM((256, 256), BF16),
         ],
     )
+    moved, packed = lax.optimization_barrier((moved, packed))
+    arrived = lax.all_to_all(packed, both, 0, 0, tiled=True)
     fields, sa, sb = call(recv_kernel, [(9, 2, COL, 128)] + [(9, 2, EDGE, 128)] * 2, moved)
     ra, rb = swap(sa, sb)
-    arrived = lax.all_to_all(packed, both, 0, 0, tiled=True)
+    states, gains, drifts, cn, cs = call(
+        forward_kernel, [(STEPS,) + plane] * 3 + [plane] * 2, fields, ra, rb, space="h"
+    )
     wsum, vsum, sa, sb = call(
         scatter_kernel,
         [(STEPS,) + middle] * 2 + [(STEPS,) + edge] * 2,
         arrived,
+        cn,
+        ins="va",
         scratch=[
-            pltpu.VMEM((1024, 128), F32),
+            pltpu.VMEM((4, 256, 128), F32),
             pltpu.VMEM((ROWS, 1024), BF16),
             pltpu.VMEM((1280, 1024), BF16),
             pltpu.VMEM((ROWS, 1280), F32),
         ],
     )
     wa, wb = swap(sa, sb)
-    states, gains, drifts, cn, cs = call(
-        forward_kernel, [(STEPS,) + plane] * 3 + [plane] * 2, fields, ra, rb
-    )
-    wide, g, sa, sb = call(
+    big = pltpu.VMEM((STEPS,) + plane, F32)
+    small = pltpu.VMEM(plane, F32)
+    sems = lambda n: pltpu.SemaphoreType.DMA((LV, n))
+    g, sa, sb = call(
         gradient_kernel,
-        [(STEPS,) + plane, middle, edge, edge],
+        [middle, edge, edge],
         wsum,
         vsum,
         wa,
@@ -466,21 +508,30 @@
         drifts,
         cn,
         cs,
+        ins="vvvvaaaaa",
+        scratch=[big, big, big, small, small, sems(5)],
     )
     ra, rb = swap(sa, sb)
+    coefs = (wsum, wa, wb, gains, drifts, cn, cs)
+    scratch = [big, big, small, small, sems(4)]
     hg, sa, sb = call(
-        hessian_kernel, [middle, edge, edge], g, ra, rb, wide, gains, drifts, cn, cs
+        hessian_kernel, [middle, edge, edge], g, ra, rb, *coefs, ins="vvvvvvaaaa", scratch=scratch
     )
     ra, rb = swap(sa, sb)
-    sent = call(
-        last_kernel, [(LAT, 10, 16, 128)], g, hg, ra, rb, wide, gains, drifts, cn, cs
-    )
+    sent, table = call(
+        last_kernel,
+        [(LAT, 9, 16, 128), (ALL, 128)],
+        g,
+        hg,
+        ra,
+        rb,
+        *coefs,
+        ins="vvvvvvvaaaa",
+        scratch=scratch,
+    )
+    parts = lax.all_to_all(table, both, 0, 0, tiled=True)
     moved = lax.all_to_all(sent, "lat", 0, 0, tiled=True)
-    mine = jnp.sum(moved[:, 9, :8], axis=0)
-    parts = lax.all_to_all(
-        jnp.broadcast_to(mine[None], (LON, 8, 128)), "lon", 0, 0, tiled=True
-    )
-    return call(final_kernel, [(12, 32, 128)] * 2, moved, parts)
+    return call(final_kernel, [(12, 32, 128)] * 2, moved, parts, space="h")
 
 
 def solution(mesh):

time: 133 us -> 117 us (0.88)
  Pallas kernels: 47.2 us -> 31.1 us
  blocking collectives: 27.4 us -> 35 us
  starting transfers between devices: 29.5 us -> 26.2 us
  local copies, waits for them, and re-layouts: 4.12 us -> 1.83 us
  waiting for transfers between devices: 22.8 us -> 20.9 us
    pallas_call x9, Pallas kernels: 47.2 us -> 31.1 us  [call(): pl.pallas_call(kernel, out_shape=shapes if len(shapes) > 1 else shapes[0]...]
    all_to_all x1, blocking collectives: 9.78 us -> 21.5 us  [on_device(): parts = lax.all_to_all(table, both, 0, 0, tiled=True)]
    all_to_all x1, waiting for transfers between devices: 11.9 us -> 3.55 us  [on_device(): arrived = lax.all_to_all(packed, both, 0, 0, tiled=True)]
    ppermute x4, starting transfers between devices: 13.5 us -> 7.05 us  [swap(): ra = lax.ppermute(sa, ('lat', 'lon'), near)]
    ppermute x4, waiting for transfers between devices: 7.67 us -> 12.6 us  [swap(): rb = lax.ppermute(sb, ('lat', 'lon'), far)]
    all_to_all x1, blocking collectives: 17.7 us -> 13.5 us  [on_device(): moved = lax.all_to_all(sent, 'lat', 0, 0, tiled=True)]
    ppermute x4, starting transfers between devices: 0.57 us -> 4.25 us  [swap(): rb = lax.ppermute(sb, ('lat', 'lon'), far)]
    all_to_all x1, waiting for transfers between devices: 0.01 us -> 3.12 us  [on_device(): moved = lax.all_to_all(sent, 'lat', 0, 0, tiled=True)]
  transfers between devices with their start and end apart: 10 -> 10, of which waited for: 7 -> 9; matrix products, arithmetic and copies ran while one was open for 0% -> 0% of each run, Pallas kernels for 15% -> 8%
where the time goes in v2:
time: 117 us; the launch traced here: 116 us
  blocking collectives  35 us (30%)
  Pallas kernels  31.1 us (27%)
  starting transfers between devices  26.2 us (22%)
  waiting for transfers between devices  20.9 us (18%)
  local copies, waits for them, and re-layouts  1.83 us (2%)
  between operations  1.34 us (1%)
    pallas_call x9, Pallas kernels, call(): pl.pallas_call(kernel, out_shape=shapes if len(shapes) > 1 else shapes[0]...  31.1 us
    all_to_all x1, blocking collectives, on_device(): parts = lax.all_to_all(table, both, 0, 0, tiled=True)  21.5 us
    all_to_all x1, blocking collectives, on_device(): moved = lax.all_to_all(sent, 'lat', 0, 0, tiled=True)  13.5 us
    ppermute x4, waiting for transfers between devices, swap(): rb = lax.ppermute(sb, ('lat', 'lon'), far)  12.6 us
    all_to_all x1, starting transfers between devices, on_device(): arrived = lax.all_to_all(packed, both, 0, 0, tiled=True)  9.11 us
    ppermute x4, starting transfers between devices, swap(): ra = lax.ppermute(sa, ('lat', 'lon'), near)  7.05 us
    all_to_all x1, starting transfers between devices, on_device(): moved = lax.all_to_all(sent, 'lat', 0, 0, tiled=True)  5.79 us
    ppermute x4, starting transfers between devices, swap(): rb = lax.ppermute(sb, ('lat', 'lon'), far)  4.25 us
  transfers between devices with their start and end apart: 10, of which 9 were waited for; matrix products, arithmetic and copies ran while one was open for 0% of the time, Pallas kernels for 8%

profile of v2, /device:TPU:1, one launch (start us, length us, event | category | flops | bytes accessed | tf_op | source)
XLA Modules:
  0.0 116.3 jit_solution(18098386824351014194)
XLA Ops:
  0.6 2.2 %prep_kernel.1 = f32[8,9,16,128]{3,2,1,0:T(8,128)} custom-call(f32[12,32,128]{2,1,0:T(8,128)} %bg.1, f32[12,32,128]{2,1,0:T(8,128)} %wl.1, f32[12,32,128]{2,1,0:T(8,128)} %wt.1), custom_call_target="tpu_custom_call" | custom-call | tf_op jit(solution)/shard_map/prep_kernel/pallas_call | solution.py:421
  2.8 5.8 %all-to-all-start = ((f32[8,9,16,128]{3,2,1,0:T(8,128)}), f32[8,9,16,128]{3,2,1,0:T(8,128)S(1)}, u32[]{:S(2)}, u32[]{:S(2)}) async-start(f32[8,9,16,128]{3,2,1,0:T(8,128)} %prep_kernel.1), calls=%async_computation | async-start | bytes 1179648 | tf_op jit(solution)/shard_map/all_to_all | solution.py:455
  9.2 6.3 %pack_kernel.1 = f32[128,8,128]{2,1,0:T(8,128)} custom-call(s32[1]{0:T(128)S(6)} %copy.12.count, s32[16,128]{1,0:T(8,128)} %bitcast.11, s32[16,128]{1,0:T(8,128)} %bitcast.12, s32[16,128]{1,0:T(8,128)} %bitcast.13, f32[16,128]{1,0:T(8,128)} %bitcast.14, f32[16,128]{1,0:T(8,128)} %bitcast.15), custom_call_target="tpu_custom_call" | custom-call | tf_op jit(solution)/shard_map/pack_kernel/pallas_call | solution.py:421
  15.5 3.1 %all-to-all-done.x = f32[8,9,16,128]{3,2,1,0:T(8,128)S(1)} async-done(((f32[8,9,16,128]{3,2,1,0:T(8,128)}), f32[8,9,16,128]{3,2,1,0:T(8,128)S(1)}, u32[]{:S(2)}, u32[]{:S(2)}) %all-to-all-start) | async-done | bytes 589856 | tf_op jit(solution)/shard_map/all_to_all | solution.py:455
  18.6 9.1 %all-to-all-start.1 = ((f32[128,8,128]{2,1,0:T(8,128)}), f32[128,8,128]{2,1,0:T(8,128)S(1)}, u32[]{:S(2)}, u32[]{:S(2)}) async-start(f32[128,8,128]{2,1,0:T(8,128)} %pack_kernel.1), calls=%async_computation.1 | async-start | bytes 1048576 | tf_op jit(solution)/shard_map/all_to_all | solution.py:476
  27.7 0.9 recv_kernel.1
  28.7 1.1 collective-permute-start
  30.7 5.2 %collective-permute-done.1.rb = f32[9,2,8,128]{3,2,1,0:T(8,128)S(1)} collective-permute-done((f32[9,2,8,128]{3,2,1,0:T(8,128)S(1)}, f32[9,2,8,128]{3,2,1,0:T(8,128)S(1)}, u32[]{:S(2)}, u32[]{:S(2)}) %collective-permute-start.1) | collective-permute-done | bytes 73760 | tf_op jit(solution)/shard_map/ppermute | solution.py:439
  35.9 2.3 %forward_kernel.1 = (f32[4,3,2,80,128]{4,3,2,1,0:T(8,128)}, f32[4,3,2,80,128]{4,3,2,1,0:T(8,128)}, f32[4,3,2,80,128]{4,3,2,1,0:T(8,128)}, f32[3,2,80,128]{3,2,1,0:T(8,128)}, f32[3,2,80,128]{3,2,1,0:T(8,128)}) custom-call(f32[9,2,64,128]{3,2,1,0:T(8,128)S(1)} %get-tuple-element.26.center, f32[9,2,8,128]{3,2,1,0:T(8,128)S(1)} %collective-permute-done.ra, ...), custom_call_target="tpu_custom_call" | custom-call | tf_op jit(solution)/shard_map/forward_kernel/pallas_call | solution.py:421
  38.2 3.5 %all-to-all-done.1.x = f32[128,8,128]{2,1,0:T(8,128)S(1)} async-done(((f32[128,8,128]{2,1,0:T(8,128)}), f32[128,8,128]{2,1,0:T(8,128)S(1)}, u32[]{:S(2)}, u32[]{:S(2)}) %all-to-all-start.1) | async-done | bytes 524320 | tf_op jit(solution)/shard_map/all_to_all | solution.py:476
  42.6 1.0 copy-done.1
  43.6 9.7 %scatter_kernel.1 = (f32[4,3,2,64,128]{4,3,2,1,0:T(8,128)S(1)}, f32[4,3,2,64,128]{4,3,2,1,0:T(8,128)S(1)}, f32[4,3,2,8,128]{4,3,2,1,0:T(8,128)S(1)}, f32[4,3,2,8,128]{4,3,2,1,0:T(8,128)S(1)}) custom-call(f32[128,8,128]{2,1,0:T(8,128)S(1)} %copy-done.1, f32[3,2,80,128]{3,2,1,0:T(8,128)} %get-tuple-element.29.after.cn_in), custom_call_target="tpu_custom_call" | custom-call | tf_op jit(solution)/shard_map/scatter_kernel/pallas_call | solution.py:421
  54.1 3.3 %collective-permute-start.3 = (f32[4,3,2,8,128]{4,3,2,1,0:T(8,128)S(1)}, f32[4,3,2,8,128]{4,3,2,1,0:T(8,128)S(1)}, u32[]{:S(2)}, u32[]{:S(2)}) collective-permute-start(f32[4,3,2,8,128]{4,3,2,1,0:T(8,128)S(1)} %get-tuple-element.33), channel_id=1, source_target_pairs={{0,31},{1,16},{2,17},{3,18},{4,19},{5,20},{6,21},{7,22},{8,23},{9,... | collective-permute-start | bytes 294920 | tf_op jit(solution)/shard_map/ppermute | solution.py:439
  57.4 2.6 %collective-permute-done.3.rb.wb = f32[4,3,2,8,128]{4,3,2,1,0:T(8,128)S(1)} collective-permute-done((f32[4,3,2,8,128]{4,3,2,1,0:T(8,128)S(1)}, f32[4,3,2,8,128]{4,3,2,1,0:T(8,128)S(1)}, u32[]{:S(2)}, u32[]{:S(2)}) %collective-permute-start.3) | collective-permute-done | bytes 98336 | tf_op jit(solution)/shard_map/ppermute | solution.py:439
  59.9 2.3 %gradient_kernel.1 = (f32[3,2,64,128]{3,2,1,0:T(8,128)S(1)}, f32[3,2,8,128]{3,2,1,0:T(8,128)S(1)}, f32[3,2,8,128]{3,2,1,0:T(8,128)S(1)}) custom-call(f32[4,3,2,64,128]{4,3,2,1,0:T(8,128)S(1)} %get-tuple-element.30.wsum, f32[4,3,2,64,128]{4,3,2,1,0:T(8,128)S(1)} %get-tuple-element.31.vsum, f32[4,3,2,8,128]{4,3,2,1,0:T(8,128)S(1)} %collective-permute-done.2.ra.wa, ...), custom_call_target="tpu_custom_call" | custom-call | tf_op jit(solution)/shard_map/gradient_kernel/pallas_call | solution.py:421
  62.3 1.7 %collective-permute-start.4 = (f32[3,2,8,128]{3,2,1,0:T(8,128)S(1)}, f32[3,2,8,128]{3,2,1,0:T(8,128)S(1)}, u32[]{:S(2)}, u32[]{:S(2)}) collective-permute-start(f32[3,2,8,128]{3,2,1,0:T(8,128)S(1)} %get-tuple-element.39), channel_id=1, source_target_pairs={{0,16},{1,17},{2,18},{3,19},{4,20},{5,21},{6,22},{7,23},{8,24},{9,... | collective-permute-start | bytes 73736 | tf_op jit(solution)/shard_map/ppermute | solution.py:440
  64.8 2.4 %collective-permute-done.5.rb = f32[3,2,8,128]{3,2,1,0:T(8,128)S(1)} collective-permute-done((f32[3,2,8,128]{3,2,1,0:T(8,128)S(1)}, f32[3,2,8,128]{3,2,1,0:T(8,128)S(1)}, u32[]{:S(2)}, u32[]{:S(2)}) %collective-permute-start.5) | collective-permute-done | bytes 24608 | tf_op jit(solution)/shard_map/ppermute | solution.py:439
  67.2 3.0 %hessian_kernel.1 = (f32[3,2,64,128]{3,2,1,0:T(8,128)S(1)}, f32[3,2,8,128]{3,2,1,0:T(8,128)S(1)}, f32[3,2,8,128]{3,2,1,0:T(8,128)S(1)}) custom-call(f32[3,2,64,128]{3,2,1,0:T(8,128)S(1)} %get-tuple-element.38.center.g, f32[3,2,8,128]{3,2,1,0:T(8,128)S(1)} %collective-permute-done.4.ra, f32[3,2,8,128]{3,2,1,0:T(8,128)S(1)} %collective-permute-done.5.rb, ...), custom_call_target="tpu_custom_call" | custom-call | tf_op jit(solution)/shard_map/hessian_kernel/pallas_call | solution.py:421
  70.2 3.5 %collective-permute-start.6 = (f32[3,2,8,128]{3,2,1,0:T(8,128)S(1)}, f32[3,2,8,128]{3,2,1,0:T(8,128)S(1)}, u32[]{:S(2)}, u32[]{:S(2)}) collective-permute-start(f32[3,2,8,128]{3,2,1,0:T(8,128)S(1)} %get-tuple-element.42), channel_id=1, source_target_pairs={{0,16},{1,17},{2,18},{3,19},{4,20},{5,21},{6,22},{7,23},{8,24},{9,... | collective-permute-start | bytes 73736 | tf_op jit(solution)/shard_map/ppermute | solution.py:440
  74.6 2.4 %collective-permute-done.7.rb = f32[3,2,8,128]{3,2,1,0:T(8,128)S(1)} collective-permute-done((f32[3,2,8,128]{3,2,1,0:T(8,128)S(1)}, f32[3,2,8,128]{3,2,1,0:T(8,128)S(1)}, u32[]{:S(2)}, u32[]{:S(2)}) %collective-permute-start.7) | collective-permute-done | bytes 24608 | tf_op jit(solution)/shard_map/ppermute | solution.py:439
  77.0 3.4 %last_kernel.1 = (f32[8,9,16,128]{3,2,1,0:T(8,128)S(1)}, f32[128,128]{1,0:T(8,128)S(1)}) custom-call(f32[3,2,64,128]{3,2,1,0:T(8,128)S(1)} %get-tuple-element.38.center.g, f32[3,2,64,128]{3,2,1,0:T(8,128)S(1)} %get-tuple-element.41.center, f32[3,2,8,128]{3,2,1,0:T(8,128)S(1)} %collective-permute-done.6.ra, f32[3,2,8,128]{3,2,1,0:T(8,128)S(1)} %collective-permute-done.7.rb, ...), custom_call_target="tpu_custom_call" | custom-call | tf_op jit(solution)/shard_map/last_kernel/pallas_call | solution.py:421
  80.4 21.5 %all_to_all.26 = f32[128,1,128]{2,1,0:T(1,128)S(1)} all-to-all(f32[128,1,128]{2,1,0:T(1,128)S(1)} %bitcast.10), channel_id=1, replica_groups=mesh['lat'=8,'lon'=16] {'lat','lon'}, dimensions={0} | all-to-all | bytes 131072 | tf_op jit(solution)/shard_map/all_to_all | solution.py:532
  101.9 13.5 %all_to_all.27.x = f32[8,9,16,128]{3,2,1,0:T(8,128)S(1)} all-to-all(f32[8,9,16,128]{3,2,1,0:T(8,128)S(1)} %get-tuple-element.44), channel_id=1, replica_groups=mesh['lat'=8,'lon'=16] {'lat'}, dimensions={0} | all-to-all | bytes 1179648 | tf_op jit(solution)/shard_map/all_to_all | solution.py:533
  115.3 1.0 final_kernel.1
  (11 shorter events, 4.1 us)
Async XLA Ops:
  2.8 15.8 %all-to-all-start = ((f32[8,9,16,128]{3,2,1,0:T(8,128)}), f32[8,9,16,128]{3,2,1,0:T(8,128)S(1)}, u32[]{:S(2)}, u32[]{:S(2)}) async-start(f32[8,9,16,128]{3,2,1,0:T(8,128)} %prep_kernel.1), calls=%async_computation | async-start | bytes 1179648 | tf_op jit(solution)/shard_map/all_to_all | solution.py:455
  18.6 23.2 %all-to-all-start.1 = ((f32[128,8,128]{2,1,0:T(8,128)}), f32[128,8,128]{2,1,0:T(8,128)S(1)}, u32[]{:S(2)}, u32[]{:S(2)}) async-start(f32[128,8,128]{2,1,0:T(8,128)} %pack_kernel.1), calls=%async_computation.1 | async-start | bytes 1048576 | tf_op jit(solution)/shard_map/all_to_all | solution.py:476
  28.7 2.1 %collective-permute-start = (f32[9,2,8,128]{3,2,1,0:T(8,128)S(1)}, f32[9,2,8,128]{3,2,1,0:T(8,128)S(1)}, u32[]{:S(2)}, u32[]{:S(2)}) collective-permute-start(f32[9,2,8,128]{3,2,1,0:T(8,128)S(1)} %get-tuple-element.27), channel_id=1, source_target_pairs={{0,16},{1,17},{2,18},{3,19},{4,20},{5,21},{6,22},{7,23},{8,24},{9,... | collective-permute-start | bytes 221192 | tf_op jit(solution)/shard_map/ppermute | solution.py:440
  29.8 6.1 %collective-permute-start.1 = (f32[9,2,8,128]{3,2,1,0:T(8,128)S(1)}, f32[9,2,8,128]{3,2,1,0:T(8,128)S(1)}, u32[]{:S(2)}, u32[]{:S(2)}) collective-permute-start(f32[9,2,8,128]{3,2,1,0:T(8,128)S(1)} %get-tuple-element.28), channel_id=1, source_target_pairs={{0,31},{1,16},{2,17},{3,18},{4,19},{5,20},{6,21},{7,22},{8,23},{9,... | collective-permute-start | bytes 221192 | tf_op jit(solution)/shard_map/ppermute | solution.py:439
  41.8 0.8 copy-start
  42.6 1.0 copy-start.1
  53.3 4.0 %collective-permute-start.2 = (f32[4,3,2,8,128]{4,3,2,1,0:T(8,128)S(1)}, f32[4,3,2,8,128]{4,3,2,1,0:T(8,128)S(1)}, u32[]{:S(2)}, u32[]{:S(2)}) collective-permute-start(f32[4,3,2,8,128]{4,3,2,1,0:T(8,128)S(1)} %get-tuple-element.32), channel_id=1, source_target_pairs={{0,16},{1,17},{2,18},{3,19},{4,20},{5,21},{6,22},{7,23},{8,24},{9,... | collective-permute-start | bytes 294920 | tf_op jit(solution)/shard_map/ppermute | solution.py:440
  54.1 5.9 %collective-permute-start.3 = (f32[4,3,2,8,128]{4,3,2,1,0:T(8,128)S(1)}, f32[4,3,2,8,128]{4,3,2,1,0:T(8,128)S(1)}, u32[]{:S(2)}, u32[]{:S(2)}) collective-permute-start(f32[4,3,2,8,128]{4,3,2,1,0:T(8,128)S(1)} %get-tuple-element.33), channel_id=1, source_target_pairs={{0,31},{1,16},{2,17},{3,18},{4,19},{5,20},{6,21},{7,22},{8,23},{9,... | collective-permute-start | bytes 294920 | tf_op jit(solution)/shard_map/ppermute | solution.py:439
  62.3 2.5 %collective-permute-start.4 = (f32[3,2,8,128]{3,2,1,0:T(8,128)S(1)}, f32[3,2,8,128]{3,2,1,0:T(8,128)S(1)}, u32[]{:S(2)}, u32[]{:S(2)}) collective-permute-start(f32[3,2,8,128]{3,2,1,0:T(8,128)S(1)} %get-tuple-element.39), channel_id=1, source_target_pairs={{0,16},{1,17},{2,18},{3,19},{4,20},{5,21},{6,22},{7,23},{8,24},{9,... | collective-permute-start | bytes 73736 | tf_op jit(solution)/shard_map/ppermute | solution.py:440
  64.0 3.3 %collective-permute-start.5 = (f32[3,2,8,128]{3,2,1,0:T(8,128)S(1)}, f32[3,2,8,128]{3,2,1,0:T(8,128)S(1)}, u32[]{:S(2)}, u32[]{:S(2)}) collective-permute-start(f32[3,2,8,128]{3,2,1,0:T(8,128)S(1)} %get-tuple-element.40), channel_id=1, source_target_pairs={{0,31},{1,16},{2,17},{3,18},{4,19},{5,20},{6,21},{7,22},{8,23},{9,... | collective-permute-start | bytes 73736 | tf_op jit(solution)/shard_map/ppermute | solution.py:439
  70.2 4.4 %collective-permute-start.6 = (f32[3,2,8,128]{3,2,1,0:T(8,128)S(1)}, f32[3,2,8,128]{3,2,1,0:T(8,128)S(1)}, u32[]{:S(2)}, u32[]{:S(2)}) collective-permute-start(f32[3,2,8,128]{3,2,1,0:T(8,128)S(1)} %get-tuple-element.42), channel_id=1, source_target_pairs={{0,16},{1,17},{2,18},{3,19},{4,20},{5,21},{6,22},{7,23},{8,24},{9,... | collective-permute-start | bytes 73736 | tf_op jit(solution)/shard_map/ppermute | solution.py:440
  73.7 3.3 %collective-permute-start.7 = (f32[3,2,8,128]{3,2,1,0:T(8,128)S(1)}, f32[3,2,8,128]{3,2,1,0:T(8,128)S(1)}, u32[]{:S(2)}, u32[]{:S(2)}) collective-permute-start(f32[3,2,8,128]{3,2,1,0:T(8,128)S(1)} %get-tuple-element.43), channel_id=1, source_target_pairs={{0,31},{1,16},{2,17},{3,18},{4,19},{5,20},{6,21},{7,22},{8,23},{9,... | collective-permute-start | bytes 73736 | tf_op jit(solution)/shard_map/ppermute | solution.py:439

commit v3 on v2

--- a/solution.py
+++ b/solution.py
@@ -5,14 +5,16 @@
 from jax.experimental.pallas import tpu as pltpu
 from jax.sharding import PartitionSpec as P
 
+
 LAT = 8
 LON = 16
 ALL = 128
 STEPS = 4
 LV = 3
 COL = 64
-EDGE = 8
+EDGE = 24
 EXT = COL + 2 * EDGE
+SLAB = 40
 ROOM = 256
 ROWS = STEPS * LV * COL
 F32 = jnp.float32
@@ -67,11 +69,13 @@
         t = x[:, f].reshape(128, 128).T
         for u in range(2):
             center[f, u] = t[u * 64 : u * 64 + 64]
-            put_edges(sa, sb, (f, u), t[u * 64 : u * 64 + 8], t[u * 64 + 56 : u * 64 + 64], h)
+            lo = t[u * 64 : u * 64 + EDGE]
+            hi = t[u * 64 + COL - EDGE : u * 64 + COL]
+            put_edges(sa, sb, (f, u), lo, hi, h)
 
 
 def up(x):
-    return pltpu.roll(x, EXT - 1, 0)
+    return pltpu.roll(x, x.shape[0] - 1, 0)
 
 
 def down(x):
@@ -141,7 +145,7 @@
     return out
 
 
-def pack_kernel(count, tile, cell, step, value, weight, out, rows, base, acc, left, right):
+def pack_kernel(count, tile, cell, step, value, weight, out, rows, member, counted, acc, left, right):
     shape = (16, 128)
     live = sublanes(shape) * 128 + lanes(shape) < count[0]
     c, t = cell[...], tile[...]
@@ -166,38 +170,36 @@
     rows[6] = v0
     rows[7] = v1
     rows[8] = wv - v0 - v1
-    base[...] = jnp.zeros_like(base)
-    acc[...] = jnp.zeros_like(acc)
     square = (128, 256)
     before = ((sublanes(square) < lanes(square)) | (lanes(square) >= 128)).astype(F32).astype(BF16)
     ids = sublanes((128, 128)).astype(F32)
     places = sublanes((ROOM, 128)).astype(F32)
-
-    def block(i, carry):
-        for j in range(2):
-            line = lambda n: rows[n, pl.ds(2 * i + j, 1), :]
-            at = slice(j * 128, j * 128 + 128)
-            mine = ids == line(0)
-            member = jnp.where(mine, 1.0, 0.0)
-            counted = jnp.dot(member.astype(BF16), before, preferred_element_type=F32)
-            rank = jnp.sum(member * (counted[:, :128] + base[...]), axis=0, keepdims=True)
-            base[...] += counted[:, 128:]
-            right[:, at] = jnp.where(places == rank, 1.0, 0.0).astype(BF16)
-            for p in range(8):
-                left[p * 128 : p * 128 + 128, at] = jnp.where(mine, line(1 + p), 0.0).astype(BF16)
-        acc[...] += lax.dot_general(
-            left[...], right[...], (((1,), (1,)), ((), ())), preferred_element_type=F32
-        )
-        return carry
-
-    lax.fori_loop(0, 8, block, 0)
+    for b in range(16):
+        at = slice(b * 128, b * 128 + 128)
+        mine = ids == rows[0, b : b + 1, :]
+        member[at, :] = jnp.where(mine, 1.0, 0.0).astype(BF16)
+        for p in range(8):
+            piece = rows[1 + p, b : b + 1, :]
+            left[p * 128 : p * 128 + 128, at] = jnp.where(mine, piece, 0.0).astype(BF16)
+    counted[...] = jnp.dot(member[...], before, preferred_element_type=F32)
+    base = jnp.zeros((128, 128), F32)
+    for b in range(16):
+        at = slice(b * 128, b * 128 + 128)
+        mine = ids == rows[0, b : b + 1, :]
+        rank = jnp.where(mine, counted[at, :128] + base, 0.0)
+        rank = jnp.sum(rank, axis=0, keepdims=True)
+        base = base + counted[at, 128:]
+        right[:, at] = jnp.where(places == rank, 1.0, 0.0).astype(BF16)
+    acc[...] = lax.dot_general(
+        left[...], right[...], (((1,), (1,)), ((), ())), preferred_element_type=F32
+    )
     for ch, pieces in enumerate(((0, 1), (2,), (3, 4), (5, 6, 7))):
         for hf in range(2):
             at = slice(hf * 128, hf * 128 + 128)
             out[:, 2 * ch + hf, :] = sum(acc[p * 128 : p * 128 + 128, at] for p in pieces)
 
 
-def scatter_kernel(x, after, wsum, vsum, sa, sb, xt, at, bt, acc):
+def scatter_kernel(x, wsum, vsum, sa, sb, xt, at, bt, acc):
     h = half()
     most = jnp.max(x[:, 2:4, :], axis=0)
     total = jnp.sum(jnp.where(most > 0.5, 1.0, 0.0)).astype(I32)
@@ -249,15 +251,11 @@
                 v = take(2) + take(3) + take(4)
                 wsum[k, l, u] = w
                 vsum[k, l, u] = v
-                lo = jnp.where(low, w[:8], pltpu.roll(v[:8], 4, 0))
-                hi = jnp.where(low, pltpu.roll(v[56:], 4, 0), w[56:])
+                mix = jnp.where(low, w[16:24], pltpu.roll(v[16:24], 4, 0))
+                lo = jnp.concatenate([w[:16], v[:16], mix], axis=0)
+                mix = jnp.where(low, pltpu.roll(v[40:48], 4, 0), w[40:48])
+                hi = jnp.concatenate([w[48:], v[48:], mix], axis=0)
                 put_edges(sa, sb, (k, l, u), lo, hi, h)
-
-
-def keep(x, out, sa, sb, l, h):
-    for u in range(2):
-        out[l, u] = x[u][EDGE : EDGE + COL]
-        put_edges(sa, sb, (l, u), x[u][EDGE : 2 * EDGE], x[u][COL : COL + EDGE], h)
 
 
 def fetch(sources, buffers, sems):
@@ -273,113 +271,110 @@
     return levels
 
 
-def gradient_kernel(
-    wsum, vsum, ra, rb, states_in, gains_in, drifts_in, cn_in, cs_in, out, sa, sb, *scratch
+def hessian(p, wide, gains, drifts, n, s):
+    e, seen = p, []
+    for k in range(STEPS):
+        e = tangent(e, gains(k), drifts(k), n, s)
+        w = wide(k)
+        seen.append([w[u] * e[u] for u in range(2)])
+    x = None
+    for k in reversed(range(STEPS)):
+        x = seen[k] if x is None else [x[u] + seen[k][u] for u in range(2)]
+        x = adjoint(x, gains(k), drifts(k), n, s)
+    return [p[u] + x[u] for u in range(2)]
+
+
+def core_kernel(
+    ra, rb, w_in, v_in, states_in, gains_in, drifts_in, cn_in, cs_in, out, *scratch
 ):
     *buffers, sems = scratch
     h = half()
-    levels = fetch((states_in, gains_in, drifts_in, cn_in, cs_in), buffers, sems)
-    states, gains, drifts, cn, cs = buffers
+    levels = fetch((w_in, v_in, states_in, gains_in, drifts_in, cn_in, cs_in), buffers, sems)
+    wsum, vsum, states, gains, drifts, cn, cs = buffers
+    sums = [jnp.zeros((8, 128), F32) for _ in range(5)]
+
+    def fold(a, b):
+        prod = a * b
+        return jnp.sum(prod.reshape(8, 8, 128), axis=0)
+
     for l in range(LV):
         for copy in levels[l]:
             copy.wait()
-        n = [cn[l, u] for u in range(2)]
-        s = [cs[l, u] for u in range(2)]
+
+        def window(ref, first):
+            return lambda k: [ref[k, l, u, first : EXT - first] for u in range(2)]
+
+        def still(ref, first):
+            return [ref[l, u, first : EXT - first] for u in range(2)]
+
+        def weights(first):
+            def at(k):
+                got = []
+                for u in range(2):
+                    left, right = get_edges(ra, rb, (k, l, u), h)
+                    skip = first - 8
+                    got.append(
+                        jnp.concatenate(
+                            [left[skip:16], wsum[k, l, u], right[: 16 - skip]], axis=0
+                        )
+                    )
+                return got
+
+            return at
+
+        n, s = still(cn, 0), still(cs, 0)
         x = None
         for k in reversed(range(STEPS)):
             m = []
             for u in range(2):
                 left, right = get_edges(ra, rb, (k, l, u), h)
-                w = jnp.concatenate([left, wsum[k, l, u], right], axis=0)
-                v = jnp.concatenate(
-                    [pltpu.roll(left, 4, 0), vsum[k, l, u], pltpu.roll(right, 4, 0)], axis=0
-                )
+                lm, rm = left[32:], right[32:]
+                w = jnp.concatenate([lm, left[:16], wsum[k, l, u], right[:16], rm], axis=0)
+                lm, rm = pltpu.roll(lm, 4, 0), pltpu.roll(rm, 4, 0)
+                v = jnp.concatenate([lm, left[16:32], vsum[k, l, u], right[16:32], rm], axis=0)
                 m.append(v - w * states[k, l, u])
             x = m if x is None else [x[u] + m[u] for u in range(2)]
-            x = adjoint(
-                x, [gains[k, l, u] for u in range(2)], [drifts[k, l, u] for u in range(2)], n, s
+            x = adjoint(x, window(gains, 0)(k), window(drifts, 0)(k), n, s)
+        vectors = [x]
+        for first in (8, 16):
+            p = [x[u][8 : x[u].shape[0] - 8] for u in range(2)]
+            x = hessian(
+                p,
+                weights(first),
+                window(gains, first),
+                window(drifts, first),
+                still(cn, first),
+                still(cs, first),
             )
-        keep(x, out, sa, sb, l, h)
-
-
-def hessian(l, p, wide, gains, drifts, cn, cs):
-    n = [cn[l, u] for u in range(2)]
-    s = [cs[l, u] for u in range(2)]
-    g = lambda k: [gains[k, l, u] for u in range(2)]
-    d = lambda k: [drifts[k, l, u] for u in range(2)]
-    e, seen = p, []
-    for k in range(STEPS):
-        e = tangent(e, g(k), d(k), n, s)
-        w = wide(k)
-        seen.append([w[u] * e[u] for u in range(2)])
-    x = None
-    for k in reversed(range(STEPS)):
-        x = seen[k] if x is None else [x[u] + seen[k][u] for u in range(2)]
-        x = adjoint(x, g(k), d(k), n, s)
-    return [p[u] + x[u] for u in range(2)]
-
-
-def extended(center, ra, rb, index, h):
-    out = []
-    for u in range(2):
-        left, right = get_edges(ra, rb, index + (u,), h)
-        out.append(jnp.concatenate([left, center[index + (u,)], right], axis=0))
-    return out
-
-
-def hessian_kernel(
-    center, ra, rb, wsum, wa, wb, gains_in, drifts_in, cn_in, cs_in, out, sa, sb, *scratch
-):
-    *buffers, sems = scratch
-    h = half()
-    levels = fetch((gains_in, drifts_in, cn_in, cs_in), buffers, sems)
-    for l in range(LV):
-        p = extended(center, ra, rb, (l,), h)
-        for copy in levels[l]:
-            copy.wait()
-        wide = lambda k: extended(wsum, wa, wb, (k, l), h)
-        keep(hessian(l, p, wide, *buffers), out, sa, sb, l, h)
-
-
-def last_kernel(
-    g, center, ra, rb, wsum, wa, wb, gains_in, drifts_in, cn_in, cs_in, out, table_ref, *scratch
-):
-    *buffers, sems = scratch
-    h = half()
-    levels = fetch((gains_in, drifts_in, cn_in, cs_in), buffers, sems)
-    sums = [jnp.zeros((8, 128), F32) for _ in range(5)]
-
-    def fold(a, b):
-        prod = a * b
-        return jnp.sum(prod.reshape(8, 8, 128), axis=0)
-
-    for l in range(LV):
-        p = extended(center, ra, rb, (l,), h)
-        for copy in levels[l]:
-            copy.wait()
-        wide = lambda k: extended(wsum, wa, wb, (k, l), h)
-        y = hessian(l, p, wide, *buffers)
+            vectors.append(x)
         v = [
-            [g[l, u] for u in range(2)],
-            [center[l, u] for u in range(2)],
-            [y[u][EDGE : EDGE + COL] for u in range(2)],
+            [y[u][edge : edge + COL] for u in range(2)] for y, edge in zip(vectors, (24, 16, 8))
         ]
         for i, (a, b) in enumerate(((0, 0), (0, 1), (1, 1), (0, 2), (1, 2))):
             for u in range(2):
                 sums[i] = sums[i] + fold(v[a][u], v[b][u])
         for i in range(3):
-            t = jnp.concatenate(v[i], axis=0).T.reshape(LAT, 16, 128)
-            out[:, i * 3 + l] = t
+            t = jnp.concatenate(v[i], axis=0).T
+            for b in range(LAT):
+                first = (i * 3 + l) * 16
+                out[b, first : first + 16] = t[b * 16 : b * 16 + 16]
     lane = lanes((1, 128))
     table = jnp.zeros((1, 128), F32)
     for i in range(5):
         whole = jnp.sum(jnp.sum(sums[i], axis=0, keepdims=True), axis=1, keepdims=True)
         table = jnp.where(lane == i, whole, table)
-    table_ref[...] = jnp.broadcast_to(table, (ALL, 128))
+    for b in range(LAT):
+        out[b, 144:] = jnp.broadcast_to(table, (8, 128))
+
+
+def share_kernel(x, out):
+    total = jnp.sum(x[:, 144:152], axis=0)
+    for j in range(LON):
+        out[j] = total
 
 
 def final_kernel(x, parts, increment, residual):
-    total = jnp.sum(parts[...], axis=0, keepdims=True)
+    total = jnp.sum(parts[...], axis=0)[:1]
     lane = lanes((1, 128))
     pick = lambda i: jnp.sum(jnp.where(lane == i, total, 0.0), axis=1, keepdims=True)
     a00, a01, a11, a02, a12 = [jnp.broadcast_to(pick(i), (1, 128)) for i in range(5)]
@@ -395,7 +390,9 @@
         q, l = level // 3, level % 3
         got = []
         for h in range(2):
-            v0, v1, v2 = [x[2 * q + h, i * 3 + l] for i in range(3)]
+            v0, v1, v2 = [
+                x[2 * q + h, (i * 3 + l) * 16 : (i * 3 + l) * 16 + 16] for i in range(3)
+            ]
             got.append((a * v0 - b * v1, v0 - a * v1 + b * v2))
         for i, ref in enumerate((increment, residual)):
             x0, x1 = got[0][i], got[1][i]
@@ -418,14 +415,17 @@
         pltpu.with_memory_space_constraint(a, pltpu.VMEM) if i == "v" else a
         for a, i in zip(args, ins)
     ]
+    return make(kernel, shapes, ins, scratch)(*args)
+
+
+def make(kernel, shapes, ins, scratch):
     return pl.pallas_call(
         kernel,
         out_shape=shapes if len(shapes) > 1 else shapes[0],
         in_specs=[{"s": SM, "a": AN}.get(i, VM) for i in ins],
         out_specs=(VM,) * len(shapes) if len(shapes) > 1 else VM,
         scratch_shapes=list(scratch),
-        name=kernel.__name__,
-    )(*args)
+    )
 
 
 def swap(sa, sb):
@@ -446,13 +446,8 @@
 ):
     both = ("lat", "lon")
     plane = (LV, 2, EXT, 128)
-    edge = (LV, 2, EDGE, 128)
     middle = (LV, 2, COL, 128)
 
-    sent = call(
-        prep_kernel, [(LAT, 9, 16, 128)], background, wind_lon, wind_lat, ins="hhh"
-    )
-    moved = lax.all_to_all(sent, "lat", 0, 0, tiled=True)
     fold = lambda a: a.reshape(16, 128)
     packed = call(
         pack_kernel,
@@ -466,25 +461,28 @@
         ins="shhhhh",
         scratch=[
             pltpu.VMEM((9, 16, 128), F32),
-            pltpu.VMEM((128, 128), F32),
+            pltpu.VMEM((2048, 128), BF16),
+            pltpu.VMEM((2048, 256), F32),
             pltpu.VMEM((1024, 256), F32),
-            pltpu.VMEM((1024, 256), BF16),
-            pltpu.VMEM((256, 256), BF16),
+            pltpu.VMEM((1024, 2048), BF16),
+            pltpu.VMEM((256, 2048), BF16),
         ],
     )
-    moved, packed = lax.optimization_barrier((moved, packed))
     arrived = lax.all_to_all(packed, both, 0, 0, tiled=True)
-    fields, sa, sb = call(recv_kernel, [(9, 2, COL, 128)] + [(9, 2, EDGE, 128)] * 2, moved)
+    sent = call(prep_kernel, [(LAT, 9, 16, 128)], background, wind_lon, wind_lat, ins="hhh")
+    moved = lax.all_to_all(sent, "lat", 0, 0, tiled=True)
+    fields, sa, sb = call(
+        recv_kernel,
+        [(9, 2, COL, 128)] + [(9, 2, EDGE, 128)] * 2,
+        moved,
+        space="hvv",
+    )
     ra, rb = swap(sa, sb)
-    states, gains, drifts, cn, cs = call(
-        forward_kernel, [(STEPS,) + plane] * 3 + [plane] * 2, fields, ra, rb, space="h"
-    )
     wsum, vsum, sa, sb = call(
         scatter_kernel,
-        [(STEPS,) + middle] * 2 + [(STEPS,) + edge] * 2,
+        [(STEPS,) + middle] * 2 + [(STEPS, LV, 2, SLAB, 128)] * 2,
         arrived,
-        cn,
-        ins="va",
+        space="hhvv",
         scratch=[
             pltpu.VMEM((4, 256, 128), F32),
             pltpu.VMEM((ROWS, 1024), BF16),
@@ -493,50 +491,32 @@
         ],
     )
     wa, wb = swap(sa, sb)
+    coefs = call(
+        forward_kernel, [(STEPS,) + plane] * 3 + [plane] * 2, fields, ra, rb, ins="hvv", space="h"
+    )
     big = pltpu.VMEM((STEPS,) + plane, F32)
+    mid = pltpu.VMEM((STEPS,) + middle, F32)
     small = pltpu.VMEM(plane, F32)
-    sems = lambda n: pltpu.SemaphoreType.DMA((LV, n))
-    g, sa, sb = call(
-        gradient_kernel,
-        [middle, edge, edge],
+    sent = call(
+        core_kernel,
+        [(LAT, 152, 128)],
+        wa,
+        wb,
         wsum,
         vsum,
-        wa,
-        wb,
-        states,
-        gains,
-        drifts,
-        cn,
-        cs,
-        ins="vvvvaaaaa",
-        scratch=[big, big, big, small, small, sems(5)],
-    )
-    ra, rb = swap(sa, sb)
-    coefs = (wsum, wa, wb, gains, drifts, cn, cs)
-    scratch = [big, big, small, small, sems(4)]
-    hg, sa, sb = call(
-        hessian_kernel, [middle, edge, edge], g, ra, rb, *coefs, ins="vvvvvvaaaa", scratch=scratch
-    )
-    ra, rb = swap(sa, sb)
-    sent, table = call(
-        last_kernel,
-        [(LAT, 9, 16, 128), (ALL, 128)],
-        g,
-        hg,
-        ra,
-        rb,
         *coefs,
-        ins="vvvvvvvaaaa",
-        scratch=scratch,
-    )
-    parts = lax.all_to_all(table, both, 0, 0, tiled=True)
+        ins="vv" + "a" * 7,
+        scratch=[mid, mid, big, big, big, small, small, pltpu.SemaphoreType.DMA((LV, 7))],
+    )
     moved = lax.all_to_all(sent, "lat", 0, 0, tiled=True)
+    parts = lax.all_to_all(call(share_kernel, [(LON, 8, 128)], moved), "lon", 0, 0, tiled=True)
     return call(final_kernel, [(12, 32, 128)] * 2, moved, parts, space="h")
 
 
 def solution(mesh):
     grid = P(None, "lat", "lon")
     flat = P(("lat", "lon"))
+
     return jax.shard_map(
         on_device,
         mesh=mesh,

time: 117 us -> 99.9 us (0.85)
  blocking collectives: 35 us -> 26.8 us
  starting transfers between devices: 26.2 us -> 20.3 us
  local copies, waits for them, and re-layouts: 1.83 us -> 0 us
  waiting for transfers between devices: 20.9 us -> 19.5 us
    all_to_all x1, blocking collectives: 21.5 us -> 10.8 us  [on_device(): lax.all_to_all(call(share_kernel, [(LON, 8, 128)], moved), 'lon', 0, 0, t...]
    all_to_all x1, waiting for transfers between devices: 3.55 us -> 11.9 us  [on_device(): arrived = lax.all_to_all(packed, both, 0, 0, tiled=True)]
    ppermute x4 -> x2, waiting for transfers between devices: 12.6 us -> 7.63 us  [swap(): rb = lax.ppermute(sb, ('lat', 'lon'), far)]
    ppermute x4 -> x2, starting transfers between devices: 7.05 us -> 3.09 us  [swap(): ra = lax.ppermute(sa, ('lat', 'lon'), near)]
    all_to_all x1, waiting for transfers between devices: 3.12 us -> 0.01 us  [on_device(): moved = lax.all_to_all(sent, 'lat', 0, 0, tiled=True)]
    all_to_all x1, blocking collectives: 13.5 us -> 16 us  [on_device(): moved = lax.all_to_all(sent, 'lat', 0, 0, tiled=True)]
    ppermute x4 -> x2, starting transfers between devices: 4.25 us -> 1.73 us  [swap(): rb = lax.ppermute(sb, ('lat', 'lon'), far)]
    all_to_all x1, starting transfers between devices: 9.11 us -> 11.5 us  [on_device(): arrived = lax.all_to_all(packed, both, 0, 0, tiled=True)]
  transfers between devices with their start and end apart: 10 -> 6, of which waited for: 9 -> 2; matrix products, arithmetic and copies ran while one was open for 0% -> 0% of each run, Pallas kernels for 8% -> 19%
where the time goes in v3:
time: 99.9 us; the launch traced here: 98.6 us
  Pallas kernels  30.6 us (31%)
  blocking collectives  26.8 us (27%)
  starting transfers between devices  20.3 us (20%)
  waiting for transfers between devices  19.5 us (20%)
  between operations  1.31 us (1%)
    pallas_call x8, Pallas kernels, call(): return make(kernel, shapes, ins, scratch)(*args)  30.6 us
    all_to_all x1, blocking collectives, on_device(): moved = lax.all_to_all(sent, 'lat', 0, 0, tiled=True)  16 us
    all_to_all x1, waiting for transfers between devices, on_device(): arrived = lax.all_to_all(packed, both, 0, 0, tiled=True)  11.9 us
    all_to_all x1, starting transfers between devices, on_device(): arrived = lax.all_to_all(packed, both, 0, 0, tiled=True)  11.5 us
    all_to_all x1, blocking collectives, on_device(): lax.all_to_all(call(share_kernel, [(LON, 8, 128)], moved), 'lon', 0, 0, t...  10.8 us
    ppermute x2, waiting for transfers between devices, swap(): rb = lax.ppermute(sb, ('lat', 'lon'), far)  7.63 us
    all_to_all x1, starting transfers between devices, on_device(): moved = lax.all_to_all(sent, 'lat', 0, 0, tiled=True)  4.03 us
    ppermute x2, starting transfers between devices, swap(): ra = lax.ppermute(sa, ('lat', 'lon'), near)  3.09 us
  transfers between devices with their start and end apart: 6, of which 2 were waited for; matrix products, arithmetic and copies ran while one was open for 0% of the time, Pallas kernels for 19%

profile of v3, /device:TPU:1, one launch (start us, length us, event | category | flops | bytes accessed | tf_op | source)
XLA Modules:
  0.0 98.6 jit_solution(11408474686163636954)
XLA Ops:
  1.3 3.9 %shard_map.104 = f32[128,8,128]{2,1,0:T(8,128)} custom-call(s32[1]{0:T(128)S(6)} %copy.11.count, s32[16,128]{1,0:T(8,128)} %bitcast.5, s32[16,128]{1,0:T(8,128)} %bitcast.6, s32[16,128]{1,0:T(8,128)} %bitcast.7, f32[16,128]{1,0:T(8,128)} %bitcast.8, f32[16,128]{1,0:T(8,128)} %bitcast.9), custom_call_target="tpu_custom_call" | custom-call | tf_op jit(solution)/shard_map/pallas_call | solution.py:418
  5.2 11.5 %all-to-all-start = ((f32[128,8,128]{2,1,0:T(8,128)}), f32[128,8,128]{2,1,0:T(8,128)S(1)}, u32[]{:S(2)}, u32[]{:S(2)}) async-start(f32[128,8,128]{2,1,0:T(8,128)} %shard_map.104), calls=%async_computation | async-start | bytes 1048576 | tf_op jit(solution)/shard_map/all_to_all | solution.py:471
  16.7 2.1 %shard_map.106 = f32[8,9,16,128]{3,2,1,0:T(8,128)} custom-call(f32[12,32,128]{2,1,0:T(8,128)} %bg.1, f32[12,32,128]{2,1,0:T(8,128)} %wl.1, f32[12,32,128]{2,1,0:T(8,128)} %wt.1), custom_call_target="tpu_custom_call" | custom-call | tf_op jit(solution)/shard_map/pallas_call | solution.py:418
  18.9 11.9 %all-to-all-done.x = f32[128,8,128]{2,1,0:T(8,128)S(1)} async-done(((f32[128,8,128]{2,1,0:T(8,128)}), f32[128,8,128]{2,1,0:T(8,128)S(1)}, u32[]{:S(2)}, u32[]{:S(2)}) %all-to-all-start) | async-done | bytes 524320 | tf_op jit(solution)/shard_map/all_to_all | solution.py:471
  30.8 4.0 %all-to-all-start.1 = ((f32[8,9,16,128]{3,2,1,0:T(8,128)}), f32[8,9,16,128]{3,2,1,0:T(8,128)S(1)}, u32[]{:S(2)}, u32[]{:S(2)}) async-start(f32[8,9,16,128]{3,2,1,0:T(8,128)} %shard_map.106), calls=%async_computation.1 | async-start | bytes 1179648 | tf_op jit(solution)/shard_map/all_to_all | solution.py:473
  34.8 11.2 %shard_map.105 = (f32[4,3,2,64,128]{4,3,2,1,0:T(8,128)}, f32[4,3,2,64,128]{4,3,2,1,0:T(8,128)}, f32[4,3,2,40,128]{4,3,2,1,0:T(8,128)}, f32[4,3,2,40,128]{4,3,2,1,0:T(8,128)}) custom-call(f32[128,8,128]{2,1,0:T(8,128)S(1)} %all-to-all-done.x), custom_call_target="tpu_custom_call" | custom-call | tf_op jit(solution)/shard_map/pallas_call | solution.py:418
  46.0 3.1 %collective-permute-start = (f32[4,3,2,40,128]{4,3,2,1,0:T(8,128)}, f32[4,3,2,40,128]{4,3,2,1,0:T(8,128)S(1)}, u32[]{:S(2)}, u32[]{:S(2)}) collective-permute-start(f32[4,3,2,40,128]{4,3,2,1,0:T(8,128)} %get-tuple-element.14), channel_id=1, source_target_pairs={{0,16},{1,17},{2,18},{3,19},{4,20},{5,21},{6,22},{7,23},{8,24},{9,... | collective-permute-start | bytes 1474568 | tf_op jit(solution)/shard_map/ppermute | solution.py:440
  49.1 0.2 collective-permute-start.1
  49.3 0.0 all-to-all-done.1.x
  49.3 1.8 %shard_map.107 = (f32[9,2,64,128]{3,2,1,0:T(8,128)}, f32[9,2,24,128]{3,2,1,0:T(8,128)S(1)}, f32[9,2,24,128]{3,2,1,0:T(8,128)S(1)}) custom-call(f32[8,9,16,128]{3,2,1,0:T(8,128)S(1)} %all-to-all-done.1.x), custom_call_target="tpu_custom_call" | custom-call | tf_op jit(solution)/shard_map/pallas_call | solution.py:418
  51.1 0.0 collective-permute-start.2
  51.1 1.5 %collective-permute-start.3 = (f32[9,2,24,128]{3,2,1,0:T(8,128)S(1)}, f32[9,2,24,128]{3,2,1,0:T(8,128)S(1)}, u32[]{:S(2)}, u32[]{:S(2)}) collective-permute-start(f32[9,2,24,128]{3,2,1,0:T(8,128)S(1)} %get-tuple-element.20), channel_id=1, source_target_pairs={{0,31},{1,16},{2,17},{3,18},{4,19},{5,20},{6,21},{7,22},{8,23},{9,... | collective-permute-start | bytes 663560 | tf_op jit(solution)/shard_map/ppermute | solution.py:439
  52.6 0.0 collective-permute-done.2.ra
  52.6 7.6 %collective-permute-done.3.rb = f32[9,2,24,128]{3,2,1,0:T(8,128)S(1)} collective-permute-done((f32[9,2,24,128]{3,2,1,0:T(8,128)S(1)}, f32[9,2,24,128]{3,2,1,0:T(8,128)S(1)}, u32[]{:S(2)}, u32[]{:S(2)}) %collective-permute-start.3) | collective-permute-done | bytes 221216 | tf_op jit(solution)/shard_map/ppermute | solution.py:439
  60.2 4.0 %shard_map.108 = (f32[4,3,2,112,128]{4,3,2,1,0:T(8,128)}, f32[4,3,2,112,128]{4,3,2,1,0:T(8,128)}, f32[4,3,2,112,128]{4,3,2,1,0:T(8,128)}, f32[3,2,112,128]{3,2,1,0:T(8,128)}, f32[3,2,112,128]{3,2,1,0:T(8,128)}) custom-call(f32[9,2,64,128]{3,2,1,0:T(8,128)} %get-tuple-element.18.center, f32[9,2,24,128]{3,2,1,0:T(8,128)S(1)} %collective-permute-done.2.ra, ...), custom_call_target="tpu_custom_call" | custom-call | tf_op jit(solution)/shard_map/pallas_call | solution.py:418
  64.2 0.0 collective-permute-done.ra
  64.2 0.0 collective-permute-done.1.rb
  64.2 6.5 %shard_map.109 = f32[8,152,128]{2,1,0:T(8,128)S(1)} custom-call(f32[4,3,2,40,128]{4,3,2,1,0:T(8,128)S(1)} %collective-permute-done.ra, f32[4,3,2,40,128]{4,3,2,1,0:T(8,128)S(1)} %collective-permute-done.1.rb, f32[4,3,2,64,128]{4,3,2,1,0:T(8,128)} %get-tuple-element.16.w_in, f32[4,3,2,64,128]{4,3,2,1,0:T(8,128)} %get-tuple-element.17.v_in, ...), custom_call_target="tpu_custom_call" | custom-call | tf_op jit(solution)/shard_map/pallas_call | solution.py:418
  70.8 16.0 %all_to_all.20.x = f32[8,152,128]{2,1,0:T(8,128)S(1)} all-to-all(f32[8,152,128]{2,1,0:T(8,128)S(1)} %shard_map.109), channel_id=1, replica_groups=mesh['lat'=8,'lon'=16] {'lat'}, dimensions={0} | all-to-all | bytes 1245184 | tf_op jit(solution)/shard_map/all_to_all | solution.py:511
  86.8 10.8 %all_to_all.21.parts = f32[16,8,128]{2,1,0:T(8,128)S(1)} all-to-all(f32[16,8,128]{2,1,0:T(8,128)S(1)} %shard_map.110), channel_id=1, replica_groups=mesh['lat'=8,'lon'=16] {'lon'}, dimensions={0} | all-to-all | bytes 131072 | tf_op jit(solution)/shard_map/all_to_all | solution.py:512
  97.6 1.0 shard_map.111
  (1 shorter events, 0.0 us)
Async XLA Ops:
  5.2 25.5 %all-to-all-start = ((f32[128,8,128]{2,1,0:T(8,128)}), f32[128,8,128]{2,1,0:T(8,128)S(1)}, u32[]{:S(2)}, u32[]{:S(2)}) async-start(f32[128,8,128]{2,1,0:T(8,128)} %shard_map.104), calls=%async_computation | async-start | bytes 1048576 | tf_op jit(solution)/shard_map/all_to_all | solution.py:471
  30.8 18.6 %all-to-all-start.1 = ((f32[8,9,16,128]{3,2,1,0:T(8,128)}), f32[8,9,16,128]{3,2,1,0:T(8,128)S(1)}, u32[]{:S(2)}, u32[]{:S(2)}) async-start(f32[8,9,16,128]{3,2,1,0:T(8,128)} %shard_map.106), calls=%async_computation.1 | async-start | bytes 1179648 | tf_op jit(solution)/shard_map/all_to_all | solution.py:473
  46.0 18.2 %collective-permute-start = (f32[4,3,2,40,128]{4,3,2,1,0:T(8,128)}, f32[4,3,2,40,128]{4,3,2,1,0:T(8,128)S(1)}, u32[]{:S(2)}, u32[]{:S(2)}) collective-permute-start(f32[4,3,2,40,128]{4,3,2,1,0:T(8,128)} %get-tuple-element.14), channel_id=1, source_target_pairs={{0,16},{1,17},{2,18},{3,19},{4,20},{5,21},{6,22},{7,23},{8,24},{9,... | collective-permute-start | bytes 1474568 | tf_op jit(solution)/shard_map/ppermute | solution.py:440
  49.1 15.2 %collective-permute-start.1 = (f32[4,3,2,40,128]{4,3,2,1,0:T(8,128)}, f32[4,3,2,40,128]{4,3,2,1,0:T(8,128)S(1)}, u32[]{:S(2)}, u32[]{:S(2)}) collective-permute-start(f32[4,3,2,40,128]{4,3,2,1,0:T(8,128)} %get-tuple-element.15), channel_id=1, source_target_pairs={{0,31},{1,16},{2,17},{3,18},{4,19},{5,20},{6,21},{7,22},{8,23},{9,... | collective-permute-start | bytes 1474568 | tf_op jit(solution)/shard_map/ppermute | solution.py:439
  51.1 1.5 %collective-permute-start.2 = (f32[9,2,24,128]{3,2,1,0:T(8,128)S(1)}, f32[9,2,24,128]{3,2,1,0:T(8,128)S(1)}, u32[]{:S(2)}, u32[]{:S(2)}) collective-permute-start(f32[9,2,24,128]{3,2,1,0:T(8,128)S(1)} %get-tuple-element.19), channel_id=1, source_target_pairs={{0,16},{1,17},{2,18},{3,19},{4,20},{5,21},{6,22},{7,23},{8,24},{9,... | collective-permute-start | bytes 663560 | tf_op jit(solution)/shard_map/ppermute | solution.py:440
  51.1 9.1 %collective-permute-start.3 = (f32[9,2,24,128]{3,2,1,0:T(8,128)S(1)}, f32[9,2,24,128]{3,2,1,0:T(8,128)S(1)}, u32[]{:S(2)}, u32[]{:S(2)}) collective-permute-start(f32[9,2,24,128]{3,2,1,0:T(8,128)S(1)} %get-tuple-element.20), channel_id=1, source_target_pairs={{0,31},{1,16},{2,17},{3,18},{4,19},{5,20},{6,21},{7,22},{8,23},{9,... | collective-permute-start | bytes 663560 | tf_op jit(solution)/shard_map/ppermute | solution.py:439

commit v4 on v3

--- a/solution.py
+++ b/solution.py
@@ -34,15 +34,19 @@
     return lax.rem(lax.axis_index("lat"), 2)
 
 
-def prep_kernel(bg, wl, wt, out):
+def prep_kernel(bg, wl, wt, *outs):
     low = lanes((16, 128)) < 64
-    for f, ref in enumerate((bg, wl, wt)):
-        for level in range(12):
-            q, l = level // 3, level % 3
-            even = ref[level, pl.ds(0, 16, stride=2), :]
-            odd = ref[level, pl.ds(1, 16, stride=2), :]
-            out[2 * q, f * 3 + l] = jnp.where(low, even, pltpu.roll(odd, 64, 1))
-            out[2 * q + 1, f * 3 + l] = jnp.where(low, pltpu.roll(even, 64, 1), odd)
+    me = lax.axis_index("lat")
+    for m, out in enumerate(outs):
+        dest = me ^ m
+        q, h = dest >> 1, dest & 1
+        for f, ref in enumerate((bg, wl, wt)):
+            for l in range(LV):
+                even = ref[3 * q + l, pl.ds(0, 16, stride=2), :]
+                odd = ref[3 * q + l, pl.ds(1, 16, stride=2), :]
+                even = pltpu.roll(even, 64 * h, 1)
+                odd = pltpu.roll(odd, 64 - 64 * h, 1)
+                out[f * 3 + l] = jnp.where(low, even, odd)
 
 
 def put_edges(sa, sb, index, lo, hi, h):
@@ -63,10 +67,16 @@
     return jnp.where(first, b, a), jnp.where(first, a, b)
 
 
-def recv_kernel(x, center, sa, sb):
+def recv_kernel(*refs):
+    *xs, center, sa, sb, buf = refs
     h = half()
+    me = lax.axis_index("lat")
+    for m, x in enumerate(xs):
+        at = pl.ds(pl.multiple_of((me ^ m) * 16, 16), 16)
+        for f in range(9):
+            buf[f, at, :] = x[f]
     for f in range(9):
-        t = x[:, f].reshape(128, 128).T
+        t = buf[f].T
         for u in range(2):
             center[f, u] = t[u * 64 : u * 64 + 64]
             lo = t[u * 64 : u * 64 + EDGE]
@@ -212,7 +222,7 @@
         for ch in range(4):
             xt[ch, 128:] = x[:, 2 * ch + 1, :].T
 
-    row_ids = sublanes((ROWS, 128))
+    row_ids = sublanes((LV * COL, 128))
     lat_ids = sublanes((256, 128))
 
     def group(g, carry):
@@ -220,7 +230,8 @@
             return xt[ch, pl.ds(pl.multiple_of(g * 8, 8), 8), :]
 
         cell = part(0).astype(I32)
-        row = (part(1).astype(I32) - 1) * (LV * COL) + (cell >> 8)
+        step = part(1).astype(I32)
+        row = cell >> 8
         lat = cell & 255
         w = part(2)
         v = part(3)
@@ -231,10 +242,20 @@
         v2 = v - v0 - v1
         for r in range(8):
             cols = slice(r * 128, r * 128 + 128)
-            at[:, cols] = jnp.where(row_ids == row[r : r + 1], 1.0, 0.0).astype(BF16)
-            here = lat_ids == lat[r : r + 1]
+
+            def line(x):
+                return jnp.broadcast_to(x[r : r + 1], (16, 128)).astype(BF16)
+
+            def times(hot, x):
+                return (hot.reshape(-1, 16, 128) * line(x)[None]).reshape(-1, 128)
+
+            hot = jnp.where(row_ids == row[r : r + 1], 1.0, 0.0).astype(BF16)
+            for k in range(STEPS):
+                now = jnp.where(step == k + 1, 1.0, 0.0)
+                at[k * 192 : k * 192 + 192, cols] = times(hot, now)
+            hot = jnp.where(lat_ids == lat[r : r + 1], 1.0, 0.0).astype(BF16)
             for p, piece in enumerate((w0, w1, v0, v1, v2)):
-                bt[p * 256 : p * 256 + 256, cols] = jnp.where(here, piece[r : r + 1], 0.0).astype(BF16)
+                bt[p * 256 : p * 256 + 256, cols] = times(hot, piece)
         acc[...] += lax.dot_general(
             at[...], bt[...], (((1,), (1,)), ((), ())), preferred_element_type=F32
         )
@@ -285,7 +306,7 @@
 
 
 def core_kernel(
-    ra, rb, w_in, v_in, states_in, gains_in, drifts_in, cn_in, cs_in, out, *scratch
+    ra, rb, w_in, v_in, states_in, gains_in, drifts_in, cn_in, cs_in, out, table_ref, *scratch
 ):
     *buffers, sems = scratch
     h = half()
@@ -354,27 +375,30 @@
             for u in range(2):
                 sums[i] = sums[i] + fold(v[a][u], v[b][u])
         for i in range(3):
-            t = jnp.concatenate(v[i], axis=0).T
-            for b in range(LAT):
-                first = (i * 3 + l) * 16
-                out[b, first : first + 16] = t[b * 16 : b * 16 + 16]
+            for u in range(2):
+                out[i * 3 + l, u] = v[i][u]
     lane = lanes((1, 128))
     table = jnp.zeros((1, 128), F32)
     for i in range(5):
         whole = jnp.sum(jnp.sum(sums[i], axis=0, keepdims=True), axis=1, keepdims=True)
         table = jnp.where(lane == i, whole, table)
-    for b in range(LAT):
-        out[b, 144:] = jnp.broadcast_to(table, (8, 128))
-
-
-def share_kernel(x, out):
-    total = jnp.sum(x[:, 144:152], axis=0)
-    for j in range(LON):
-        out[j] = total
-
-
-def final_kernel(x, parts, increment, residual):
-    total = jnp.sum(parts[...], axis=0)[:1]
+    table_ref[...] = jnp.broadcast_to(table, (ALL, 128))
+
+
+def turn_kernel(x, *refs):
+    *outs, buf = refs
+    me = lax.axis_index("lat")
+    for f in range(9):
+        buf[f] = jnp.concatenate([x[f, 0], x[f, 1]], axis=0).T
+    for m, out in enumerate(outs):
+        at = pl.ds(pl.multiple_of((me ^ m) * 16, 16), 16)
+        for f in range(9):
+            out[f] = buf[f, at, :]
+
+
+def final_kernel(parts, *refs):
+    *xs, increment, residual = refs
+    total = jnp.sum(parts[...], axis=0, keepdims=True)
     lane = lanes((1, 128))
     pick = lambda i: jnp.sum(jnp.where(lane == i, total, 0.0), axis=1, keepdims=True)
     a00, a01, a11, a02, a12 = [jnp.broadcast_to(pick(i), (1, 128)) for i in range(5)]
@@ -386,18 +410,21 @@
     a = alpha + second * keep1
     b = alpha * second
     low = lanes((16, 128)) < 64
-    for level in range(12):
-        q, l = level // 3, level % 3
-        got = []
-        for h in range(2):
-            v0, v1, v2 = [
-                x[2 * q + h, (i * 3 + l) * 16 : (i * 3 + l) * 16 + 16] for i in range(3)
-            ]
-            got.append((a * v0 - b * v1, v0 - a * v1 + b * v2))
-        for i, ref in enumerate((increment, residual)):
-            x0, x1 = got[0][i], got[1][i]
-            ref[level, pl.ds(0, 16, stride=2), :] = jnp.where(low, x0, pltpu.roll(x1, 64, 1))
-            ref[level, pl.ds(1, 16, stride=2), :] = jnp.where(low, pltpu.roll(x0, 64, 1), x1)
+    me = lax.axis_index("lat")
+    first = jnp.full((16, 128), lax.rem(me, 2), I32) == 0
+    for m in range(0, LAT, 2):
+        q = (me ^ m) >> 1
+        for l in range(LV):
+            got = []
+            for x in xs[m : m + 2]:
+                v0, v1, v2 = x[l], x[3 + l], x[6 + l]
+                got.append((a * v0 - b * v1, v0 - a * v1 + b * v2))
+            for i, ref in enumerate((increment, residual)):
+                x0 = jnp.where(first, got[0][i], got[1][i])
+                x1 = jnp.where(first, got[1][i], got[0][i])
+                level = 3 * q + l
+                ref[level, pl.ds(0, 16, stride=2), :] = jnp.where(low, x0, pltpu.roll(x1, 64, 1))
+                ref[level, pl.ds(1, 16, stride=2), :] = jnp.where(low, pltpu.roll(x0, 64, 1), x1)
 
 
 VM = pl.BlockSpec(memory_space=pltpu.VMEM)
@@ -439,6 +466,14 @@
     rb = lax.ppermute(sb, ("lat", "lon"), far)
     ra = lax.ppermute(sa, ("lat", "lon"), near)
     return ra, rb
+
+
+def exchange(blocks):
+    got = [blocks[0]]
+    for m in range(1, LAT):
+        pairs = [(i * LON + j, (i ^ m) * LON + j) for i in range(LAT) for j in range(LON)]
+        got.append(lax.ppermute(blocks[m], ("lat", "lon"), pairs))
+    return got
 
 
 def on_device(
@@ -469,13 +504,14 @@
         ],
     )
     arrived = lax.all_to_all(packed, both, 0, 0, tiled=True)
-    sent = call(prep_kernel, [(LAT, 9, 16, 128)], background, wind_lon, wind_lat, ins="hhh")
-    moved = lax.all_to_all(sent, "lat", 0, 0, tiled=True)
+    blocks = call(prep_kernel, [(9, 16, 128)] * LAT, background, wind_lon, wind_lat, ins="hhh")
+    blocks = exchange(blocks)
     fields, sa, sb = call(
         recv_kernel,
         [(9, 2, COL, 128)] + [(9, 2, EDGE, 128)] * 2,
-        moved,
+        *blocks,
         space="hvv",
+        scratch=[pltpu.VMEM((9, 128, 128), F32)],
     )
     ra, rb = swap(sa, sb)
     wsum, vsum, sa, sb = call(
@@ -497,9 +533,9 @@
     big = pltpu.VMEM((STEPS,) + plane, F32)
     mid = pltpu.VMEM((STEPS,) + middle, F32)
     small = pltpu.VMEM(plane, F32)
-    sent = call(
+    vectors, table = call(
         core_kernel,
-        [(LAT, 152, 128)],
+        [(9, 2, COL, 128), (ALL, 128)],
         wa,
         wb,
         wsum,
@@ -508,9 +544,12 @@
         ins="vv" + "a" * 7,
         scratch=[mid, mid, big, big, big, small, small, pltpu.SemaphoreType.DMA((LV, 7))],
     )
-    moved = lax.all_to_all(sent, "lat", 0, 0, tiled=True)
-    parts = lax.all_to_all(call(share_kernel, [(LON, 8, 128)], moved), "lon", 0, 0, tiled=True)
-    return call(final_kernel, [(12, 32, 128)] * 2, moved, parts, space="h")
+    parts = lax.all_to_all(table, both, 0, 0, tiled=True)
+    blocks = call(
+        turn_kernel, [(9, 16, 128)] * LAT, vectors, scratch=[pltpu.VMEM((9, 128, 128), F32)]
+    )
+    blocks = exchange(blocks)
+    return call(final_kernel, [(12, 32, 128)] * 2, parts, *blocks, space="h")
 
 
 def solution(mesh):

time: 99.9 us -> 106 us (1.061)
  blocking collectives: 26.8 us -> 40.2 us
  waiting for transfers between devices: 19.5 us -> 6.18 us
  starting transfers between devices: 20.3 us -> 29.3 us
  Pallas kernels: 30.6 us -> 28.6 us
    ppermute x0 -> x14, starting transfers between devices: none -> 22.1 us  [exchange(): got.append(lax.ppermute(blocks[m], ('lat', 'lon'), pairs))]
    all_to_all x2 -> x0, starting transfers between devices: 15.5 us -> none  [the longest x1 11.5 us: on_device(): arrived = lax.all_to_all(packed, both, 0, 0, tiled=True)]
    all_to_all x2, blocking collectives: 26.8 us -> 40.2 us  [the longest x1 25.3 us: on_device(): arrived = lax.all_to_all(packed, both, 0, 0, tiled=True)]
    all_to_all x2 -> x0, waiting for transfers between devices: 11.9 us -> none  [the longest x1 11.9 us: on_device(): arrived = lax.all_to_all(packed, both, 0, 0, tiled=True)]
    ppermute x2, waiting for transfers between devices: 7.63 us -> 1.78 us  [swap(): rb = lax.ppermute(sb, ('lat', 'lon'), far)]
    ppermute x0 -> x14, waiting for transfers between devices: none -> 4.4 us  [exchange(): got.append(lax.ppermute(blocks[m], ('lat', 'lon'), pairs))]
    ppermute x2, starting transfers between devices: 3.09 us -> 6.95 us  [swap(): ra = lax.ppermute(sa, ('lat', 'lon'), near)]
    pallas_call x8, Pallas kernels: 30.6 us -> 28.6 us  [call(): return make(kernel, shapes, ins, scratch)(*args)]
  transfers between devices with their start and end apart: 6 -> 18, of which waited for: 2 -> 3; matrix products, arithmetic and copies ran while one was open for 0% -> 0% of each run, Pallas kernels for 19% -> 7%
where the time goes in v4:
time: 106 us
  blocking collectives  40.2 us (38%)
  starting transfers between devices  29.3 us (28%)
  Pallas kernels  28.6 us (27%)
  waiting for transfers between devices  6.18 us (6%)
  between operations  1.36 us (1%)
    pallas_call x8, Pallas kernels, call(): return make(kernel, shapes, ins, scratch)(*args)  28.6 us
    all_to_all x1, blocking collectives, on_device(): arrived = lax.all_to_all(packed, both, 0, 0, tiled=True)  25.3 us
    ppermute x14, starting transfers between devices, exchange(): got.append(lax.ppermute(blocks[m], ('lat', 'lon'), pairs))  22.1 us
    all_to_all x1, blocking collectives, on_device(): parts = lax.all_to_all(table, both, 0, 0, tiled=True)  14.9 us
    ppermute x2, starting transfers between devices, swap(): ra = lax.ppermute(sa, ('lat', 'lon'), near)  6.95 us
    ppermute x14, waiting for transfers between devices, exchange(): got.append(lax.ppermute(blocks[m], ('lat', 'lon'), pairs))  4.4 us
  transfers between devices with their start and end apart: 18, of which 3 were waited for; matrix products, arithmetic and copies ran while one was open for 0% of the time, Pallas kernels for 7%

profile of v4, /device:TPU:1, one launch (start us, length us, event | category | flops | bytes accessed | tf_op | source)
XLA Modules:
  0.0 105.6 jit_solution(14318646960499737362)
XLA Ops:
  1.3 3.1 %shard_map.104 = f32[128,8,128]{2,1,0:T(8,128)S(1)} custom-call(s32[1]{0:T(128)S(6)} %copy.12.count, s32[16,128]{1,0:T(8,128)} %bitcast.11, s32[16,128]{1,0:T(8,128)} %bitcast.12, s32[16,128]{1,0:T(8,128)} %bitcast.13, f32[16,128]{1,0:T(8,128)} %bitcast.14, f32[16,128]{1,0:T(8,128)} %bitcast.15), custom_call_target="tpu_custom_call" | custom-call | tf_op jit(solution)/shard_map/pallas_call | solution.py:445
  4.4 25.3 %all_to_all.16.x = f32[128,8,128]{2,1,0:T(8,128)S(1)} all-to-all(f32[128,8,128]{2,1,0:T(8,128)S(1)} %shard_map.104), channel_id=1, replica_groups=mesh['lat'=8,'lon'=16] {'lat','lon'}, dimensions={0} | all-to-all | bytes 1048576 | tf_op jit(solution)/shard_map/all_to_all | solution.py:506
  29.8 10.5 %shard_map.105 = (f32[4,3,2,64,128]{4,3,2,1,0:T(8,128)}, f32[4,3,2,64,128]{4,3,2,1,0:T(8,128)}, f32[4,3,2,40,128]{4,3,2,1,0:T(8,128)}, f32[4,3,2,40,128]{4,3,2,1,0:T(8,128)S(1)}) custom-call(f32[128,8,128]{2,1,0:T(8,128)S(1)} %all_to_all.16.x), custom_call_target="tpu_custom_call" | custom-call | tf_op jit(solution)/shard_map/pallas_call | solution.py:445
  40.3 3.4 %collective-permute-start = (f32[4,3,2,40,128]{4,3,2,1,0:T(8,128)}, f32[4,3,2,40,128]{4,3,2,1,0:T(8,128)S(1)}, u32[]{:S(2)}, u32[]{:S(2)}) collective-permute-start(f32[4,3,2,40,128]{4,3,2,1,0:T(8,128)} %get-tuple-element.32), channel_id=1, source_target_pairs={{0,16},{1,17},{2,18},{3,19},{4,20},{5,21},{6,22},{7,23},{8,24},{9,... | collective-permute-start | bytes 1474568 | tf_op jit(solution)/shard_map/ppermute | solution.py:467
  43.9 1.5 %shard_map.106 = (f32[9,16,128]{2,1,0:T(8,128)S(1)}, f32[9,16,128]{2,1,0:T(8,128)S(1)}, f32[9,16,128]{2,1,0:T(8,128)S(1)}, f32[9,16,128]{2,1,0:T(8,128)S(1)}, f3...) custom-call(f32[12,32,128]{2,1,0:T(8,128)} %bg.1, ...), custom_call_target="tpu_custom_call" | custom-call | tf_op jit(solution)/shard_map/pallas_call | solution.py:445
  45.5 1.2 %collective-permute-start.3 = (f32[9,16,128]{2,1,0:T(8,128)S(1)}, f32[9,16,128]{2,1,0:T(8,128)S(1)}, u32[]{:S(2)}, u32[]{:S(2)}) collective-permute-start(f32[9,16,128]{2,1,0:T(8,128)S(1)} %get-tuple-element.38), channel_id=1, source_target_pairs={{0,32},{1,33},{2,34},{3,35},{4,36},{5,37},{6,38},{7,39},{8,40},{9,... | collective-permute-start | bytes 221192 | tf_op jit(solution)/shard_map/ppermute | solution.py:475
  47.6 1.3 %collective-permute-start.5 = (f32[9,16,128]{2,1,0:T(8,128)S(1)}, f32[9,16,128]{2,1,0:T(8,128)S(1)}, u32[]{:S(2)}, u32[]{:S(2)}) collective-permute-start(f32[9,16,128]{2,1,0:T(8,128)S(1)} %get-tuple-element.40), channel_id=1, source_target_pairs={{0,64},{1,65},{2,66},{3,67},{4,68},{5,69},{6,70},{7,71},{8,72},{9,... | collective-permute-start | bytes 221192 | tf_op jit(solution)/shard_map/ppermute | solution.py:475
  48.9 3.0 %collective-permute-start.6 = (f32[9,16,128]{2,1,0:T(8,128)S(1)}, f32[9,16,128]{2,1,0:T(8,128)S(1)}, u32[]{:S(2)}, u32[]{:S(2)}) collective-permute-start(f32[9,16,128]{2,1,0:T(8,128)S(1)} %get-tuple-element.41), channel_id=1, source_target_pairs={{0,80},{1,81},{2,82},{3,83},{4,84},{5,85},{6,86},{7,87},{8,88},{9,... | collective-permute-start | bytes 221192 | tf_op jit(solution)/shard_map/ppermute | solution.py:475
  51.9 2.2 %collective-permute-start.7 = (f32[9,16,128]{2,1,0:T(8,128)S(1)}, f32[9,16,128]{2,1,0:T(8,128)S(1)}, u32[]{:S(2)}, u32[]{:S(2)}) collective-permute-start(f32[9,16,128]{2,1,0:T(8,128)S(1)} %get-tuple-element.42), channel_id=1, source_target_pairs={{0,96},{1,97},{2,98},{3,99},{4,100},{5,101},{6,102},{7,103},{8,104... | collective-permute-start | bytes 221192 | tf_op jit(solution)/shard_map/ppermute | solution.py:475
  54.1 1.6 %collective-permute-start.8 = (f32[9,16,128]{2,1,0:T(8,128)S(1)}, f32[9,16,128]{2,1,0:T(8,128)S(1)}, u32[]{:S(2)}, u32[]{:S(2)}) collective-permute-start(f32[9,16,128]{2,1,0:T(8,128)S(1)} %get-tuple-element.43), channel_id=1, source_target_pairs={{0,112},{1,113},{2,114},{3,115},{4,116},{5,117},{6,118},{7,119},{8... | collective-permute-start | bytes 221192 | tf_op jit(solution)/shard_map/ppermute | solution.py:475
  55.7 1.8 %collective-permute-done.7.refs_6_ = f32[9,16,128]{2,1,0:T(8,128)S(1)} collective-permute-done((f32[9,16,128]{2,1,0:T(8,128)S(1)}, f32[9,16,128]{2,1,0:T(8,128)S(1)}, u32[]{:S(2)}, u32[]{:S(2)}) %collective-permute-start.7) | collective-permute-done | bytes 73760 | tf_op jit(solution)/shard_map/ppermute | solution.py:475
  57.5 2.6 %collective-permute-done.8.refs_7_ = f32[9,16,128]{2,1,0:T(8,128)S(1)} collective-permute-done((f32[9,16,128]{2,1,0:T(8,128)S(1)}, f32[9,16,128]{2,1,0:T(8,128)S(1)}, u32[]{:S(2)}, u32[]{:S(2)}) %collective-permute-start.8) | collective-permute-done | bytes 73760 | tf_op jit(solution)/shard_map/ppermute | solution.py:475
  60.1 1.8 %shard_map.107 = (f32[9,2,64,128]{3,2,1,0:T(8,128)}, f32[9,2,24,128]{3,2,1,0:T(8,128)S(1)}, f32[9,2,24,128]{3,2,1,0:T(8,128)S(1)}) custom-call(f32[9,16,128]{2,1,0:T(8,128)S(1)} %get-tuple-element.36.refs_0_, f32[9,16,128]{2,1,0:T(8,128)S(1)} %collective-permute-done.2.refs_1_, f32[9,16,128]{2,1,0:T(8,128)S(1)} %collective-permute-done.3.refs_2_, ...), custom_call_target="tpu_custom_call" | custom-call | tf_op jit(solution)/shard_map/pallas_call | solution.py:445
  62.0 3.6 %collective-permute-start.9 = (f32[9,2,24,128]{3,2,1,0:T(8,128)S(1)}, f32[9,2,24,128]{3,2,1,0:T(8,128)S(1)}, u32[]{:S(2)}, u32[]{:S(2)}) collective-permute-start(f32[9,2,24,128]{3,2,1,0:T(8,128)S(1)} %get-tuple-element.45), channel_id=1, source_target_pairs={{0,16},{1,17},{2,18},{3,19},{4,20},{5,21},{6,22},{7,23},{8,24},{9,... | collective-permute-start | bytes 663560 | tf_op jit(solution)/shard_map/ppermute | solution.py:467
  65.5 1.8 %collective-permute-done.10.rb = f32[9,2,24,128]{3,2,1,0:T(8,128)S(1)} collective-permute-done((f32[9,2,24,128]{3,2,1,0:T(8,128)S(1)}, f32[9,2,24,128]{3,2,1,0:T(8,128)S(1)}, u32[]{:S(2)}, u32[]{:S(2)}) %collective-permute-start.10) | collective-permute-done | bytes 221216 | tf_op jit(solution)/shard_map/ppermute | solution.py:466
  67.3 4.0 %shard_map.108 = (f32[4,3,2,112,128]{4,3,2,1,0:T(8,128)}, f32[4,3,2,112,128]{4,3,2,1,0:T(8,128)}, f32[4,3,2,112,128]{4,3,2,1,0:T(8,128)}, f32[3,2,112,128]{3,2,1,0:T(8,128)}, f32[3,2,112,128]{3,2,1,0:T(8,128)}) custom-call(f32[9,2,64,128]{3,2,1,0:T(8,128)} %get-tuple-element.44.center, f32[9,2,24,128]{3,2,1,0:T(8,128)S(1)} %collective-permute-done.9.ra, ...), custom_call_target="tpu_custom_call" | custom-call | tf_op jit(solution)/shard_map/pallas_call | solution.py:445
  71.3 6.4 %shard_map.109 = (f32[9,2,64,128]{3,2,1,0:T(8,128)S(1)}, f32[128,128]{1,0:T(8,128)S(1)}) custom-call(f32[4,3,2,40,128]{4,3,2,1,0:T(8,128)S(1)} %collective-permute-done.ra, f32[4,3,2,40,128]{4,3,2,1,0:T(8,128)S(1)} %collective-permute-done.1.rb, f32[4,3,2,64,128]{4,3,2,1,0:T(8,128)} %get-tuple-element.34.w_in, f32[4,3,2,64,128]{4,3,2,1,0:T(8,128)} %get-tuple-element.35.v_in, ...), custom_call_target="tpu_custom_call" | custom-call | tf_op jit(solution)/shard_map/pallas_call | solution.py:445
  78.0 3.8 %collective-permute-start.11 = (f32[9,16,128]{2,1,0:T(8,128)S(1)}, f32[9,16,128]{2,1,0:T(8,128)S(1)}, u32[]{:S(2)}, u32[]{:S(2)}) collective-permute-start(f32[9,16,128]{2,1,0:T(8,128)S(1)} %get-tuple-element.55), channel_id=1, source_target_pairs={{0,16},{1,17},{2,18},{3,19},{4,20},{5,21},{6,22},{7,23},{8,24},{9,... | collective-permute-start | bytes 221192 | tf_op jit(solution)/shard_map/ppermute | solution.py:475
  81.8 1.7 %collective-permute-start.13 = (f32[9,16,128]{2,1,0:T(8,128)S(1)}, f32[9,16,128]{2,1,0:T(8,128)S(1)}, u32[]{:S(2)}, u32[]{:S(2)}) collective-permute-start(f32[9,16,128]{2,1,0:T(8,128)S(1)} %get-tuple-element.57), channel_id=1, source_target_pairs={{0,48},{1,49},{2,50},{3,51},{4,52},{5,53},{6,54},{7,55},{8,56},{9,... | collective-permute-start | bytes 221192 | tf_op jit(solution)/shard_map/ppermute | solution.py:475
  84.1 2.7 %collective-permute-start.15 = (f32[9,16,128]{2,1,0:T(8,128)S(1)}, f32[9,16,128]{2,1,0:T(8,128)S(1)}, u32[]{:S(2)}, u32[]{:S(2)}) collective-permute-start(f32[9,16,128]{2,1,0:T(8,128)S(1)} %get-tuple-element.59), channel_id=1, source_target_pairs={{0,80},{1,81},{2,82},{3,83},{4,84},{5,85},{6,86},{7,87},{8,88},{9,... | collective-permute-start | bytes 221192 | tf_op jit(solution)/shard_map/ppermute | solution.py:475
  86.8 1.1 %collective-permute-start.16 = (f32[9,16,128]{2,1,0:T(8,128)S(1)}, f32[9,16,128]{2,1,0:T(8,128)S(1)}, u32[]{:S(2)}, u32[]{:S(2)}) collective-permute-start(f32[9,16,128]{2,1,0:T(8,128)S(1)} %get-tuple-element.60), channel_id=1, source_target_pairs={{0,96},{1,97},{2,98},{3,99},{4,100},{5,101},{6,102},{7,103},{8,104... | collective-permute-start | bytes 221192 | tf_op jit(solution)/shard_map/ppermute | solution.py:475
  87.9 1.8 %collective-permute-start.17 = (f32[9,16,128]{2,1,0:T(8,128)S(1)}, f32[9,16,128]{2,1,0:T(8,128)S(1)}, u32[]{:S(2)}, u32[]{:S(2)}) collective-permute-start(f32[9,16,128]{2,1,0:T(8,128)S(1)} %get-tuple-element.61), channel_id=1, source_target_pairs={{0,112},{1,113},{2,114},{3,115},{4,116},{5,117},{6,118},{7,119},{8... | collective-permute-start | bytes 221192 | tf_op jit(solution)/shard_map/ppermute | solution.py:475
  89.7 14.9 %all_to_all.17 = f32[128,1,128]{2,1,0:T(1,128)S(1)} all-to-all(f32[128,1,128]{2,1,0:T(1,128)S(1)} %bitcast.10), channel_id=1, replica_groups=mesh['lat'=8,'lon'=16] {'lat','lon'}, dimensions={0} | all-to-all | bytes 131072 | tf_op jit(solution)/shard_map/all_to_all | solution.py:547
  104.6 1.0 shard_map.111
  (22 shorter events, 2.3 us)
Async XLA Ops:
  40.3 31.1 %collective-permute-start = (f32[4,3,2,40,128]{4,3,2,1,0:T(8,128)}, f32[4,3,2,40,128]{4,3,2,1,0:T(8,128)S(1)}, u32[]{:S(2)}, u32[]{:S(2)}) collective-permute-start(f32[4,3,2,40,128]{4,3,2,1,0:T(8,128)} %get-tuple-element.32), channel_id=1, source_target_pairs={{0,16},{1,17},{2,18},{3,19},{4,20},{5,21},{6,22},{7,23},{8,24},{9,... | collective-permute-start | bytes 1474568 | tf_op jit(solution)/shard_map/ppermute | solution.py:467
  43.6 27.7 %collective-permute-start.1 = (f32[4,3,2,40,128]{4,3,2,1,0:T(8,128)S(1)}, f32[4,3,2,40,128]{4,3,2,1,0:T(8,128)S(1)}, u32[]{:S(2)}, u32[]{:S(2)}) collective-permute-start(f32[4,3,2,40,128]{4,3,2,1,0:T(8,128)S(1)} %get-tuple-element.33), channel_id=1, source_target_pairs={{0,31},{1,16},{2,17},{3,18},{4,19},{5,20},{6,21},{7,22},{8,23},{9,... | collective-permute-start | bytes 1474568 | tf_op jit(solution)/shard_map/ppermute | solution.py:466
  45.4 2.2 %collective-permute-start.2 = (f32[9,16,128]{2,1,0:T(8,128)S(1)}, f32[9,16,128]{2,1,0:T(8,128)S(1)}, u32[]{:S(2)}, u32[]{:S(2)}) collective-permute-start(f32[9,16,128]{2,1,0:T(8,128)S(1)} %get-tuple-element.37), channel_id=1, source_target_pairs={{0,16},{1,17},{2,18},{3,19},{4,20},{5,21},{6,22},{7,23},{8,24},{9,... | collective-permute-start | bytes 221192 | tf_op jit(solution)/shard_map/ppermute | solution.py:475
  45.5 3.5 %collective-permute-start.3 = (f32[9,16,128]{2,1,0:T(8,128)S(1)}, f32[9,16,128]{2,1,0:T(8,128)S(1)}, u32[]{:S(2)}, u32[]{:S(2)}) collective-permute-start(f32[9,16,128]{2,1,0:T(8,128)S(1)} %get-tuple-element.38), channel_id=1, source_target_pairs={{0,32},{1,33},{2,34},{3,35},{4,36},{5,37},{6,38},{7,39},{8,40},{9,... | collective-permute-start | bytes 221192 | tf_op jit(solution)/shard_map/ppermute | solution.py:475
  46.6 5.3 %collective-permute-start.4 = (f32[9,16,128]{2,1,0:T(8,128)S(1)}, f32[9,16,128]{2,1,0:T(8,128)S(1)}, u32[]{:S(2)}, u32[]{:S(2)}) collective-permute-start(f32[9,16,128]{2,1,0:T(8,128)S(1)} %get-tuple-element.39), channel_id=1, source_target_pairs={{0,48},{1,49},{2,50},{3,51},{4,52},{5,53},{6,54},{7,55},{8,56},{9,... | collective-permute-start | bytes 221192 | tf_op jit(solution)/shard_map/ppermute | solution.py:475
  47.6 6.5 %collective-permute-start.5 = (f32[9,16,128]{2,1,0:T(8,128)S(1)}, f32[9,16,128]{2,1,0:T(8,128)S(1)}, u32[]{:S(2)}, u32[]{:S(2)}) collective-permute-start(f32[9,16,128]{2,1,0:T(8,128)S(1)} %get-tuple-element.40), channel_id=1, source_target_pairs={{0,64},{1,65},{2,66},{3,67},{4,68},{5,69},{6,70},{7,71},{8,72},{9,... | collective-permute-start | bytes 221192 | tf_op jit(solution)/shard_map/ppermute | solution.py:475
  48.9 6.8 %collective-permute-start.6 = (f32[9,16,128]{2,1,0:T(8,128)S(1)}, f32[9,16,128]{2,1,0:T(8,128)S(1)}, u32[]{:S(2)}, u32[]{:S(2)}) collective-permute-start(f32[9,16,128]{2,1,0:T(8,128)S(1)} %get-tuple-element.41), channel_id=1, source_target_pairs={{0,80},{1,81},{2,82},{3,83},{4,84},{5,85},{6,86},{7,87},{8,88},{9,... | collective-permute-start | bytes 221192 | tf_op jit(solution)/shard_map/ppermute | solution.py:475
  51.9 5.6 %collective-permute-start.7 = (f32[9,16,128]{2,1,0:T(8,128)S(1)}, f32[9,16,128]{2,1,0:T(8,128)S(1)}, u32[]{:S(2)}, u32[]{:S(2)}) collective-permute-start(f32[9,16,128]{2,1,0:T(8,128)S(1)} %get-tuple-element.42), channel_id=1, source_target_pairs={{0,96},{1,97},{2,98},{3,99},{4,100},{5,101},{6,102},{7,103},{8,104... | collective-permute-start | bytes 221192 | tf_op jit(solution)/shard_map/ppermute | solution.py:475
  54.1 6.0 %collective-permute-start.8 = (f32[9,16,128]{2,1,0:T(8,128)S(1)}, f32[9,16,128]{2,1,0:T(8,128)S(1)}, u32[]{:S(2)}, u32[]{:S(2)}) collective-permute-start(f32[9,16,128]{2,1,0:T(8,128)S(1)} %get-tuple-element.43), channel_id=1, source_target_pairs={{0,112},{1,113},{2,114},{3,115},{4,116},{5,117},{6,118},{7,119},{8... | collective-permute-start | bytes 221192 | tf_op jit(solution)/shard_map/ppermute | solution.py:475
  61.9 5.4 %collective-permute-start.10 = (f32[9,2,24,128]{3,2,1,0:T(8,128)S(1)}, f32[9,2,24,128]{3,2,1,0:T(8,128)S(1)}, u32[]{:S(2)}, u32[]{:S(2)}) collective-permute-start(f32[9,2,24,128]{3,2,1,0:T(8,128)S(1)} %get-tuple-element.46), channel_id=1, source_target_pairs={{0,31},{1,16},{2,17},{3,18},{4,19},{5,20},{6,21},{7,22},{8,23},{9,... | collective-permute-start | bytes 663560 | tf_op jit(solution)/shard_map/ppermute | solution.py:466
  62.0 5.3 %collective-permute-start.9 = (f32[9,2,24,128]{3,2,1,0:T(8,128)S(1)}, f32[9,2,24,128]{3,2,1,0:T(8,128)S(1)}, u32[]{:S(2)}, u32[]{:S(2)}) collective-permute-start(f32[9,2,24,128]{3,2,1,0:T(8,128)S(1)} %get-tuple-element.45), channel_id=1, source_target_pairs={{0,16},{1,17},{2,18},{3,19},{4,20},{5,21},{6,22},{7,23},{8,24},{9,... | collective-permute-start | bytes 663560 | tf_op jit(solution)/shard_map/ppermute | solution.py:467
  78.0 8.8 %collective-permute-start.11 = (f32[9,16,128]{2,1,0:T(8,128)S(1)}, f32[9,16,128]{2,1,0:T(8,128)S(1)}, u32[]{:S(2)}, u32[]{:S(2)}) collective-permute-start(f32[9,16,128]{2,1,0:T(8,128)S(1)} %get-tuple-element.55), channel_id=1, source_target_pairs={{0,16},{1,17},{2,18},{3,19},{4,20},{5,21},{6,22},{7,23},{8,24},{9,... | collective-permute-start | bytes 221192 | tf_op jit(solution)/shard_map/ppermute | solution.py:475
  81.8 6.1 %collective-permute-start.12 = (f32[9,16,128]{2,1,0:T(8,128)S(1)}, f32[9,16,128]{2,1,0:T(8,128)S(1)}, u32[]{:S(2)}, u32[]{:S(2)}) collective-permute-start(f32[9,16,128]{2,1,0:T(8,128)S(1)} %get-tuple-element.56), channel_id=1, source_target_pairs={{0,32},{1,33},{2,34},{3,35},{4,36},{5,37},{6,38},{7,39},{8,40},{9,... | collective-permute-start | bytes 221192 | tf_op jit(solution)/shard_map/ppermute | solution.py:475
  81.8 22.8 %collective-permute-start.13 = (f32[9,16,128]{2,1,0:T(8,128)S(1)}, f32[9,16,128]{2,1,0:T(8,128)S(1)}, u32[]{:S(2)}, u32[]{:S(2)}) collective-permute-start(f32[9,16,128]{2,1,0:T(8,128)S(1)} %get-tuple-element.57), channel_id=1, source_target_pairs={{0,48},{1,49},{2,50},{3,51},{4,52},{5,53},{6,54},{7,55},{8,56},{9,... | collective-permute-start | bytes 221192 | tf_op jit(solution)/shard_map/ppermute | solution.py:475
  83.5 21.1 %collective-permute-start.14 = (f32[9,16,128]{2,1,0:T(8,128)S(1)}, f32[9,16,128]{2,1,0:T(8,128)S(1)}, u32[]{:S(2)}, u32[]{:S(2)}) collective-permute-start(f32[9,16,128]{2,1,0:T(8,128)S(1)} %get-tuple-element.58), channel_id=1, source_target_pairs={{0,64},{1,65},{2,66},{3,67},{4,68},{5,69},{6,70},{7,71},{8,72},{9,... | collective-permute-start | bytes 221192 | tf_op jit(solution)/shard_map/ppermute | solution.py:475
  84.1 20.5 %collective-permute-start.15 = (f32[9,16,128]{2,1,0:T(8,128)S(1)}, f32[9,16,128]{2,1,0:T(8,128)S(1)}, u32[]{:S(2)}, u32[]{:S(2)}) collective-permute-start(f32[9,16,128]{2,1,0:T(8,128)S(1)} %get-tuple-element.59), channel_id=1, source_target_pairs={{0,80},{1,81},{2,82},{3,83},{4,84},{5,85},{6,86},{7,87},{8,88},{9,... | collective-permute-start | bytes 221192 | tf_op jit(solution)/shard_map/ppermute | solution.py:475
  86.8 17.8 %collective-permute-start.16 = (f32[9,16,128]{2,1,0:T(8,128)S(1)}, f32[9,16,128]{2,1,0:T(8,128)S(1)}, u32[]{:S(2)}, u32[]{:S(2)}) collective-permute-start(f32[9,16,128]{2,1,0:T(8,128)S(1)} %get-tuple-element.60), channel_id=1, source_target_pairs={{0,96},{1,97},{2,98},{3,99},{4,100},{5,101},{6,102},{7,103},{8,104... | collective-permute-start | bytes 221192 | tf_op jit(solution)/shard_map/ppermute | solution.py:475
  87.9 16.8 %collective-permute-start.17 = (f32[9,16,128]{2,1,0:T(8,128)S(1)}, f32[9,16,128]{2,1,0:T(8,128)S(1)}, u32[]{:S(2)}, u32[]{:S(2)}) collective-permute-start(f32[9,16,128]{2,1,0:T(8,128)S(1)} %get-tuple-element.61), channel_id=1, source_target_pairs={{0,112},{1,113},{2,114},{3,115},{4,116},{5,117},{6,118},{7,119},{8... | collective-permute-start | bytes 221192 | tf_op jit(solution)/shard_map/ppermute | solution.py:475

commit v5 on v3

--- a/solution.py
+++ b/solution.py
@@ -16,7 +16,8 @@
 EXT = COL + 2 * EDGE
 SLAB = 40
 ROOM = 256
-ROWS = STEPS * LV * COL
+SEG = 64
+GROUP = 4
 F32 = jnp.float32
 BF16 = jnp.bfloat16
 I32 = jnp.int32
@@ -34,15 +35,34 @@
     return lax.rem(lax.axis_index("lat"), 2)
 
 
-def prep_kernel(bg, wl, wt, out):
+def prep_kernel(bg, wl, wt, keep, give):
     low = lanes((16, 128)) < 64
+    h = half()
     for f, ref in enumerate((bg, wl, wt)):
         for level in range(12):
             q, l = level // 3, level % 3
             even = ref[level, pl.ds(0, 16, stride=2), :]
             odd = ref[level, pl.ds(1, 16, stride=2), :]
-            out[2 * q, f * 3 + l] = jnp.where(low, even, pltpu.roll(odd, 64, 1))
-            out[2 * q + 1, f * 3 + l] = jnp.where(low, pltpu.roll(even, 64, 1), odd)
+            first = jnp.where(low, even, pltpu.roll(odd, 64, 1))
+            second = jnp.where(low, pltpu.roll(even, 64, 1), odd)
+
+            @pl.when(h == 0)
+            def _():
+                keep[q, f * 3 + l] = first
+                give[q, f * 3 + l] = second
+
+            @pl.when(h != 0)
+            def _():
+                keep[q, f * 3 + l] = second
+                give[q, f * 3 + l] = first
+
+
+def merge_in_kernel(keep, got, *outs):
+    h = half()
+    x = lax.axis_index("lat") >> 1
+    for t, out in enumerate(outs):
+        out[h] = keep[x ^ t]
+        out[1 - h] = got[x ^ t]
 
 
 def put_edges(sa, sb, index, lo, hi, h):
@@ -63,10 +83,17 @@
     return jnp.where(first, b, a), jnp.where(first, a, b)
 
 
-def recv_kernel(x, center, sa, sb):
-    h = half()
+def recv_kernel(*refs):
+    *xs, center, sa, sb, buf = refs
+    h = half()
+    mine = lax.axis_index("lat") >> 1
+    for t, x in enumerate(xs):
+        for c in range(2):
+            at = pl.ds(pl.multiple_of((mine ^ t) * 32 + c * 16, 16), 16)
+            for f in range(9):
+                buf[f, at, :] = x[c, f]
     for f in range(9):
-        t = x[:, f].reshape(128, 128).T
+        t = buf[f].T
         for u in range(2):
             center[f, u] = t[u * 64 : u * 64 + 64]
             lo = t[u * 64 : u * 64 + EDGE]
@@ -199,7 +226,7 @@
             out[:, 2 * ch + hf, :] = sum(acc[p * 128 : p * 128 + 128, at] for p in pieces)
 
 
-def scatter_kernel(x, wsum, vsum, sa, sb, xt, at, bt, acc):
+def scatter_kernel(x, wsum, vsum, sa, sb, xt, sorted_, at, bt, acc):
     h = half()
     most = jnp.max(x[:, 2:4, :], axis=0)
     total = jnp.sum(jnp.where(most > 0.5, 1.0, 0.0)).astype(I32)
@@ -212,41 +239,74 @@
         for ch in range(4):
             xt[ch, 128:] = x[:, 2 * ch + 1, :].T
 
-    row_ids = sublanes((ROWS, 128))
+    block = (SEG, 128)
+    place = sublanes(block)
+    square = (SEG, SEG)
+    before = (lanes(square) < sublanes(square)).astype(F32).astype(BF16)
+    row_ids = sublanes((LV * COL, 128))
     lat_ids = sublanes((256, 128))
 
-    def group(g, carry):
-        def part(ch):
-            return xt[ch, pl.ds(pl.multiple_of(g * 8, 8), 8), :]
-
-        cell = part(0).astype(I32)
-        row = (part(1).astype(I32) - 1) * (LV * COL) + (cell >> 8)
-        lat = cell & 255
-        w = part(2)
-        v = part(3)
-        w0 = w.astype(BF16).astype(F32)
-        w1 = w - w0
-        v0 = v.astype(BF16).astype(F32)
-        v1 = (v - v0).astype(BF16).astype(F32)
-        v2 = v - v0 - v1
-        for r in range(8):
-            cols = slice(r * 128, r * 128 + 128)
-            at[:, cols] = jnp.where(row_ids == row[r : r + 1], 1.0, 0.0).astype(BF16)
-            here = lat_ids == lat[r : r + 1]
-            for p, piece in enumerate((w0, w1, v0, v1, v2)):
-                bt[p * 256 : p * 256 + 256, cols] = jnp.where(here, piece[r : r + 1], 0.0).astype(BF16)
-        acc[...] += lax.dot_general(
-            at[...], bt[...], (((1,), (1,)), ((), ())), preferred_element_type=F32
-        )
+    def line(ref):
+        return jnp.broadcast_to(ref, (16, 128)).astype(BF16)
+
+    def times(hot, scale):
+        return (hot.reshape(-1, 16, 128) * scale[None]).reshape(-1, 128)
+
+    def segment(i, carry):
+        first = pl.multiple_of(i * SEG, SEG)
+        part = lambda ch: xt[ch, pl.ds(first, SEG), :]
+        step = part(1)
+        for k in range(STEPS):
+            valid = jnp.where(step == k + 1.0, 1.0, 0.0)
+            count = jnp.sum(valid, axis=0, keepdims=True)
+            ahead = jnp.dot(before, valid.astype(BF16), preferred_element_type=F32).astype(I32)
+            shift = jnp.where(step == k + 1.0, place - ahead, 0)
+            moved = [part(0), part(2), part(3)]
+            for bit in (1, 2, 4, 8, 16, 32):
+                go = shift & bit
+                come = pltpu.roll(go, SEG - bit, 0) != 0
+                moved = [jnp.where(come, pltpu.roll(y, SEG - bit, 0), y) for y in moved]
+                shift = jnp.where(
+                    come, pltpu.roll(shift, SEG - bit, 0), jnp.where(go != 0, 0, shift)
+                )
+            there = place < count.astype(I32)
+            cell = moved[0].astype(I32)
+            w = jnp.where(there, moved[1], 0.0)
+            v = jnp.where(there, moved[2], 0.0)
+            w0 = w.astype(BF16).astype(F32)
+            v0 = v.astype(BF16).astype(F32)
+            v1 = (v - v0).astype(BF16).astype(F32)
+            pieces = ((cell >> 8).astype(F32), (cell & 255).astype(F32), w0, w - w0, v0, v1, v - v0 - v1)
+            for n, piece in enumerate(pieces):
+                sorted_[n] = piece
+            longest = jnp.max(count).astype(I32)
+
+            def group(g, carry):
+                for r in range(GROUP):
+                    cols = slice(r * 128, r * 128 + 128)
+                    get = lambda n: sorted_[n, pl.ds(g * GROUP + r, 1), :]
+                    hot = jnp.where(row_ids == get(0).astype(I32), 1.0, 0.0).astype(BF16)
+                    for p in range(5):
+                        at[p * 192 : p * 192 + 192, cols] = times(hot, line(get(2 + p)))
+                    bt[:, cols] = jnp.where(lat_ids == get(1).astype(I32), 1.0, 0.0).astype(BF16)
+                acc[k * 960 : k * 960 + 960, :] += lax.dot_general(
+                    at[...], bt[...], (((1,), (1,)), ((), ())), preferred_element_type=F32
+                )
+                return carry
+
+            lax.fori_loop(0, (longest + GROUP - 1) // GROUP, group, 0)
         return carry
 
-    lax.fori_loop(0, (total + 7) // 8, group, 0)
+    lax.fori_loop(0, (total + SEG - 1) // SEG, segment, 0)
     low = sublanes((8, 128)) < 4
     for k in range(STEPS):
         for l in range(LV):
             for u in range(2):
-                rows = slice((k * LV + l) * COL, (k * LV + l + 1) * COL)
-                take = lambda p: acc[rows, p * 256 + u * 128 : p * 256 + u * 128 + 128]
+                top = k * 960 + l * COL
+
+                def take(p):
+                    return acc[top + p * 192 : top + p * 192 + COL, u * 128 : u * 128 + 128]
+
                 w = take(0) + take(1)
                 v = take(2) + take(3) + take(4)
                 wsum[k, l, u] = w
@@ -285,7 +345,7 @@
 
 
 def core_kernel(
-    ra, rb, w_in, v_in, states_in, gains_in, drifts_in, cn_in, cs_in, out, *scratch
+    ra, rb, w_in, v_in, states_in, gains_in, drifts_in, cn_in, cs_in, out, table_ref, *scratch
 ):
     *buffers, sems = scratch
     h = half()
@@ -354,27 +414,50 @@
             for u in range(2):
                 sums[i] = sums[i] + fold(v[a][u], v[b][u])
         for i in range(3):
-            t = jnp.concatenate(v[i], axis=0).T
-            for b in range(LAT):
-                first = (i * 3 + l) * 16
-                out[b, first : first + 16] = t[b * 16 : b * 16 + 16]
+            for u in range(2):
+                out[i * 3 + l, u] = v[i][u]
     lane = lanes((1, 128))
     table = jnp.zeros((1, 128), F32)
     for i in range(5):
         whole = jnp.sum(jnp.sum(sums[i], axis=0, keepdims=True), axis=1, keepdims=True)
         table = jnp.where(lane == i, whole, table)
-    for b in range(LAT):
-        out[b, 144:] = jnp.broadcast_to(table, (8, 128))
-
-
-def share_kernel(x, out):
-    total = jnp.sum(x[:, 144:152], axis=0)
-    for j in range(LON):
-        out[j] = total
-
-
-def final_kernel(x, parts, increment, residual):
-    total = jnp.sum(parts[...], axis=0)[:1]
+    table_ref[...] = jnp.broadcast_to(table, (ALL, 128))
+
+
+def turn_kernel(x, keep, give):
+    h = half()
+    for f in range(9):
+        t = jnp.concatenate([x[f, 0], x[f, 1]], axis=0).T
+        for n in range(4):
+            first, second = t[n * 32 : n * 32 + 16], t[n * 32 + 16 : n * 32 + 32]
+
+            @pl.when(h == 0)
+            def _():
+                keep[n, f] = first
+                give[n, f] = second
+
+            @pl.when(h != 0)
+            def _():
+                keep[n, f] = second
+                give[n, f] = first
+
+
+def merge_out_kernel(keep, got, *outs):
+    h = half()
+    x = lax.axis_index("lat") >> 1
+    low = lanes((16, 128)) < 64
+    first = jnp.full((16, 128), h, I32) == 0
+    for t, out in enumerate(outs):
+        for f in range(9):
+            a, b = keep[x ^ t, f], got[x ^ t, f]
+            x0, x1 = jnp.where(first, a, b), jnp.where(first, b, a)
+            out[f, pl.ds(0, 16, stride=2), :] = jnp.where(low, x0, pltpu.roll(x1, 64, 1))
+            out[f, pl.ds(1, 16, stride=2), :] = jnp.where(low, pltpu.roll(x0, 64, 1), x1)
+
+
+def final_kernel(parts, *refs):
+    *xs, increment, residual = refs
+    total = jnp.sum(parts[...], axis=0, keepdims=True)
     lane = lanes((1, 128))
     pick = lambda i: jnp.sum(jnp.where(lane == i, total, 0.0), axis=1, keepdims=True)
     a00, a01, a11, a02, a12 = [jnp.broadcast_to(pick(i), (1, 128)) for i in range(5)]
@@ -385,19 +468,13 @@
     second = new / curve
     a = alpha + second * keep1
     b = alpha * second
-    low = lanes((16, 128)) < 64
-    for level in range(12):
-        q, l = level // 3, level % 3
-        got = []
-        for h in range(2):
-            v0, v1, v2 = [
-                x[2 * q + h, (i * 3 + l) * 16 : (i * 3 + l) * 16 + 16] for i in range(3)
-            ]
-            got.append((a * v0 - b * v1, v0 - a * v1 + b * v2))
-        for i, ref in enumerate((increment, residual)):
-            x0, x1 = got[0][i], got[1][i]
-            ref[level, pl.ds(0, 16, stride=2), :] = jnp.where(low, x0, pltpu.roll(x1, 64, 1))
-            ref[level, pl.ds(1, 16, stride=2), :] = jnp.where(low, pltpu.roll(x0, 64, 1), x1)
+    mine = lax.axis_index("lat") >> 1
+    for t, x in enumerate(xs):
+        for l in range(LV):
+            v0, v1, v2 = x[l], x[3 + l], x[6 + l]
+            level = 3 * (mine ^ t) + l
+            increment[level] = a * v0 - b * v1
+            residual[level] = v0 - a * v1 + b * v2
 
 
 VM = pl.BlockSpec(memory_space=pltpu.VMEM)
@@ -441,6 +518,15 @@
     return ra, rb
 
 
+def flip(x, bits):
+    pairs = [(i * LON + j, (i ^ bits) * LON + j) for i in range(LAT) for j in range(LON)]
+    return lax.ppermute(x, ("lat", "lon"), pairs)
+
+
+def ring(blocks):
+    return [blocks[0]] + [flip(blocks[t], 2 * t) for t in range(1, 4)]
+
+
 def on_device(
     background, wind_lon, wind_lat, obs_value, obs_weight, obs_tile, obs_cell, obs_step, obs_count
 ):
@@ -448,6 +534,9 @@
     plane = (LV, 2, EXT, 128)
     middle = (LV, 2, COL, 128)
 
+    group = (4, 9, 16, 128)
+    keep, give = call(prep_kernel, [group] * 2, background, wind_lon, wind_lat, ins="hhh")
+    got = flip(give, 1)
     fold = lambda a: a.reshape(16, 128)
     packed = call(
         pack_kernel,
@@ -469,13 +558,13 @@
         ],
     )
     arrived = lax.all_to_all(packed, both, 0, 0, tiled=True)
-    sent = call(prep_kernel, [(LAT, 9, 16, 128)], background, wind_lon, wind_lat, ins="hhh")
-    moved = lax.all_to_all(sent, "lat", 0, 0, tiled=True)
+    blocks = ring(call(merge_in_kernel, [(2, 9, 16, 128)] * 4, keep, got))
     fields, sa, sb = call(
         recv_kernel,
         [(9, 2, COL, 128)] + [(9, 2, EDGE, 128)] * 2,
-        moved,
+        *blocks,
         space="hvv",
+        scratch=[pltpu.VMEM((9, 128, 128), F32)],
     )
     ra, rb = swap(sa, sb)
     wsum, vsum, sa, sb = call(
@@ -485,9 +574,10 @@
         space="hhvv",
         scratch=[
             pltpu.VMEM((4, 256, 128), F32),
-            pltpu.VMEM((ROWS, 1024), BF16),
-            pltpu.VMEM((1280, 1024), BF16),
-            pltpu.VMEM((ROWS, 1280), F32),
+            pltpu.VMEM((7, SEG, 128), F32),
+            pltpu.VMEM((5 * LV * COL, GROUP * 128), BF16),
+            pltpu.VMEM((256, GROUP * 128), BF16),
+            pltpu.VMEM((STEPS * 5 * LV * COL, 256), F32),
         ],
     )
     wa, wb = swap(sa, sb)
@@ -497,9 +587,9 @@
     big = pltpu.VMEM((STEPS,) + plane, F32)
     mid = pltpu.VMEM((STEPS,) + middle, F32)
     small = pltpu.VMEM(plane, F32)
-    sent = call(
+    vectors, table = call(
         core_kernel,
-        [(LAT, 152, 128)],
+        [(9, 2, COL, 128), (ALL, 128)],
         wa,
         wb,
         wsum,
@@ -508,9 +598,11 @@
         ins="vv" + "a" * 7,
         scratch=[mid, mid, big, big, big, small, small, pltpu.SemaphoreType.DMA((LV, 7))],
     )
-    moved = lax.all_to_all(sent, "lat", 0, 0, tiled=True)
-    parts = lax.all_to_all(call(share_kernel, [(LON, 8, 128)], moved), "lon", 0, 0, tiled=True)
-    return call(final_kernel, [(12, 32, 128)] * 2, moved, parts, space="h")
+    keep, give = call(turn_kernel, [group] * 2, vectors)
+    got = flip(give, 1)
+    parts = lax.all_to_all(table, both, 0, 0, tiled=True)
+    blocks = ring(call(merge_out_kernel, [(9, 32, 128)] * 4, keep, got))
+    return call(final_kernel, [(12, 32, 128)] * 2, parts, *blocks, space="h")
 
 
 def solution(mesh):

time: 99.9 us -> 98.1 us (0.982)
  blocking collectives: 26.8 us -> 16.9 us
  starting transfers between devices: 20.3 us -> 26.8 us
  waiting for transfers between devices: 19.5 us -> 22.6 us
    ppermute x0 -> x8, starting transfers between devices: none -> 11.1 us  [flip(): return lax.ppermute(x, ('lat', 'lon'), pairs)]
    all_to_all x2 -> x1, blocking collectives: 26.8 us -> 16.9 us  [on_device(): parts = lax.all_to_all(table, both, 0, 0, tiled=True)]
    ppermute x0 -> x8, waiting for transfers between devices: none -> 8.84 us  [flip(): return lax.ppermute(x, ('lat', 'lon'), pairs)]
    all_to_all x1 -> x0, starting transfers between devices: 4.03 us -> none  [on_device(): moved = lax.all_to_all(sent, 'lat', 0, 0, tiled=True)]
    ppermute x2, waiting for transfers between devices: 7.63 us -> 4.26 us  [swap(): rb = lax.ppermute(sb, ('lat', 'lon'), far)]
    all_to_all x1, waiting for transfers between devices: 11.9 us -> 8.59 us  [on_device(): arrived = lax.all_to_all(packed, both, 0, 0, tiled=True)]
    pallas_call x8 -> x10, Pallas kernels: 30.6 us -> 30.1 us  [call(): return make(kernel, shapes, ins, scratch)(*args)]
  transfers between devices with their start and end apart: 6 -> 13, of which waited for: 2 -> 7; matrix products, arithmetic and copies ran while one was open for 0% -> 0% of each run, Pallas kernels for 19% -> 18%
where the time goes in v5:
time: 98.1 us; the launch traced here: 97.8 us
  Pallas kernels  30.1 us (31%)
  starting transfers between devices  26.8 us (27%)
  waiting for transfers between devices  22.6 us (23%)
  blocking collectives  16.9 us (17%)
  between operations  1.33 us (1%)
    pallas_call x10, Pallas kernels, call(): return make(kernel, shapes, ins, scratch)(*args)  30.1 us
    all_to_all x1, blocking collectives, on_device(): parts = lax.all_to_all(table, both, 0, 0, tiled=True)  16.9 us
    all_to_all x1, starting transfers between devices, on_device(): arrived = lax.all_to_all(packed, both, 0, 0, tiled=True)  11.5 us
    ppermute x8, starting transfers between devices, flip(): return lax.ppermute(x, ('lat', 'lon'), pairs)  11.1 us
    ppermute x8, waiting for transfers between devices, flip(): return lax.ppermute(x, ('lat', 'lon'), pairs)  8.84 us
    all_to_all x1, waiting for transfers between devices, on_device(): arrived = lax.all_to_all(packed, both, 0, 0, tiled=True)  8.59 us
    ppermute x2, waiting for transfers between devices, swap(): rb = lax.ppermute(sb, ('lat', 'lon'), far)  4.26 us
    ppermute x2, starting transfers between devices, swap(): ra = lax.ppermute(sa, ('lat', 'lon'), near)  2.77 us
  transfers between devices with their start and end apart: 13, of which 7 were waited for; matrix products, arithmetic and copies ran while one was open for 0% of the time, Pallas kernels for 18%

profile of v5, /device:TPU:1, one launch (start us, length us, event | category | flops | bytes accessed | tf_op | source)
XLA Modules:
  0.0 97.8 jit_solution(7571996197867841107)
XLA Ops:
  1.3 3.9 %shard_map.104 = f32[128,8,128]{2,1,0:T(8,128)} custom-call(s32[1]{0:T(128)S(6)} %copy.12.count, s32[16,128]{1,0:T(8,128)} %bitcast.11, s32[16,128]{1,0:T(8,128)} %bitcast.12, s32[16,128]{1,0:T(8,128)} %bitcast.13, f32[16,128]{1,0:T(8,128)} %bitcast.14, f32[16,128]{1,0:T(8,128)} %bitcast.15), custom_call_target="tpu_custom_call" | custom-call | tf_op jit(solution)/shard_map/pallas_call | solution.py:495
  5.2 11.5 %all-to-all-start = ((f32[128,8,128]{2,1,0:T(8,128)}), f32[128,8,128]{2,1,0:T(8,128)S(1)}, u32[]{:S(2)}, u32[]{:S(2)}) async-start(f32[128,8,128]{2,1,0:T(8,128)} %shard_map.104), calls=%async_computation | async-start | bytes 1048576 | tf_op jit(solution)/shard_map/all_to_all | solution.py:560
  16.7 4.4 %shard_map.106 = (f32[4,9,16,128]{3,2,1,0:T(8,128)S(1)}, f32[4,9,16,128]{3,2,1,0:T(8,128)}) custom-call(f32[12,32,128]{2,1,0:T(8,128)} %bg.1, f32[12,32,128]{2,1,0:T(8,128)} %wl.1, f32[12,32,128]{2,1,0:T(8,128)} %wt.1), custom_call_target="tpu_custom_call" | custom-call | tf_op jit(solution)/shard_map/pallas_call | solution.py:495
  21.1 1.0 %collective-permute-start.2 = (f32[4,9,16,128]{3,2,1,0:T(8,128)}, f32[4,9,16,128]{3,2,1,0:T(8,128)S(1)}, u32[]{:S(2)}, u32[]{:S(2)}) collective-permute-start(f32[4,9,16,128]{3,2,1,0:T(8,128)} %get-tuple-element.33), channel_id=1, source_target_pairs={{0,16},{1,17},{2,18},{3,19},{4,20},{5,21},{6,22},{7,23},{8,24},{9,... | collective-permute-start | bytes 884744 | tf_op jit(solution)/shard_map/ppermute | solution.py:523
  22.2 8.6 %all-to-all-done.x = f32[128,8,128]{2,1,0:T(8,128)S(1)} async-done(((f32[128,8,128]{2,1,0:T(8,128)}), f32[128,8,128]{2,1,0:T(8,128)S(1)}, u32[]{:S(2)}, u32[]{:S(2)}) %all-to-all-start) | async-done | bytes 524320 | tf_op jit(solution)/shard_map/all_to_all | solution.py:560
  30.8 7.5 %shard_map.105 = (f32[4,3,2,64,128]{4,3,2,1,0:T(8,128)}, f32[4,3,2,64,128]{4,3,2,1,0:T(8,128)}, f32[4,3,2,40,128]{4,3,2,1,0:T(8,128)}, f32[4,3,2,40,128]{4,3,2,1,0:T(8,128)}) custom-call(f32[128,8,128]{2,1,0:T(8,128)S(1)} %all-to-all-done.x), custom_call_target="tpu_custom_call" | custom-call | tf_op jit(solution)/shard_map/pallas_call | solution.py:495
  38.3 1.7 %collective-permute-start = (f32[4,3,2,40,128]{4,3,2,1,0:T(8,128)}, f32[4,3,2,40,128]{4,3,2,1,0:T(8,128)S(1)}, u32[]{:S(2)}, u32[]{:S(2)}) collective-permute-start(f32[4,3,2,40,128]{4,3,2,1,0:T(8,128)} %get-tuple-element.28), channel_id=1, source_target_pairs={{0,16},{1,17},{2,18},{3,19},{4,20},{5,21},{6,22},{7,23},{8,24},{9,... | collective-permute-start | bytes 1474568 | tf_op jit(solution)/shard_map/ppermute | solution.py:517
  39.9 1.3 %collective-permute-start.1 = (f32[4,3,2,40,128]{4,3,2,1,0:T(8,128)}, f32[4,3,2,40,128]{4,3,2,1,0:T(8,128)S(1)}, u32[]{:S(2)}, u32[]{:S(2)}) collective-permute-start(f32[4,3,2,40,128]{4,3,2,1,0:T(8,128)} %get-tuple-element.29), channel_id=1, source_target_pairs={{0,31},{1,16},{2,17},{3,18},{4,19},{5,20},{6,21},{7,22},{8,23},{9,... | collective-permute-start | bytes 1474568 | tf_op jit(solution)/shard_map/ppermute | solution.py:516
  41.7 1.8 %collective-permute-start.4 = (f32[2,9,16,128]{3,2,1,0:T(8,128)S(1)}, f32[2,9,16,128]{3,2,1,0:T(8,128)S(1)}, u32[]{:S(2)}, u32[]{:S(2)}) collective-permute-start(f32[2,9,16,128]{3,2,1,0:T(8,128)S(1)} %get-tuple-element.36), channel_id=1, source_target_pairs={{0,64},{1,65},{2,66},{3,67},{4,68},{5,69},{6,70},{7,71},{8,72},{9,... | collective-permute-start | bytes 442376 | tf_op jit(solution)/shard_map/ppermute | solution.py:523
  43.4 1.8 %collective-permute-start.5 = (f32[2,9,16,128]{3,2,1,0:T(8,128)S(1)}, f32[2,9,16,128]{3,2,1,0:T(8,128)S(1)}, u32[]{:S(2)}, u32[]{:S(2)}) collective-permute-start(f32[2,9,16,128]{3,2,1,0:T(8,128)S(1)} %get-tuple-element.37), channel_id=1, source_target_pairs={{0,96},{1,97},{2,98},{3,99},{4,100},{5,101},{6,102},{7,103},{8,104... | collective-permute-start | bytes 442376 | tf_op jit(solution)/shard_map/ppermute | solution.py:523
  45.2 2.0 %collective-permute-done.3.refs_1_ = f32[2,9,16,128]{3,2,1,0:T(8,128)S(1)} collective-permute-done((f32[2,9,16,128]{3,2,1,0:T(8,128)S(1)}, f32[2,9,16,128]{3,2,1,0:T(8,128)S(1)}, u32[]{:S(2)}, u32[]{:S(2)}) %collective-permute-start.3) | collective-permute-done | bytes 147488 | tf_op jit(solution)/shard_map/ppermute | solution.py:523
  47.2 3.0 %collective-permute-done.4.refs_2_ = f32[2,9,16,128]{3,2,1,0:T(8,128)S(1)} collective-permute-done((f32[2,9,16,128]{3,2,1,0:T(8,128)S(1)}, f32[2,9,16,128]{3,2,1,0:T(8,128)S(1)}, u32[]{:S(2)}, u32[]{:S(2)}) %collective-permute-start.4) | collective-permute-done | bytes 147488 | tf_op jit(solution)/shard_map/ppermute | solution.py:523
  50.3 2.6 %collective-permute-done.5.refs_3_ = f32[2,9,16,128]{3,2,1,0:T(8,128)S(1)} collective-permute-done((f32[2,9,16,128]{3,2,1,0:T(8,128)S(1)}, f32[2,9,16,128]{3,2,1,0:T(8,128)S(1)}, u32[]{:S(2)}, u32[]{:S(2)}) %collective-permute-start.5) | collective-permute-done | bytes 147488 | tf_op jit(solution)/shard_map/ppermute | solution.py:523
  52.8 1.8 %shard_map.108 = (f32[9,2,64,128]{3,2,1,0:T(8,128)}, f32[9,2,24,128]{3,2,1,0:T(8,128)S(1)}, f32[9,2,24,128]{3,2,1,0:T(8,128)S(1)}) custom-call(f32[2,9,16,128]{3,2,1,0:T(8,128)S(1)} %get-tuple-element.34.refs_0_, f32[2,9,16,128]{3,2,1,0:T(8,128)S(1)} %collective-permute-done.3.refs_1_, f32[2,9,16,128]{3,2,1,0:T(8,128)S(1)} %collective-permute-done.4.refs_2_, ...), custom_call_target="tpu_custom_call" | custom-call | tf_op jit(solution)/shard_map/pallas_call | solution.py:495
  54.6 1.1 %collective-permute-start.6 = (f32[9,2,24,128]{3,2,1,0:T(8,128)S(1)}, f32[9,2,24,128]{3,2,1,0:T(8,128)S(1)}, u32[]{:S(2)}, u32[]{:S(2)}) collective-permute-start(f32[9,2,24,128]{3,2,1,0:T(8,128)S(1)} %get-tuple-element.39), channel_id=1, source_target_pairs={{0,16},{1,17},{2,18},{3,19},{4,20},{5,21},{6,22},{7,23},{8,24},{9,... | collective-permute-start | bytes 663560 | tf_op jit(solution)/shard_map/ppermute | solution.py:517
  55.9 0.9 collective-permute-done.6.ra
  56.8 4.3 %collective-permute-done.7.rb = f32[9,2,24,128]{3,2,1,0:T(8,128)S(1)} collective-permute-done((f32[9,2,24,128]{3,2,1,0:T(8,128)S(1)}, f32[9,2,24,128]{3,2,1,0:T(8,128)S(1)}, u32[]{:S(2)}, u32[]{:S(2)}) %collective-permute-start.7) | collective-permute-done | bytes 221216 | tf_op jit(solution)/shard_map/ppermute | solution.py:516
  61.1 4.0 %shard_map.109 = (f32[4,3,2,112,128]{4,3,2,1,0:T(8,128)}, f32[4,3,2,112,128]{4,3,2,1,0:T(8,128)}, f32[4,3,2,112,128]{4,3,2,1,0:T(8,128)}, f32[3,2,112,128]{3,2,1,0:T(8,128)}, f32[3,2,112,128]{3,2,1,0:T(8,128)}) custom-call(f32[9,2,64,128]{3,2,1,0:T(8,128)} %get-tuple-element.38.center, f32[9,2,24,128]{3,2,1,0:T(8,128)S(1)} %collective-permute-done.6.ra, ...), custom_call_target="tpu_custom_call" | custom-call | tf_op jit(solution)/shard_map/pallas_call | solution.py:495
  65.1 6.4 %shard_map.110 = (f32[9,2,64,128]{3,2,1,0:T(8,128)S(1)}, f32[128,128]{1,0:T(8,128)S(1)}) custom-call(f32[4,3,2,40,128]{4,3,2,1,0:T(8,128)S(1)} %collective-permute-done.ra, f32[4,3,2,40,128]{4,3,2,1,0:T(8,128)S(1)} %collective-permute-done.1.rb, f32[4,3,2,64,128]{4,3,2,1,0:T(8,128)} %get-tuple-element.30.w_in, f32[4,3,2,64,128]{4,3,2,1,0:T(8,128)} %get-tuple-element.31.v_in, ...), custom_call_target="tpu_custom_call" | custom-call | tf_op jit(solution)/shard_map/pallas_call | solution.py:495
  71.5 0.9 shard_map.111
  72.4 3.4 %collective-permute-start.8 = (f32[4,9,16,128]{3,2,1,0:T(8,128)S(1)}, f32[4,9,16,128]{3,2,1,0:T(8,128)S(1)}, u32[]{:S(2)}, u32[]{:S(2)}) collective-permute-start(f32[4,9,16,128]{3,2,1,0:T(8,128)S(1)} %get-tuple-element.49), channel_id=1, source_target_pairs={{0,16},{1,17},{2,18},{3,19},{4,20},{5,21},{6,22},{7,23},{8,24},{9,... | collective-permute-start | bytes 884744 | tf_op jit(solution)/shard_map/ppermute | solution.py:523
  75.8 1.2 %collective-permute-done.8.got = f32[4,9,16,128]{3,2,1,0:T(8,128)S(1)} collective-permute-done((f32[4,9,16,128]{3,2,1,0:T(8,128)S(1)}, f32[4,9,16,128]{3,2,1,0:T(8,128)S(1)}, u32[]{:S(2)}, u32[]{:S(2)}) %collective-permute-start.8) | collective-permute-done | bytes 294944 | tf_op jit(solution)/shard_map/ppermute | solution.py:523
  77.5 1.8 %collective-permute-start.11 = (f32[9,32,128]{2,1,0:T(8,128)S(1)}, f32[9,32,128]{2,1,0:T(8,128)S(1)}, u32[]{:S(2)}, u32[]{:S(2)}) collective-permute-start(f32[9,32,128]{2,1,0:T(8,128)S(1)} %get-tuple-element.53), channel_id=1, source_target_pairs={{0,96},{1,97},{2,98},{3,99},{4,100},{5,101},{6,102},{7,103},{8,104... | collective-permute-start | bytes 442376 | tf_op jit(solution)/shard_map/ppermute | solution.py:523
  80.0 16.9 %all_to_all.16 = f32[128,1,128]{2,1,0:T(1,128)S(1)} all-to-all(f32[128,1,128]{2,1,0:T(1,128)S(1)} %bitcast.10), channel_id=1, replica_groups=mesh['lat'=8,'lon'=16] {'lat','lon'}, dimensions={0} | all-to-all | bytes 131072 | tf_op jit(solution)/shard_map/all_to_all | solution.py:603
  (13 shorter events, 2.7 us)
Async XLA Ops:
  5.2 25.5 %all-to-all-start = ((f32[128,8,128]{2,1,0:T(8,128)}), f32[128,8,128]{2,1,0:T(8,128)S(1)}, u32[]{:S(2)}, u32[]{:S(2)}) async-start(f32[128,8,128]{2,1,0:T(8,128)} %shard_map.104), calls=%async_computation | async-start | bytes 1048576 | tf_op jit(solution)/shard_map/all_to_all | solution.py:560
  21.1 20.1 %collective-permute-start.2 = (f32[4,9,16,128]{3,2,1,0:T(8,128)}, f32[4,9,16,128]{3,2,1,0:T(8,128)S(1)}, u32[]{:S(2)}, u32[]{:S(2)}) collective-permute-start(f32[4,9,16,128]{3,2,1,0:T(8,128)} %get-tuple-element.33), channel_id=1, source_target_pairs={{0,16},{1,17},{2,18},{3,19},{4,20},{5,21},{6,22},{7,23},{8,24},{9,... | collective-permute-start | bytes 884744 | tf_op jit(solution)/shard_map/ppermute | solution.py:523
  38.3 26.8 %collective-permute-start = (f32[4,3,2,40,128]{4,3,2,1,0:T(8,128)}, f32[4,3,2,40,128]{4,3,2,1,0:T(8,128)S(1)}, u32[]{:S(2)}, u32[]{:S(2)}) collective-permute-start(f32[4,3,2,40,128]{4,3,2,1,0:T(8,128)} %get-tuple-element.28), channel_id=1, source_target_pairs={{0,16},{1,17},{2,18},{3,19},{4,20},{5,21},{6,22},{7,23},{8,24},{9,... | collective-permute-start | bytes 1474568 | tf_op jit(solution)/shard_map/ppermute | solution.py:517
  39.9 25.2 %collective-permute-start.1 = (f32[4,3,2,40,128]{4,3,2,1,0:T(8,128)}, f32[4,3,2,40,128]{4,3,2,1,0:T(8,128)S(1)}, u32[]{:S(2)}, u32[]{:S(2)}) collective-permute-start(f32[4,3,2,40,128]{4,3,2,1,0:T(8,128)} %get-tuple-element.29), channel_id=1, source_target_pairs={{0,31},{1,16},{2,17},{3,18},{4,19},{5,20},{6,21},{7,22},{8,23},{9,... | collective-permute-start | bytes 1474568 | tf_op jit(solution)/shard_map/ppermute | solution.py:516
  41.3 5.9 %collective-permute-start.3 = (f32[2,9,16,128]{3,2,1,0:T(8,128)S(1)}, f32[2,9,16,128]{3,2,1,0:T(8,128)S(1)}, u32[]{:S(2)}, u32[]{:S(2)}) collective-permute-start(f32[2,9,16,128]{3,2,1,0:T(8,128)S(1)} %get-tuple-element.35), channel_id=1, source_target_pairs={{0,32},{1,33},{2,34},{3,35},{4,36},{5,37},{6,38},{7,39},{8,40},{9,... | collective-permute-start | bytes 442376 | tf_op jit(solution)/shard_map/ppermute | solution.py:523
  41.7 8.6 %collective-permute-start.4 = (f32[2,9,16,128]{3,2,1,0:T(8,128)S(1)}, f32[2,9,16,128]{3,2,1,0:T(8,128)S(1)}, u32[]{:S(2)}, u32[]{:S(2)}) collective-permute-start(f32[2,9,16,128]{3,2,1,0:T(8,128)S(1)} %get-tuple-element.36), channel_id=1, source_target_pairs={{0,64},{1,65},{2,66},{3,67},{4,68},{5,69},{6,70},{7,71},{8,72},{9,... | collective-permute-start | bytes 442376 | tf_op jit(solution)/shard_map/ppermute | solution.py:523
  43.4 9.4 %collective-permute-start.5 = (f32[2,9,16,128]{3,2,1,0:T(8,128)S(1)}, f32[2,9,16,128]{3,2,1,0:T(8,128)S(1)}, u32[]{:S(2)}, u32[]{:S(2)}) collective-permute-start(f32[2,9,16,128]{3,2,1,0:T(8,128)S(1)} %get-tuple-element.37), channel_id=1, source_target_pairs={{0,96},{1,97},{2,98},{3,99},{4,100},{5,101},{6,102},{7,103},{8,104... | collective-permute-start | bytes 442376 | tf_op jit(solution)/shard_map/ppermute | solution.py:523
  54.6 2.2 %collective-permute-start.6 = (f32[9,2,24,128]{3,2,1,0:T(8,128)S(1)}, f32[9,2,24,128]{3,2,1,0:T(8,128)S(1)}, u32[]{:S(2)}, u32[]{:S(2)}) collective-permute-start(f32[9,2,24,128]{3,2,1,0:T(8,128)S(1)} %get-tuple-element.39), channel_id=1, source_target_pairs={{0,16},{1,17},{2,18},{3,19},{4,20},{5,21},{6,22},{7,23},{8,24},{9,... | collective-permute-start | bytes 663560 | tf_op jit(solution)/shard_map/ppermute | solution.py:517
  55.7 5.4 %collective-permute-start.7 = (f32[9,2,24,128]{3,2,1,0:T(8,128)S(1)}, f32[9,2,24,128]{3,2,1,0:T(8,128)S(1)}, u32[]{:S(2)}, u32[]{:S(2)}) collective-permute-start(f32[9,2,24,128]{3,2,1,0:T(8,128)S(1)} %get-tuple-element.40), channel_id=1, source_target_pairs={{0,31},{1,16},{2,17},{3,18},{4,19},{5,20},{6,21},{7,22},{8,23},{9,... | collective-permute-start | bytes 663560 | tf_op jit(solution)/shard_map/ppermute | solution.py:516
  72.4 4.6 %collective-permute-start.8 = (f32[4,9,16,128]{3,2,1,0:T(8,128)S(1)}, f32[4,9,16,128]{3,2,1,0:T(8,128)S(1)}, u32[]{:S(2)}, u32[]{:S(2)}) collective-permute-start(f32[4,9,16,128]{3,2,1,0:T(8,128)S(1)} %get-tuple-element.49), channel_id=1, source_target_pairs={{0,16},{1,17},{2,18},{3,19},{4,20},{5,21},{6,22},{7,23},{8,24},{9,... | collective-permute-start | bytes 884744 | tf_op jit(solution)/shard_map/ppermute | solution.py:523
  77.2 19.6 %collective-permute-start.10 = (f32[9,32,128]{2,1,0:T(8,128)S(1)}, f32[9,32,128]{2,1,0:T(8,128)S(1)}, u32[]{:S(2)}, u32[]{:S(2)}) collective-permute-start(f32[9,32,128]{2,1,0:T(8,128)S(1)} %get-tuple-element.52), channel_id=1, source_target_pairs={{0,64},{1,65},{2,66},{3,67},{4,68},{5,69},{6,70},{7,71},{8,72},{9,... | collective-permute-start | bytes 442376 | tf_op jit(solution)/shard_map/ppermute | solution.py:523
  77.5 19.4 %collective-permute-start.11 = (f32[9,32,128]{2,1,0:T(8,128)S(1)}, f32[9,32,128]{2,1,0:T(8,128)S(1)}, u32[]{:S(2)}, u32[]{:S(2)}) collective-permute-start(f32[9,32,128]{2,1,0:T(8,128)S(1)} %get-tuple-element.53), channel_id=1, source_target_pairs={{0,96},{1,97},{2,98},{3,99},{4,100},{5,101},{6,102},{7,103},{8,104... | collective-permute-start | bytes 442376 | tf_op jit(solution)/shard_map/ppermute | solution.py:523
  79.3 17.6 %collective-permute-start.9 = (f32[9,32,128]{2,1,0:T(8,128)S(1)}, f32[9,32,128]{2,1,0:T(8,128)S(1)}, u32[]{:S(2)}, u32[]{:S(2)}) collective-permute-start(f32[9,32,128]{2,1,0:T(8,128)S(1)} %get-tuple-element.51), channel_id=1, source_target_pairs={{0,32},{1,33},{2,34},{3,35},{4,36},{5,37},{6,38},{7,39},{8,40},{9,... | collective-permute-start | bytes 442376 | tf_op jit(solution)/shard_map/ppermute | solution.py:523

commit v6 on v5

--- a/solution.py
+++ b/solution.py
@@ -35,6 +35,11 @@
     return lax.rem(lax.axis_index("lat"), 2)
 
 
+def sort_halves(h, x, y):
+    first = jnp.full(x.shape, h, I32) == 0
+    return jnp.where(first, x, y), jnp.where(first, y, x)
+
+
 def prep_kernel(bg, wl, wt, keep, give):
     low = lanes((16, 128)) < 64
     h = half()
@@ -43,18 +48,9 @@
             q, l = level // 3, level % 3
             even = ref[level, pl.ds(0, 16, stride=2), :]
             odd = ref[level, pl.ds(1, 16, stride=2), :]
-            first = jnp.where(low, even, pltpu.roll(odd, 64, 1))
-            second = jnp.where(low, pltpu.roll(even, 64, 1), odd)
-
-            @pl.when(h == 0)
-            def _():
-                keep[q, f * 3 + l] = first
-                give[q, f * 3 + l] = second
-
-            @pl.when(h != 0)
-            def _():
-                keep[q, f * 3 + l] = second
-                give[q, f * 3 + l] = first
+            x = jnp.where(low, even, pltpu.roll(odd, 64, 1))
+            y = jnp.where(low, pltpu.roll(even, 64, 1), odd)
+            keep[q, f * 3 + l], give[q, f * 3 + l] = sort_halves(h, x, y)
 
 
 def merge_in_kernel(keep, got, *outs):
@@ -66,21 +62,11 @@
 
 
 def put_edges(sa, sb, index, lo, hi, h):
-    @pl.when(h == 0)
-    def _():
-        sa[index] = hi
-        sb[index] = lo
-
-    @pl.when(h != 0)
-    def _():
-        sa[index] = lo
-        sb[index] = hi
+    sa[index], sb[index] = sort_halves(h, hi, lo)
 
 
 def get_edges(ra, rb, index, h):
-    a, b = ra[index], rb[index]
-    first = jnp.full(a.shape, h, I32) == 0
-    return jnp.where(first, b, a), jnp.where(first, a, b)
+    return sort_halves(h, rb[index], ra[index])
 
 
 def recv_kernel(*refs):
@@ -430,27 +416,16 @@
         t = jnp.concatenate([x[f, 0], x[f, 1]], axis=0).T
         for n in range(4):
             first, second = t[n * 32 : n * 32 + 16], t[n * 32 + 16 : n * 32 + 32]
-
-            @pl.when(h == 0)
-            def _():
-                keep[n, f] = first
-                give[n, f] = second
-
-            @pl.when(h != 0)
-            def _():
-                keep[n, f] = second
-                give[n, f] = first
+            keep[n, f], give[n, f] = sort_halves(h, first, second)
 
 
 def merge_out_kernel(keep, got, *outs):
     h = half()
     x = lax.axis_index("lat") >> 1
     low = lanes((16, 128)) < 64
-    first = jnp.full((16, 128), h, I32) == 0
     for t, out in enumerate(outs):
         for f in range(9):
-            a, b = keep[x ^ t, f], got[x ^ t, f]
-            x0, x1 = jnp.where(first, a, b), jnp.where(first, b, a)
+            x0, x1 = sort_halves(h, keep[x ^ t, f], got[x ^ t, f])
             out[f, pl.ds(0, 16, stride=2), :] = jnp.where(low, x0, pltpu.roll(x1, 64, 1))
             out[f, pl.ds(1, 16, stride=2), :] = jnp.where(low, pltpu.roll(x0, 64, 1), x1)
 

time: 98.1 us -> 96.4 us (0.983)
  Pallas kernels: 30.1 us -> 26.1 us
  waiting for transfers between devices: 22.6 us -> 25 us
    pallas_call x10, Pallas kernels: 30.1 us -> 26.1 us  [call(): return make(kernel, shapes, ins, scratch)(*args)]
    all_to_all x1, waiting for transfers between devices: 8.59 us -> 10.9 us  [on_device(): arrived = lax.all_to_all(packed, both, 0, 0, tiled=True)]
  transfers between devices with their start and end apart: 13 -> 13, of which waited for: 7 -> 7; matrix products, arithmetic and copies ran while one was open for 0% -> 0% of each run, Pallas kernels for 18% -> 15%
where the time goes in v6:
time: 96.4 us; the launch traced here: 96.1 us
  starting transfers between devices  26.8 us (28%)
  Pallas kernels  26.1 us (27%)
  waiting for transfers between devices  25 us (26%)
  blocking collectives  16.9 us (18%)
  between operations  1.33 us (1%)
    pallas_call x10, Pallas kernels, call(): return make(kernel, shapes, ins, scratch)(*args)  26.1 us
    all_to_all x1, blocking collectives, on_device(): parts = lax.all_to_all(table, both, 0, 0, tiled=True)  16.9 us
    all_to_all x1, starting transfers between devices, on_device(): arrived = lax.all_to_all(packed, both, 0, 0, tiled=True)  11.5 us
    ppermute x8, starting transfers between devices, flip(): return lax.ppermute(x, ('lat', 'lon'), pairs)  11.1 us
    all_to_all x1, waiting for transfers between devices, on_device(): arrived = lax.all_to_all(packed, both, 0, 0, tiled=True)  10.9 us
    ppermute x8, waiting for transfers between devices, flip(): return lax.ppermute(x, ('lat', 'lon'), pairs)  8.84 us
    ppermute x2, waiting for transfers between devices, swap(): rb = lax.ppermute(sb, ('lat', 'lon'), far)  4.26 us
    ppermute x2, starting transfers between devices, swap(): ra = lax.ppermute(sa, ('lat', 'lon'), near)  2.74 us
  transfers between devices with their start and end apart: 13, of which 7 were waited for; matrix products, arithmetic and copies ran while one was open for 0% of the time, Pallas kernels for 15%

profile of v6, /device:TPU:1, one launch (start us, length us, event | category | flops | bytes accessed | tf_op | source)
XLA Modules:
  0.0 96.1 jit_solution(7773286787560345077)
XLA Ops:
  1.3 3.9 %shard_map.104 = f32[128,8,128]{2,1,0:T(8,128)} custom-call(s32[1]{0:T(128)S(6)} %copy.12.count, s32[16,128]{1,0:T(8,128)} %bitcast.11, s32[16,128]{1,0:T(8,128)} %bitcast.12, s32[16,128]{1,0:T(8,128)} %bitcast.13, f32[16,128]{1,0:T(8,128)} %bitcast.14, f32[16,128]{1,0:T(8,128)} %bitcast.15), custom_call_target="tpu_custom_call" | custom-call | tf_op jit(solution)/shard_map/pallas_call | solution.py:470
  5.2 11.5 %all-to-all-start = ((f32[128,8,128]{2,1,0:T(8,128)}), f32[128,8,128]{2,1,0:T(8,128)S(1)}, u32[]{:S(2)}, u32[]{:S(2)}) async-start(f32[128,8,128]{2,1,0:T(8,128)} %shard_map.104), calls=%async_computation | async-start | bytes 1048576 | tf_op jit(solution)/shard_map/all_to_all | solution.py:535
  16.7 2.1 %shard_map.106 = (f32[4,9,16,128]{3,2,1,0:T(8,128)S(1)}, f32[4,9,16,128]{3,2,1,0:T(8,128)}) custom-call(f32[12,32,128]{2,1,0:T(8,128)} %bg.1, f32[12,32,128]{2,1,0:T(8,128)} %wl.1, f32[12,32,128]{2,1,0:T(8,128)} %wt.1), custom_call_target="tpu_custom_call" | custom-call | tf_op jit(solution)/shard_map/pallas_call | solution.py:470
  18.8 1.1 %collective-permute-start.2 = (f32[4,9,16,128]{3,2,1,0:T(8,128)}, f32[4,9,16,128]{3,2,1,0:T(8,128)S(1)}, u32[]{:S(2)}, u32[]{:S(2)}) collective-permute-start(f32[4,9,16,128]{3,2,1,0:T(8,128)} %get-tuple-element.33), channel_id=1, source_target_pairs={{0,16},{1,17},{2,18},{3,19},{4,20},{5,21},{6,22},{7,23},{8,24},{9,... | collective-permute-start | bytes 884744 | tf_op jit(solution)/shard_map/ppermute | solution.py:498
  19.8 10.9 %all-to-all-done.x = f32[128,8,128]{2,1,0:T(8,128)S(1)} async-done(((f32[128,8,128]{2,1,0:T(8,128)}), f32[128,8,128]{2,1,0:T(8,128)S(1)}, u32[]{:S(2)}, u32[]{:S(2)}) %all-to-all-start) | async-done | bytes 524320 | tf_op jit(solution)/shard_map/all_to_all | solution.py:535
  30.8 7.2 %shard_map.105 = (f32[4,3,2,64,128]{4,3,2,1,0:T(8,128)}, f32[4,3,2,64,128]{4,3,2,1,0:T(8,128)}, f32[4,3,2,40,128]{4,3,2,1,0:T(8,128)}, f32[4,3,2,40,128]{4,3,2,1,0:T(8,128)}) custom-call(f32[128,8,128]{2,1,0:T(8,128)S(1)} %all-to-all-done.x), custom_call_target="tpu_custom_call" | custom-call | tf_op jit(solution)/shard_map/pallas_call | solution.py:470
  38.0 1.6 %collective-permute-start = (f32[4,3,2,40,128]{4,3,2,1,0:T(8,128)}, f32[4,3,2,40,128]{4,3,2,1,0:T(8,128)S(1)}, u32[]{:S(2)}, u32[]{:S(2)}) collective-permute-start(f32[4,3,2,40,128]{4,3,2,1,0:T(8,128)} %get-tuple-element.28), channel_id=1, source_target_pairs={{0,16},{1,17},{2,18},{3,19},{4,20},{5,21},{6,22},{7,23},{8,24},{9,... | collective-permute-start | bytes 1474568 | tf_op jit(solution)/shard_map/ppermute | solution.py:492
  39.6 1.3 %collective-permute-start.1 = (f32[4,3,2,40,128]{4,3,2,1,0:T(8,128)}, f32[4,3,2,40,128]{4,3,2,1,0:T(8,128)S(1)}, u32[]{:S(2)}, u32[]{:S(2)}) collective-permute-start(f32[4,3,2,40,128]{4,3,2,1,0:T(8,128)} %get-tuple-element.29), channel_id=1, source_target_pairs={{0,31},{1,16},{2,17},{3,18},{4,19},{5,20},{6,21},{7,22},{8,23},{9,... | collective-permute-start | bytes 1474568 | tf_op jit(solution)/shard_map/ppermute | solution.py:491
  41.4 1.8 %collective-permute-start.4 = (f32[2,9,16,128]{3,2,1,0:T(8,128)S(1)}, f32[2,9,16,128]{3,2,1,0:T(8,128)S(1)}, u32[]{:S(2)}, u32[]{:S(2)}) collective-permute-start(f32[2,9,16,128]{3,2,1,0:T(8,128)S(1)} %get-tuple-element.36), channel_id=1, source_target_pairs={{0,64},{1,65},{2,66},{3,67},{4,68},{5,69},{6,70},{7,71},{8,72},{9,... | collective-permute-start | bytes 442376 | tf_op jit(solution)/shard_map/ppermute | solution.py:498
  43.1 1.8 %collective-permute-start.5 = (f32[2,9,16,128]{3,2,1,0:T(8,128)S(1)}, f32[2,9,16,128]{3,2,1,0:T(8,128)S(1)}, u32[]{:S(2)}, u32[]{:S(2)}) collective-permute-start(f32[2,9,16,128]{3,2,1,0:T(8,128)S(1)} %get-tuple-element.37), channel_id=1, source_target_pairs={{0,96},{1,97},{2,98},{3,99},{4,100},{5,101},{6,102},{7,103},{8,104... | collective-permute-start | bytes 442376 | tf_op jit(solution)/shard_map/ppermute | solution.py:498
  44.9 2.0 %collective-permute-done.3.refs_1_ = f32[2,9,16,128]{3,2,1,0:T(8,128)S(1)} collective-permute-done((f32[2,9,16,128]{3,2,1,0:T(8,128)S(1)}, f32[2,9,16,128]{3,2,1,0:T(8,128)S(1)}, u32[]{:S(2)}, u32[]{:S(2)}) %collective-permute-start.3) | collective-permute-done | bytes 147488 | tf_op jit(solution)/shard_map/ppermute | solution.py:498
  46.9 3.1 %collective-permute-done.4.refs_2_ = f32[2,9,16,128]{3,2,1,0:T(8,128)S(1)} collective-permute-done((f32[2,9,16,128]{3,2,1,0:T(8,128)S(1)}, f32[2,9,16,128]{3,2,1,0:T(8,128)S(1)}, u32[]{:S(2)}, u32[]{:S(2)}) %collective-permute-start.4) | collective-permute-done | bytes 147488 | tf_op jit(solution)/shard_map/ppermute | solution.py:498
  50.0 2.6 %collective-permute-done.5.refs_3_ = f32[2,9,16,128]{3,2,1,0:T(8,128)S(1)} collective-permute-done((f32[2,9,16,128]{3,2,1,0:T(8,128)S(1)}, f32[2,9,16,128]{3,2,1,0:T(8,128)S(1)}, u32[]{:S(2)}, u32[]{:S(2)}) %collective-permute-start.5) | collective-permute-done | bytes 147488 | tf_op jit(solution)/shard_map/ppermute | solution.py:498
  52.5 1.1 %shard_map.108 = (f32[9,2,64,128]{3,2,1,0:T(8,128)}, f32[9,2,24,128]{3,2,1,0:T(8,128)S(1)}, f32[9,2,24,128]{3,2,1,0:T(8,128)S(1)}) custom-call(f32[2,9,16,128]{3,2,1,0:T(8,128)S(1)} %get-tuple-element.34.refs_0_, f32[2,9,16,128]{3,2,1,0:T(8,128)S(1)} %collective-permute-done.3.refs_1_, f32[2,9,16,128]{3,2,1,0:T(8,128)S(1)} %collective-permute-done.4.refs_2_, ...), custom_call_target="tpu_custom_call" | custom-call | tf_op jit(solution)/shard_map/pallas_call | solution.py:470
  53.6 1.1 %collective-permute-start.6 = (f32[9,2,24,128]{3,2,1,0:T(8,128)S(1)}, f32[9,2,24,128]{3,2,1,0:T(8,128)S(1)}, u32[]{:S(2)}, u32[]{:S(2)}) collective-permute-start(f32[9,2,24,128]{3,2,1,0:T(8,128)S(1)} %get-tuple-element.39), channel_id=1, source_target_pairs={{0,16},{1,17},{2,18},{3,19},{4,20},{5,21},{6,22},{7,23},{8,24},{9,... | collective-permute-start | bytes 663560 | tf_op jit(solution)/shard_map/ppermute | solution.py:492
  54.9 0.9 collective-permute-done.6.ra
  55.8 4.3 %collective-permute-done.7.rb = f32[9,2,24,128]{3,2,1,0:T(8,128)S(1)} collective-permute-done((f32[9,2,24,128]{3,2,1,0:T(8,128)S(1)}, f32[9,2,24,128]{3,2,1,0:T(8,128)S(1)}, u32[]{:S(2)}, u32[]{:S(2)}) %collective-permute-start.7) | collective-permute-done | bytes 221216 | tf_op jit(solution)/shard_map/ppermute | solution.py:491
  60.1 4.0 %shard_map.109 = (f32[4,3,2,112,128]{4,3,2,1,0:T(8,128)}, f32[4,3,2,112,128]{4,3,2,1,0:T(8,128)}, f32[4,3,2,112,128]{4,3,2,1,0:T(8,128)}, f32[3,2,112,128]{3,2,1,0:T(8,128)}, f32[3,2,112,128]{3,2,1,0:T(8,128)}) custom-call(f32[9,2,64,128]{3,2,1,0:T(8,128)} %get-tuple-element.38.center, f32[9,2,24,128]{3,2,1,0:T(8,128)S(1)} %collective-permute-done.6.ra, ...), custom_call_target="tpu_custom_call" | custom-call | tf_op jit(solution)/shard_map/pallas_call | solution.py:470
  64.1 6.4 %shard_map.110 = (f32[9,2,64,128]{3,2,1,0:T(8,128)S(1)}, f32[128,128]{1,0:T(8,128)S(1)}) custom-call(f32[4,3,2,40,128]{4,3,2,1,0:T(8,128)S(1)} %collective-permute-done.ra, f32[4,3,2,40,128]{4,3,2,1,0:T(8,128)S(1)} %collective-permute-done.1.rb, f32[4,3,2,64,128]{4,3,2,1,0:T(8,128)} %get-tuple-element.30.w_in, f32[4,3,2,64,128]{4,3,2,1,0:T(8,128)} %get-tuple-element.31.v_in, ...), custom_call_target="tpu_custom_call" | custom-call | tf_op jit(solution)/shard_map/pallas_call | solution.py:470
  70.7 3.4 %collective-permute-start.8 = (f32[4,9,16,128]{3,2,1,0:T(8,128)S(1)}, f32[4,9,16,128]{3,2,1,0:T(8,128)S(1)}, u32[]{:S(2)}, u32[]{:S(2)}) collective-permute-start(f32[4,9,16,128]{3,2,1,0:T(8,128)S(1)} %get-tuple-element.49), channel_id=1, source_target_pairs={{0,16},{1,17},{2,18},{3,19},{4,20},{5,21},{6,22},{7,23},{8,24},{9,... | collective-permute-start | bytes 884744 | tf_op jit(solution)/shard_map/ppermute | solution.py:498
  74.1 1.2 %collective-permute-done.8.got = f32[4,9,16,128]{3,2,1,0:T(8,128)S(1)} collective-permute-done((f32[4,9,16,128]{3,2,1,0:T(8,128)S(1)}, f32[4,9,16,128]{3,2,1,0:T(8,128)S(1)}, u32[]{:S(2)}, u32[]{:S(2)}) %collective-permute-start.8) | collective-permute-done | bytes 294944 | tf_op jit(solution)/shard_map/ppermute | solution.py:498
  75.8 1.8 %collective-permute-start.11 = (f32[9,32,128]{2,1,0:T(8,128)S(1)}, f32[9,32,128]{2,1,0:T(8,128)S(1)}, u32[]{:S(2)}, u32[]{:S(2)}) collective-permute-start(f32[9,32,128]{2,1,0:T(8,128)S(1)} %get-tuple-element.53), channel_id=1, source_target_pairs={{0,96},{1,97},{2,98},{3,99},{4,100},{5,101},{6,102},{7,103},{8,104... | collective-permute-start | bytes 442376 | tf_op jit(solution)/shard_map/ppermute | solution.py:498
  78.3 16.9 %all_to_all.16 = f32[128,1,128]{2,1,0:T(1,128)S(1)} all-to-all(f32[128,1,128]{2,1,0:T(1,128)S(1)} %bitcast.10), channel_id=1, replica_groups=mesh['lat'=8,'lon'=16] {'lat','lon'}, dimensions={0} | all-to-all | bytes 131072 | tf_op jit(solution)/shard_map/all_to_all | solution.py:578
  95.2 0.9 shard_map.113
  (13 shorter events, 2.0 us)
Async XLA Ops:
  5.2 25.5 %all-to-all-start = ((f32[128,8,128]{2,1,0:T(8,128)}), f32[128,8,128]{2,1,0:T(8,128)S(1)}, u32[]{:S(2)}, u32[]{:S(2)}) async-start(f32[128,8,128]{2,1,0:T(8,128)} %shard_map.104), calls=%async_computation | async-start | bytes 1048576 | tf_op jit(solution)/shard_map/all_to_all | solution.py:535
  18.8 22.1 %collective-permute-start.2 = (f32[4,9,16,128]{3,2,1,0:T(8,128)}, f32[4,9,16,128]{3,2,1,0:T(8,128)S(1)}, u32[]{:S(2)}, u32[]{:S(2)}) collective-permute-start(f32[4,9,16,128]{3,2,1,0:T(8,128)} %get-tuple-element.33), channel_id=1, source_target_pairs={{0,16},{1,17},{2,18},{3,19},{4,20},{5,21},{6,22},{7,23},{8,24},{9,... | collective-permute-start | bytes 884744 | tf_op jit(solution)/shard_map/ppermute | solution.py:498
  38.0 26.1 %collective-permute-start = (f32[4,3,2,40,128]{4,3,2,1,0:T(8,128)}, f32[4,3,2,40,128]{4,3,2,1,0:T(8,128)S(1)}, u32[]{:S(2)}, u32[]{:S(2)}) collective-permute-start(f32[4,3,2,40,128]{4,3,2,1,0:T(8,128)} %get-tuple-element.28), channel_id=1, source_target_pairs={{0,16},{1,17},{2,18},{3,19},{4,20},{5,21},{6,22},{7,23},{8,24},{9,... | collective-permute-start | bytes 1474568 | tf_op jit(solution)/shard_map/ppermute | solution.py:492
  39.6 24.5 %collective-permute-start.1 = (f32[4,3,2,40,128]{4,3,2,1,0:T(8,128)}, f32[4,3,2,40,128]{4,3,2,1,0:T(8,128)S(1)}, u32[]{:S(2)}, u32[]{:S(2)}) collective-permute-start(f32[4,3,2,40,128]{4,3,2,1,0:T(8,128)} %get-tuple-element.29), channel_id=1, source_target_pairs={{0,31},{1,16},{2,17},{3,18},{4,19},{5,20},{6,21},{7,22},{8,23},{9,... | collective-permute-start | bytes 1474568 | tf_op jit(solution)/shard_map/ppermute | solution.py:491
  41.0 5.9 %collective-permute-start.3 = (f32[2,9,16,128]{3,2,1,0:T(8,128)S(1)}, f32[2,9,16,128]{3,2,1,0:T(8,128)S(1)}, u32[]{:S(2)}, u32[]{:S(2)}) collective-permute-start(f32[2,9,16,128]{3,2,1,0:T(8,128)S(1)} %get-tuple-element.35), channel_id=1, source_target_pairs={{0,32},{1,33},{2,34},{3,35},{4,36},{5,37},{6,38},{7,39},{8,40},{9,... | collective-permute-start | bytes 442376 | tf_op jit(solution)/shard_map/ppermute | solution.py:498
  41.4 8.6 %collective-permute-start.4 = (f32[2,9,16,128]{3,2,1,0:T(8,128)S(1)}, f32[2,9,16,128]{3,2,1,0:T(8,128)S(1)}, u32[]{:S(2)}, u32[]{:S(2)}) collective-permute-start(f32[2,9,16,128]{3,2,1,0:T(8,128)S(1)} %get-tuple-element.36), channel_id=1, source_target_pairs={{0,64},{1,65},{2,66},{3,67},{4,68},{5,69},{6,70},{7,71},{8,72},{9,... | collective-permute-start | bytes 442376 | tf_op jit(solution)/shard_map/ppermute | solution.py:498
  43.1 9.4 %collective-permute-start.5 = (f32[2,9,16,128]{3,2,1,0:T(8,128)S(1)}, f32[2,9,16,128]{3,2,1,0:T(8,128)S(1)}, u32[]{:S(2)}, u32[]{:S(2)}) collective-permute-start(f32[2,9,16,128]{3,2,1,0:T(8,128)S(1)} %get-tuple-element.37), channel_id=1, source_target_pairs={{0,96},{1,97},{2,98},{3,99},{4,100},{5,101},{6,102},{7,103},{8,104... | collective-permute-start | bytes 442376 | tf_op jit(solution)/shard_map/ppermute | solution.py:498
  53.6 2.2 %collective-permute-start.6 = (f32[9,2,24,128]{3,2,1,0:T(8,128)S(1)}, f32[9,2,24,128]{3,2,1,0:T(8,128)S(1)}, u32[]{:S(2)}, u32[]{:S(2)}) collective-permute-start(f32[9,2,24,128]{3,2,1,0:T(8,128)S(1)} %get-tuple-element.39), channel_id=1, source_target_pairs={{0,16},{1,17},{2,18},{3,19},{4,20},{5,21},{6,22},{7,23},{8,24},{9,... | collective-permute-start | bytes 663560 | tf_op jit(solution)/shard_map/ppermute | solution.py:492
  54.7 5.4 %collective-permute-start.7 = (f32[9,2,24,128]{3,2,1,0:T(8,128)S(1)}, f32[9,2,24,128]{3,2,1,0:T(8,128)S(1)}, u32[]{:S(2)}, u32[]{:S(2)}) collective-permute-start(f32[9,2,24,128]{3,2,1,0:T(8,128)S(1)} %get-tuple-element.40), channel_id=1, source_target_pairs={{0,31},{1,16},{2,17},{3,18},{4,19},{5,20},{6,21},{7,22},{8,23},{9,... | collective-permute-start | bytes 663560 | tf_op jit(solution)/shard_map/ppermute | solution.py:491
  70.7 4.6 %collective-permute-start.8 = (f32[4,9,16,128]{3,2,1,0:T(8,128)S(1)}, f32[4,9,16,128]{3,2,1,0:T(8,128)S(1)}, u32[]{:S(2)}, u32[]{:S(2)}) collective-permute-start(f32[4,9,16,128]{3,2,1,0:T(8,128)S(1)} %get-tuple-element.49), channel_id=1, source_target_pairs={{0,16},{1,17},{2,18},{3,19},{4,20},{5,21},{6,22},{7,23},{8,24},{9,... | collective-permute-start | bytes 884744 | tf_op jit(solution)/shard_map/ppermute | solution.py:498
  75.6 19.6 %collective-permute-start.10 = (f32[9,32,128]{2,1,0:T(8,128)S(1)}, f32[9,32,128]{2,1,0:T(8,128)S(1)}, u32[]{:S(2)}, u32[]{:S(2)}) collective-permute-start(f32[9,32,128]{2,1,0:T(8,128)S(1)} %get-tuple-element.52), channel_id=1, source_target_pairs={{0,64},{1,65},{2,66},{3,67},{4,68},{5,69},{6,70},{7,71},{8,72},{9,... | collective-permute-start | bytes 442376 | tf_op jit(solution)/shard_map/ppermute | solution.py:498
  75.8 19.4 %collective-permute-start.11 = (f32[9,32,128]{2,1,0:T(8,128)S(1)}, f32[9,32,128]{2,1,0:T(8,128)S(1)}, u32[]{:S(2)}, u32[]{:S(2)}) collective-permute-start(f32[9,32,128]{2,1,0:T(8,128)S(1)} %get-tuple-element.53), channel_id=1, source_target_pairs={{0,96},{1,97},{2,98},{3,99},{4,100},{5,101},{6,102},{7,103},{8,104... | collective-permute-start | bytes 442376 | tf_op jit(solution)/shard_map/ppermute | solution.py:498
  77.6 17.6 %collective-permute-start.9 = (f32[9,32,128]{2,1,0:T(8,128)S(1)}, f32[9,32,128]{2,1,0:T(8,128)S(1)}, u32[]{:S(2)}, u32[]{:S(2)}) collective-permute-start(f32[9,32,128]{2,1,0:T(8,128)S(1)} %get-tuple-element.51), channel_id=1, source_target_pairs={{0,32},{1,33},{2,34},{3,35},{4,36},{5,37},{6,38},{7,39},{8,40},{9,... | collective-permute-start | bytes 442376 | tf_op jit(solution)/shard_map/ppermute | solution.py:498

commit v7 on v6

--- a/solution.py
+++ b/solution.py
@@ -15,8 +15,8 @@
 EDGE = 24
 EXT = COL + 2 * EDGE
 SLAB = 40
-ROOM = 256
-SEG = 64
+MOST = 256
+ROOM = 64
 GROUP = 4
 F32 = jnp.float32
 BF16 = jnp.bfloat16
@@ -158,9 +158,18 @@
     return out
 
 
-def pack_kernel(count, tile, cell, step, value, weight, out, rows, member, counted, acc, left, right):
+def line(x):
+    return jnp.broadcast_to(x, (16, 128)).astype(BF16)
+
+
+def times(hot, scale):
+    return (hot.reshape(-1, 16, 128) * scale[None]).reshape(-1, 128)
+
+
+def pack_kernel(count, first, tile, cell, step, value, weight, out, over, *scratch):
+    rows, member, counted, acc, left, right = scratch
     shape = (16, 128)
-    live = sublanes(shape) * 128 + lanes(shape) < count[0]
+    live = sublanes(shape) * 128 + lanes(shape) < jnp.broadcast_to(count[...], shape)
     c, t = cell[...], tile[...]
     level = c >> 12
     q = (level >= 3).astype(I32) + (level >= 6).astype(I32) + (level >= 9).astype(I32)
@@ -186,61 +195,49 @@
     square = (128, 256)
     before = ((sublanes(square) < lanes(square)) | (lanes(square) >= 128)).astype(F32).astype(BF16)
     ids = sublanes((128, 128)).astype(F32)
-    places = sublanes((ROOM, 128)).astype(F32)
     for b in range(16):
         at = slice(b * 128, b * 128 + 128)
-        mine = ids == rows[0, b : b + 1, :]
-        member[at, :] = jnp.where(mine, 1.0, 0.0).astype(BF16)
+        hot = jnp.where(ids == rows[0, b : b + 1, :], 1.0, 0.0).astype(BF16)
+        member[at, :] = hot
         for p in range(8):
-            piece = rows[1 + p, b : b + 1, :]
-            left[p * 128 : p * 128 + 128, at] = jnp.where(mine, piece, 0.0).astype(BF16)
+            left[p * 128 : p * 128 + 128, at] = times(hot, line(rows[1 + p, b : b + 1, :]))
     counted[...] = jnp.dot(member[...], before, preferred_element_type=F32)
     base = jnp.zeros((128, 128), F32)
+    place = (sublanes((ROOM, 128)) + jnp.broadcast_to(first[...], (ROOM, 128))).astype(F32)
     for b in range(16):
         at = slice(b * 128, b * 128 + 128)
         mine = ids == rows[0, b : b + 1, :]
         rank = jnp.where(mine, counted[at, :128] + base, 0.0)
         rank = jnp.sum(rank, axis=0, keepdims=True)
         base = base + counted[at, 128:]
-        right[:, at] = jnp.where(places == rank, 1.0, 0.0).astype(BF16)
+        hot = jnp.where(place == rank, 1.0, 0.0).astype(BF16)
+        right[:ROOM, at] = hot
+        right[ROOM:, at] = hot
     acc[...] = lax.dot_general(
         left[...], right[...], (((1,), (1,)), ((), ())), preferred_element_type=F32
     )
-    for ch, pieces in enumerate(((0, 1), (2,), (3, 4), (5, 6, 7))):
-        for hf in range(2):
-            at = slice(hf * 128, hf * 128 + 128)
-            out[:, 2 * ch + hf, :] = sum(acc[p * 128 : p * 128 + 128, at] for p in pieces)
+    part = lambda *pieces: sum(acc[p * 128 : p * 128 + 128, :] for p in pieces)
+    low = lanes((128, 128)) < ROOM
+    out[:, 0, :] = jnp.where(low, part(0, 1), part(2))
+    out[:, 1, :] = jnp.where(low, part(3, 4), part(5, 6, 7))
+    longest = jnp.max(jnp.max(base, axis=0, keepdims=True), axis=1, keepdims=True)
+    over[...] = jnp.broadcast_to(jnp.where(longest > ROOM, 1.0, 0.0), (8, 128))
 
 
 def scatter_kernel(x, wsum, vsum, sa, sb, xt, sorted_, at, bt, acc):
     h = half()
-    most = jnp.max(x[:, 2:4, :], axis=0)
-    total = jnp.sum(jnp.where(most > 0.5, 1.0, 0.0)).astype(I32)
     acc[...] = jnp.zeros_like(acc)
-    for ch in range(4):
-        xt[ch, :128] = x[:, 2 * ch, :].T
-
-    @pl.when(total > 128)
-    def _():
-        for ch in range(4):
-            xt[ch, 128:] = x[:, 2 * ch + 1, :].T
-
-    block = (SEG, 128)
+    for pair in range(2):
+        xt[pair] = x[:, pair, :].T
+    block = (ROOM, 128)
     place = sublanes(block)
-    square = (SEG, SEG)
+    square = (ROOM, ROOM)
     before = (lanes(square) < sublanes(square)).astype(F32).astype(BF16)
     row_ids = sublanes((LV * COL, 128))
     lat_ids = sublanes((256, 128))
 
-    def line(ref):
-        return jnp.broadcast_to(ref, (16, 128)).astype(BF16)
-
-    def times(hot, scale):
-        return (hot.reshape(-1, 16, 128) * scale[None]).reshape(-1, 128)
-
-    def segment(i, carry):
-        first = pl.multiple_of(i * SEG, SEG)
-        part = lambda ch: xt[ch, pl.ds(first, SEG), :]
+    def segment():
+        part = lambda ch: xt[ch // 2, ch % 2 * ROOM : ch % 2 * ROOM + ROOM, :]
         step = part(1)
         for k in range(STEPS):
             valid = jnp.where(step == k + 1.0, 1.0, 0.0)
@@ -250,10 +247,10 @@
             moved = [part(0), part(2), part(3)]
             for bit in (1, 2, 4, 8, 16, 32):
                 go = shift & bit
-                come = pltpu.roll(go, SEG - bit, 0) != 0
-                moved = [jnp.where(come, pltpu.roll(y, SEG - bit, 0), y) for y in moved]
+                come = pltpu.roll(go, ROOM - bit, 0) != 0
+                moved = [jnp.where(come, pltpu.roll(y, ROOM - bit, 0), y) for y in moved]
                 shift = jnp.where(
-                    come, pltpu.roll(shift, SEG - bit, 0), jnp.where(go != 0, 0, shift)
+                    come, pltpu.roll(shift, ROOM - bit, 0), jnp.where(go != 0, 0, shift)
                 )
             there = place < count.astype(I32)
             cell = moved[0].astype(I32)
@@ -281,10 +278,8 @@
                 return carry
 
             lax.fori_loop(0, (longest + GROUP - 1) // GROUP, group, 0)
-        return carry
-
-    lax.fori_loop(0, (total + SEG - 1) // SEG, segment, 0)
-    low = sublanes((8, 128)) < 4
+
+    segment()
     for k in range(STEPS):
         for l in range(LV):
             for u in range(2):
@@ -297,11 +292,24 @@
                 v = take(2) + take(3) + take(4)
                 wsum[k, l, u] = w
                 vsum[k, l, u] = v
-                mix = jnp.where(low, w[16:24], pltpu.roll(v[16:24], 4, 0))
-                lo = jnp.concatenate([w[:16], v[:16], mix], axis=0)
-                mix = jnp.where(low, pltpu.roll(v[40:48], 4, 0), w[40:48])
-                hi = jnp.concatenate([w[48:], v[48:], mix], axis=0)
-                put_edges(sa, sb, (k, l, u), lo, hi, h)
+                put_slabs(sa, sb, (k, l, u), w, v, h)
+
+
+def put_slabs(sa, sb, index, w, v, h):
+    low = sublanes((8, 128)) < 4
+    mix = jnp.where(low, w[16:24], pltpu.roll(v[16:24], 4, 0))
+    lo = jnp.concatenate([w[:16], v[:16], mix], axis=0)
+    mix = jnp.where(low, pltpu.roll(v[40:48], 4, 0), w[40:48])
+    hi = jnp.concatenate([w[48:], v[48:], mix], axis=0)
+    put_edges(sa, sb, index, lo, hi, h)
+
+
+def slab_kernel(wsum, vsum, sa, sb):
+    h = half()
+    for k in range(STEPS):
+        for l in range(LV):
+            for u in range(2):
+                put_slabs(sa, sb, (k, l, u), wsum[k, l, u], vsum[k, l, u], h)
 
 
 def fetch(sources, buffers, sems):
@@ -331,7 +339,7 @@
 
 
 def core_kernel(
-    ra, rb, w_in, v_in, states_in, gains_in, drifts_in, cn_in, cs_in, out, table_ref, *scratch
+    over, ra, rb, w_in, v_in, states_in, gains_in, drifts_in, cn_in, cs_in, out, table_ref, *scratch
 ):
     *buffers, sems = scratch
     h = half()
@@ -407,6 +415,7 @@
     for i in range(5):
         whole = jnp.sum(jnp.sum(sums[i], axis=0, keepdims=True), axis=1, keepdims=True)
         table = jnp.where(lane == i, whole, table)
+    table = jnp.where(lane == 5, over[:1], table)
     table_ref[...] = jnp.broadcast_to(table, (ALL, 128))
 
 
@@ -502,36 +511,107 @@
     return [blocks[0]] + [flip(blocks[t], 2 * t) for t in range(1, 4)]
 
 
+def pack(observed):
+    return call(
+        pack_kernel,
+        [(ALL, 2, 128), (8, 128)],
+        *observed,
+        ins="h" * 7,
+        scratch=[
+            pltpu.VMEM((9, 16, 128), F32),
+            pltpu.VMEM((2048, 128), BF16),
+            pltpu.VMEM((2048, 256), F32),
+            pltpu.VMEM((1024, 128), F32),
+            pltpu.VMEM((1024, 2048), BF16),
+            pltpu.VMEM((128, 2048), BF16),
+        ],
+    )
+
+
+def scatter(arrived):
+    return call(
+        scatter_kernel,
+        [(STEPS, LV, 2, COL, 128)] * 2 + [(STEPS, LV, 2, SLAB, 128)] * 2,
+        arrived,
+        space="hhvv",
+        scratch=[
+            pltpu.VMEM((2, 128, 128), F32),
+            pltpu.VMEM((7, ROOM, 128), F32),
+            pltpu.VMEM((5 * LV * COL, GROUP * 128), BF16),
+            pltpu.VMEM((256, GROUP * 128), BF16),
+            pltpu.VMEM((STEPS * 5 * LV * COL, 256), F32),
+        ],
+    )
+
+
+BOTH = ("lat", "lon")
+PLANE = (LV, 2, EXT, 128)
+MIDDLE = (LV, 2, COL, 128)
+SPLIT = (4, 9, 16, 128)
+
+
+def solve(over, wsum, vsum, wa, wb, coefs):
+    big = pltpu.VMEM((STEPS,) + PLANE, F32)
+    mid = pltpu.VMEM((STEPS,) + MIDDLE, F32)
+    small = pltpu.VMEM(PLANE, F32)
+    vectors, table = call(
+        core_kernel,
+        [(9, 2, COL, 128), (ALL, 128)],
+        over,
+        wa,
+        wb,
+        wsum,
+        vsum,
+        *coefs,
+        ins="vvv" + "a" * 7,
+        scratch=[mid, mid, big, big, big, small, small, pltpu.SemaphoreType.DMA((LV, 7))],
+    )
+    keep, give = call(turn_kernel, [SPLIT] * 2, vectors)
+    got = flip(give, 1)
+    parts = lax.all_to_all(table, BOTH, 0, 0, tiled=True)
+    blocks = ring(call(merge_out_kernel, [(9, 32, 128)] * 4, keep, got))
+    increment, residual = call(
+        final_kernel, [(12, 32, 128)] * 2, parts, *blocks, space="h"
+    )
+    return increment, residual, parts
+
+
+def every_window(observed, coefs):
+    def window(i, sums):
+        first = jnp.full((1, 1), i * ROOM, I32)
+        packed, _ = pack(observed[:1] + (first,) + observed[2:])
+        arrived = lax.all_to_all(packed, BOTH, 0, 0, tiled=True)
+        w, v, _, _ = scatter(arrived)
+        return sums[0] + w, sums[1] + v
+
+    zeros = jnp.zeros((STEPS,) + MIDDLE, F32)
+    wsum, vsum = lax.fori_loop(0, MOST // ROOM, window, (zeros, zeros))
+    sa, sb = call(slab_kernel, [(STEPS, LV, 2, SLAB, 128)] * 2, wsum, vsum, ins="hh")
+    wa, wb = swap(sa, sb)
+    increment, residual, _ = solve(jnp.zeros((8, 128), F32), wsum, vsum, wa, wb, coefs)
+    return increment, residual
+
+
 def on_device(
     background, wind_lon, wind_lat, obs_value, obs_weight, obs_tile, obs_cell, obs_step, obs_count
 ):
     both = ("lat", "lon")
     plane = (LV, 2, EXT, 128)
-    middle = (LV, 2, COL, 128)
 
     group = (4, 9, 16, 128)
     keep, give = call(prep_kernel, [group] * 2, background, wind_lon, wind_lat, ins="hhh")
     got = flip(give, 1)
     fold = lambda a: a.reshape(16, 128)
-    packed = call(
-        pack_kernel,
-        [(ALL, 8, 128)],
-        obs_count,
+    observed = (
+        obs_count.reshape(1, 1),
+        jnp.zeros((1, 1), I32),
         fold(obs_tile),
         fold(obs_cell),
         fold(obs_step),
         fold(obs_value),
         fold(obs_weight),
-        ins="shhhhh",
-        scratch=[
-            pltpu.VMEM((9, 16, 128), F32),
-            pltpu.VMEM((2048, 128), BF16),
-            pltpu.VMEM((2048, 256), F32),
-            pltpu.VMEM((1024, 256), F32),
-            pltpu.VMEM((1024, 2048), BF16),
-            pltpu.VMEM((256, 2048), BF16),
-        ],
-    )
+    )
+    packed, over = pack(observed)
     arrived = lax.all_to_all(packed, both, 0, 0, tiled=True)
     blocks = ring(call(merge_in_kernel, [(2, 9, 16, 128)] * 4, keep, got))
     fields, sa, sb = call(
@@ -542,42 +622,16 @@
         scratch=[pltpu.VMEM((9, 128, 128), F32)],
     )
     ra, rb = swap(sa, sb)
-    wsum, vsum, sa, sb = call(
-        scatter_kernel,
-        [(STEPS,) + middle] * 2 + [(STEPS, LV, 2, SLAB, 128)] * 2,
-        arrived,
-        space="hhvv",
-        scratch=[
-            pltpu.VMEM((4, 256, 128), F32),
-            pltpu.VMEM((7, SEG, 128), F32),
-            pltpu.VMEM((5 * LV * COL, GROUP * 128), BF16),
-            pltpu.VMEM((256, GROUP * 128), BF16),
-            pltpu.VMEM((STEPS * 5 * LV * COL, 256), F32),
-        ],
-    )
+    wsum, vsum, sa, sb = scatter(arrived)
     wa, wb = swap(sa, sb)
     coefs = call(
         forward_kernel, [(STEPS,) + plane] * 3 + [plane] * 2, fields, ra, rb, ins="hvv", space="h"
     )
-    big = pltpu.VMEM((STEPS,) + plane, F32)
-    mid = pltpu.VMEM((STEPS,) + middle, F32)
-    small = pltpu.VMEM(plane, F32)
-    vectors, table = call(
-        core_kernel,
-        [(9, 2, COL, 128), (ALL, 128)],
-        wa,
-        wb,
-        wsum,
-        vsum,
-        *coefs,
-        ins="vv" + "a" * 7,
-        scratch=[mid, mid, big, big, big, small, small, pltpu.SemaphoreType.DMA((LV, 7))],
-    )
-    keep, give = call(turn_kernel, [group] * 2, vectors)
-    got = flip(give, 1)
-    parts = lax.all_to_all(table, both, 0, 0, tiled=True)
-    blocks = ring(call(merge_out_kernel, [(9, 32, 128)] * 4, keep, got))
-    return call(final_kernel, [(12, 32, 128)] * 2, parts, *blocks, space="h")
+    increment, residual, parts = solve(over, wsum, vsum, wa, wb, coefs)
+    crowded = jnp.sum(parts[:, 5]) > 0.5
+    return lax.cond(
+        crowded, lambda: every_window(observed, coefs), lambda: (increment, residual)
+    )
 
 
 def solution(mesh):

time: 96.4 us -> 87.9 us (0.912)
  starting transfers between devices: 26.8 us -> 19.1 us
  waiting for transfers between devices: 25 us -> 20.9 us
  blocking collectives: 16.9 us -> 20.4 us
  Pallas kernels: 26.1 us -> 24.4 us
    all_to_all x1, starting transfers between devices: 11.5 us -> 4.13 us  [solve(): parts = lax.all_to_all(table, BOTH, 0, 0, tiled=True)]
    all_to_all x1, waiting for transfers between devices: 10.9 us -> 5.55 us  [solve(): parts = lax.all_to_all(table, BOTH, 0, 0, tiled=True)]
    all_to_all x1, blocking collectives: 16.9 us -> 20.4 us  [on_device(): arrived = lax.all_to_all(packed, both, 0, 0, tiled=True)]
    pallas_call x10, Pallas kernels: 26.1 us -> 24.4 us  [call(): return make(kernel, shapes, ins, scratch)(*args)]
    ppermute x8, waiting for transfers between devices: 8.84 us -> 10 us  [flip(): return lax.ppermute(x, ('lat', 'lon'), pairs)]
  transfers between devices with their start and end apart: 13 -> 13, of which waited for: 7 -> 6; matrix products, arithmetic and copies ran while one was open for 0% -> 1% of each run, Pallas kernels for 15% -> 17%
where the time goes in v7:
time: 87.9 us; the launch traced here: 87.6 us
  Pallas kernels  24.4 us (28%)
  waiting for transfers between devices  20.9 us (24%)
  blocking collectives  20.4 us (23%)
  starting transfers between devices  19.1 us (22%)
  between operations  2.02 us (2%)
    pallas_call x10, Pallas kernels, call(): return make(kernel, shapes, ins, scratch)(*args)  24.4 us
    all_to_all x1, blocking collectives, on_device(): arrived = lax.all_to_all(packed, both, 0, 0, tiled=True)  20.4 us
    ppermute x8, starting transfers between devices, flip(): return lax.ppermute(x, ('lat', 'lon'), pairs)  11.6 us
    ppermute x8, waiting for transfers between devices, flip(): return lax.ppermute(x, ('lat', 'lon'), pairs)  10 us
    all_to_all x1, waiting for transfers between devices, solve(): parts = lax.all_to_all(table, BOTH, 0, 0, tiled=True)  5.55 us
    ppermute x2, waiting for transfers between devices, swap(): rb = lax.ppermute(sb, ('lat', 'lon'), far)  4.26 us
    all_to_all x1, starting transfers between devices, solve(): parts = lax.all_to_all(table, BOTH, 0, 0, tiled=True)  4.13 us
    ppermute x2, starting transfers between devices, swap(): ra = lax.ppermute(sa, ('lat', 'lon'), near)  2.03 us
  transfers between devices with their start and end apart: 13, of which 6 were waited for; matrix products, arithmetic and copies ran while one was open for 1% of the time, Pallas kernels for 17%

profile of v7, /device:TPU:1, one launch (start us, length us, event | category | flops | bytes accessed | tf_op | source)
XLA Modules:
  0.0 87.6 jit_solution(1120458331113959723)
XLA Ops:
  0.6 1.3 %shard_map.110 = (f32[4,9,16,128]{3,2,1,0:T(8,128)S(1)}, f32[4,9,16,128]{3,2,1,0:T(8,128)S(1)}) custom-call(f32[12,32,128]{2,1,0:T(8,128)} %bg.1, f32[12,32,128]{2,1,0:T(8,128)} %wl.1, f32[12,32,128]{2,1,0:T(8,128)} %wt.1), custom_call_target="tpu_custom_call" | custom-call | tf_op jit(solution)/shard_map/pallas_call | solution.py:479
  2.0 1.5 %collective-permute-start.8 = (f32[4,9,16,128]{3,2,1,0:T(8,128)S(1)}, f32[4,9,16,128]{3,2,1,0:T(8,128)S(1)}, u32[]{:S(2)}, u32[]{:S(2)}) collective-permute-start(f32[4,9,16,128]{3,2,1,0:T(8,128)S(1)} %get-tuple-element.230), channel_id=1, source_target_pairs={{0,16},{1,17},{2,18},{3,19},{4,20},{5,21},{6,22},{7,23},{8,24},{9,... | collective-permute-start | bytes 884744 | tf_op jit(solution)/shard_map/ppermute | solution.py:507
  4.1 2.9 %shard_map.108 = (f32[128,2,128]{2,1,0:T(2,128)S(1)}, f32[8,128]{1,0:T(8,128)S(1)}) custom-call(s32[1,1]{1,0:T(1,128)} %bitcast.17.count, s32[1,1]{1,0:T(1,128)} %constant.24.clone.1.first, s32[16,128]{1,0:T(8,128)} %bitcast.22, s32[16,128]{1,0:T(8,128)} %bitcast.24, s32[16,128]{1,0:T(8,128)} %bitcast.26, f32[16,128]{1,0:T(8,128)} %bitcast.28, ...), custom_call_target="tpu_custom_call" | custom-call | tf_op jit(solution)/shard_map/pallas_call | solution.py:479
  7.0 20.4 %all_to_all.32.x = f32[128,2,128]{2,1,0:T(2,128)S(1)} all-to-all(f32[128,2,128]{2,1,0:T(2,128)S(1)} %get-tuple-element.224), channel_id=1, replica_groups=mesh['lat'=8,'lon'=16] {'lat','lon'}, dimensions={0} | all-to-all | bytes 262144 | tf_op jit(solution)/shard_map/all_to_all | solution.py:615
  27.4 7.1 %shard_map.109 = (f32[4,3,2,64,128]{4,3,2,1,0:T(8,128)}, f32[4,3,2,64,128]{4,3,2,1,0:T(8,128)}, f32[4,3,2,40,128]{4,3,2,1,0:T(8,128)}, f32[4,3,2,40,128]{4,3,2,1,0:T(8,128)}) custom-call(f32[128,2,128]{2,1,0:T(2,128)S(1)} %all_to_all.32.x), custom_call_target="tpu_custom_call" | custom-call | tf_op jit(solution)/shard_map/pallas_call | solution.py:479
  34.5 1.5 %collective-permute-start.6 = (f32[4,3,2,40,128]{4,3,2,1,0:T(8,128)}, f32[4,3,2,40,128]{4,3,2,1,0:T(8,128)S(1)}, u32[]{:S(2)}, u32[]{:S(2)}) collective-permute-start(f32[4,3,2,40,128]{4,3,2,1,0:T(8,128)} %get-tuple-element.225), channel_id=1, source_target_pairs={{0,16},{1,17},{2,18},{3,19},{4,20},{5,21},{6,22},{7,23},{8,24},{9,... | collective-permute-start | bytes 1474568 | tf_op jit(solution)/shard_map/ppermute | solution.py:501
  36.0 1.3 %collective-permute-start.7 = (f32[4,3,2,40,128]{4,3,2,1,0:T(8,128)}, f32[4,3,2,40,128]{4,3,2,1,0:T(8,128)S(1)}, u32[]{:S(2)}, u32[]{:S(2)}) collective-permute-start(f32[4,3,2,40,128]{4,3,2,1,0:T(8,128)} %get-tuple-element.226), channel_id=1, source_target_pairs={{0,31},{1,16},{2,17},{3,18},{4,19},{5,20},{6,21},{7,22},{8,23},{9,... | collective-permute-start | bytes 1474568 | tf_op jit(solution)/shard_map/ppermute | solution.py:500
  37.3 0.6 collective-permute-start.10
  38.0 2.2 %collective-permute-start.11 = (f32[2,9,16,128]{3,2,1,0:T(8,128)S(1)}, f32[2,9,16,128]{3,2,1,0:T(8,128)S(1)}, u32[]{:S(2)}, u32[]{:S(2)}) collective-permute-start(f32[2,9,16,128]{3,2,1,0:T(8,128)S(1)} %get-tuple-element.234), channel_id=1, source_target_pairs={{0,96},{1,97},{2,98},{3,99},{4,100},{5,101},{6,102},{7,103},{8,104... | collective-permute-start | bytes 442376 | tf_op jit(solution)/shard_map/ppermute | solution.py:507
  40.1 4.3 %collective-permute-done.10.refs_2_ = f32[2,9,16,128]{3,2,1,0:T(8,128)S(1)} collective-permute-done((f32[2,9,16,128]{3,2,1,0:T(8,128)S(1)}, f32[2,9,16,128]{3,2,1,0:T(8,128)S(1)}, u32[]{:S(2)}, u32[]{:S(2)}) %collective-permute-start.10) | collective-permute-done | bytes 147488 | tf_op jit(solution)/shard_map/ppermute | solution.py:507
  44.4 3.4 %collective-permute-done.11.refs_3_ = f32[2,9,16,128]{3,2,1,0:T(8,128)S(1)} collective-permute-done((f32[2,9,16,128]{3,2,1,0:T(8,128)S(1)}, f32[2,9,16,128]{3,2,1,0:T(8,128)S(1)}, u32[]{:S(2)}, u32[]{:S(2)}) %collective-permute-start.11) | collective-permute-done | bytes 147488 | tf_op jit(solution)/shard_map/ppermute | solution.py:507
  47.9 1.1 %shard_map.112 = (f32[9,2,64,128]{3,2,1,0:T(8,128)}, f32[9,2,24,128]{3,2,1,0:T(8,128)S(1)}, f32[9,2,24,128]{3,2,1,0:T(8,128)S(1)}) custom-call(f32[2,9,16,128]{3,2,1,0:T(8,128)S(1)} %get-tuple-element.231.refs_0_, f32[2,9,16,128]{3,2,1,0:T(8,128)S(1)} %collective-permute-done.9.refs_1_, f32[2,9,16,128]{3,2,1,0:T(8,128)S(1)} %collective-permute-done.10.refs_2_, ...), custom_call_target="tpu_custom_call" | custom-call | tf_op jit(solution)/shard_map/pallas_call | solution.py:479
  49.5 1.1 %collective-permute-done.12.ra = f32[9,2,24,128]{3,2,1,0:T(8,128)S(1)} collective-permute-done((f32[9,2,24,128]{3,2,1,0:T(8,128)S(1)}, f32[9,2,24,128]{3,2,1,0:T(8,128)S(1)}, u32[]{:S(2)}, u32[]{:S(2)}) %collective-permute-start.12) | collective-permute-done | bytes 221216 | tf_op jit(solution)/shard_map/ppermute | solution.py:501
  50.6 4.3 %collective-permute-done.13.rb = f32[9,2,24,128]{3,2,1,0:T(8,128)S(1)} collective-permute-done((f32[9,2,24,128]{3,2,1,0:T(8,128)S(1)}, f32[9,2,24,128]{3,2,1,0:T(8,128)S(1)}, u32[]{:S(2)}, u32[]{:S(2)}) %collective-permute-start.13) | collective-permute-done | bytes 221216 | tf_op jit(solution)/shard_map/ppermute | solution.py:500
  54.8 3.7 %shard_map.113 = (f32[4,3,2,112,128]{4,3,2,1,0:T(8,128)S(1)}, f32[4,3,2,112,128]{4,3,2,1,0:T(8,128)}, f32[4,3,2,112,128]{4,3,2,1,0:T(8,128)}, f32[3,2,112,128]{3,2,1,0:T(8,128)S(1)}, f32[3,2,112,128]{3,2,1,0:T(8,128)}) custom-call(f32[9,2,64,128]{3,2,1,0:T(8,128)} %get-tuple-element.235.center, f32[9,2,24,128]{3,2,1,0:T(8,128)S(1)} %collective-permute-done.12.ra, ...), custom_call_target="tpu_custom_call" | custom-call | tf_op jit(solution)/shard_map/pallas_call | solution.py:479
  58.5 6.9 %shard_map.114 = (f32[9,2,64,128]{3,2,1,0:T(8,128)S(1)}, f32[128,128]{1,0:T(8,128)}) custom-call(f32[8,128]{1,0:T(8,128)S(1)} %get-tuple-element.223.over, f32[4,3,2,40,128]{4,3,2,1,0:T(8,128)S(1)} %collective-permute-done.6.ra, f32[4,3,2,40,128]{4,3,2,1,0:T(8,128)S(1)} %collective-permute-done.7.rb, f32[4,3,2,64,128]{4,3,2,1,0:T(8,128)} %get-tuple-element.227.w_in, ...), custom_call_target="tpu_custom_call" | custom-call | tf_op jit(solution)/shard_map/pallas_call | solution.py:479
  65.7 3.4 %collective-permute-start.14 = (f32[4,9,16,128]{3,2,1,0:T(8,128)S(1)}, f32[4,9,16,128]{3,2,1,0:T(8,128)S(1)}, u32[]{:S(2)}, u32[]{:S(2)}) collective-permute-start(f32[4,9,16,128]{3,2,1,0:T(8,128)S(1)} %get-tuple-element.246), channel_id=1, source_target_pairs={{0,16},{1,17},{2,18},{3,19},{4,20},{5,21},{6,22},{7,23},{8,24},{9,... | collective-permute-start | bytes 884744 | tf_op jit(solution)/shard_map/ppermute | solution.py:507
  69.1 4.1 %all-to-all-start.3 = ((f32[128,1,128]{2,1,0:T(1,128)}), f32[128,1,128]{2,1,0:T(1,128)S(1)}, u32[]{:S(2)}, u32[]{:S(2)}) async-start(f32[128,1,128]{2,1,0:T(1,128)} %bitcast.11), calls=%async_computation.3 | async-start | bytes 131072 | tf_op jit(solution)/shard_map/all_to_all | solution.py:571
  73.5 1.4 %collective-permute-start.15 = (f32[9,32,128]{2,1,0:T(8,128)S(1)}, f32[9,32,128]{2,1,0:T(8,128)S(1)}, u32[]{:S(2)}, u32[]{:S(2)}) collective-permute-start(f32[9,32,128]{2,1,0:T(8,128)S(1)} %get-tuple-element.248), channel_id=1, source_target_pairs={{0,32},{1,33},{2,34},{3,35},{4,36},{5,37},{6,38},{7,39},{8,40},{9,... | collective-permute-start | bytes 442376 | tf_op jit(solution)/shard_map/ppermute | solution.py:507
  74.9 2.4 %collective-permute-start.16 = (f32[9,32,128]{2,1,0:T(8,128)S(1)}, f32[9,32,128]{2,1,0:T(8,128)S(1)}, u32[]{:S(2)}, u32[]{:S(2)}) collective-permute-start(f32[9,32,128]{2,1,0:T(8,128)S(1)} %get-tuple-element.249), channel_id=1, source_target_pairs={{0,64},{1,65},{2,66},{3,67},{4,68},{5,69},{6,70},{7,71},{8,72},{9,... | collective-permute-start | bytes 442376 | tf_op jit(solution)/shard_map/ppermute | solution.py:507
  77.4 5.5 %all-to-all-done.3 = f32[128,1,128]{2,1,0:T(1,128)S(1)} async-done(((f32[128,1,128]{2,1,0:T(1,128)}), f32[128,1,128]{2,1,0:T(1,128)S(1)}, u32[]{:S(2)}, u32[]{:S(2)}) %all-to-all-start.3) | async-done | bytes 65568 | tf_op jit(solution)/shard_map/all_to_all | solution.py:571
  83.0 0.7 slice_reduce_fusion
  84.3 2.3 %collective-permute-done.17.refs_3_ = f32[9,32,128]{2,1,0:T(8,128)S(1)} collective-permute-done((f32[9,32,128]{2,1,0:T(8,128)S(1)}, f32[9,32,128]{2,1,0:T(8,128)S(1)}, u32[]{:S(2)}, u32[]{:S(2)}) %collective-permute-start.17) | collective-permute-done | bytes 147488 | tf_op jit(solution)/shard_map/ppermute | solution.py:507
  86.6 0.9 %shard_map.117 = (f32[12,32,128]{2,1,0:T(8,128)}, f32[12,32,128]{2,1,0:T(8,128)}) custom-call(f32[128,128]{1,0:T(8,128)S(1)} %bitcast.19, f32[9,32,128]{2,1,0:T(8,128)S(1)} %get-tuple-element.247.refs_0_, f32[9,32,128]{2,1,0:T(8,128)S(1)} %collective-permute-done.15.refs_1_, f32[9,32,128]{2,1,0:T(8,128)S(1)} %collective-permute-done.16.refs_2_, ...), custom_call_target="tpu_custom_call" | custom-call | tf_op jit(solution)/shard_map/pallas_call | solution.py:479
  (15 shorter events, 1.2 us)
Async XLA Ops:
  2.0 35.3 %collective-permute-start.8 = (f32[4,9,16,128]{3,2,1,0:T(8,128)S(1)}, f32[4,9,16,128]{3,2,1,0:T(8,128)S(1)}, u32[]{:S(2)}, u32[]{:S(2)}) collective-permute-start(f32[4,9,16,128]{3,2,1,0:T(8,128)S(1)} %get-tuple-element.230), channel_id=1, source_target_pairs={{0,16},{1,17},{2,18},{3,19},{4,20},{5,21},{6,22},{7,23},{8,24},{9,... | collective-permute-start | bytes 884744 | tf_op jit(solution)/shard_map/ppermute | solution.py:507
  34.5 24.0 %collective-permute-start.6 = (f32[4,3,2,40,128]{4,3,2,1,0:T(8,128)}, f32[4,3,2,40,128]{4,3,2,1,0:T(8,128)S(1)}, u32[]{:S(2)}, u32[]{:S(2)}) collective-permute-start(f32[4,3,2,40,128]{4,3,2,1,0:T(8,128)} %get-tuple-element.225), channel_id=1, source_target_pairs={{0,16},{1,17},{2,18},{3,19},{4,20},{5,21},{6,22},{7,23},{8,24},{9,... | collective-permute-start | bytes 1474568 | tf_op jit(solution)/shard_map/ppermute | solution.py:501
  36.0 22.5 %collective-permute-start.7 = (f32[4,3,2,40,128]{4,3,2,1,0:T(8,128)}, f32[4,3,2,40,128]{4,3,2,1,0:T(8,128)S(1)}, u32[]{:S(2)}, u32[]{:S(2)}) collective-permute-start(f32[4,3,2,40,128]{4,3,2,1,0:T(8,128)} %get-tuple-element.226), channel_id=1, source_target_pairs={{0,31},{1,16},{2,17},{3,18},{4,19},{5,20},{6,21},{7,22},{8,23},{9,... | collective-permute-start | bytes 1474568 | tf_op jit(solution)/shard_map/ppermute | solution.py:500
  37.3 7.1 %collective-permute-start.10 = (f32[2,9,16,128]{3,2,1,0:T(8,128)S(1)}, f32[2,9,16,128]{3,2,1,0:T(8,128)S(1)}, u32[]{:S(2)}, u32[]{:S(2)}) collective-permute-start(f32[2,9,16,128]{3,2,1,0:T(8,128)S(1)} %get-tuple-element.233), channel_id=1, source_target_pairs={{0,64},{1,65},{2,66},{3,67},{4,68},{5,69},{6,70},{7,71},{8,72},{9,... | collective-permute-start | bytes 442376 | tf_op jit(solution)/shard_map/ppermute | solution.py:507
  38.0 9.9 %collective-permute-start.11 = (f32[2,9,16,128]{3,2,1,0:T(8,128)S(1)}, f32[2,9,16,128]{3,2,1,0:T(8,128)S(1)}, u32[]{:S(2)}, u32[]{:S(2)}) collective-permute-start(f32[2,9,16,128]{3,2,1,0:T(8,128)S(1)} %get-tuple-element.234), channel_id=1, source_target_pairs={{0,96},{1,97},{2,98},{3,99},{4,100},{5,101},{6,102},{7,103},{8,104... | collective-permute-start | bytes 442376 | tf_op jit(solution)/shard_map/ppermute | solution.py:507
  40.1 7.7 %collective-permute-start.9 = (f32[2,9,16,128]{3,2,1,0:T(8,128)S(1)}, f32[2,9,16,128]{3,2,1,0:T(8,128)S(1)}, u32[]{:S(2)}, u32[]{:S(2)}) collective-permute-start(f32[2,9,16,128]{3,2,1,0:T(8,128)S(1)} %get-tuple-element.232), channel_id=1, source_target_pairs={{0,32},{1,33},{2,34},{3,35},{4,36},{5,37},{6,38},{7,39},{8,40},{9,... | collective-permute-start | bytes 442376 | tf_op jit(solution)/shard_map/ppermute | solution.py:507
  49.0 1.6 %collective-permute-start.12 = (f32[9,2,24,128]{3,2,1,0:T(8,128)S(1)}, f32[9,2,24,128]{3,2,1,0:T(8,128)S(1)}, u32[]{:S(2)}, u32[]{:S(2)}) collective-permute-start(f32[9,2,24,128]{3,2,1,0:T(8,128)S(1)} %get-tuple-element.236), channel_id=1, source_target_pairs={{0,16},{1,17},{2,18},{3,19},{4,20},{5,21},{6,22},{7,23},{8,24},{9,... | collective-permute-start | bytes 663560 | tf_op jit(solution)/shard_map/ppermute | solution.py:501
  49.5 5.4 %collective-permute-start.13 = (f32[9,2,24,128]{3,2,1,0:T(8,128)S(1)}, f32[9,2,24,128]{3,2,1,0:T(8,128)S(1)}, u32[]{:S(2)}, u32[]{:S(2)}) collective-permute-start(f32[9,2,24,128]{3,2,1,0:T(8,128)S(1)} %get-tuple-element.237), channel_id=1, source_target_pairs={{0,31},{1,16},{2,17},{3,18},{4,19},{5,20},{6,21},{7,22},{8,23},{9,... | collective-permute-start | bytes 663560 | tf_op jit(solution)/shard_map/ppermute | solution.py:500
  65.7 7.6 %collective-permute-start.14 = (f32[4,9,16,128]{3,2,1,0:T(8,128)S(1)}, f32[4,9,16,128]{3,2,1,0:T(8,128)S(1)}, u32[]{:S(2)}, u32[]{:S(2)}) collective-permute-start(f32[4,9,16,128]{3,2,1,0:T(8,128)S(1)} %get-tuple-element.246), channel_id=1, source_target_pairs={{0,16},{1,17},{2,18},{3,19},{4,20},{5,21},{6,22},{7,23},{8,24},{9,... | collective-permute-start | bytes 884744 | tf_op jit(solution)/shard_map/ppermute | solution.py:507
  69.1 13.9 %all-to-all-start.3 = ((f32[128,1,128]{2,1,0:T(1,128)}), f32[128,1,128]{2,1,0:T(1,128)S(1)}, u32[]{:S(2)}, u32[]{:S(2)}) async-start(f32[128,1,128]{2,1,0:T(1,128)} %bitcast.11), calls=%async_computation.3 | async-start | bytes 131072 | tf_op jit(solution)/shard_map/all_to_all | solution.py:571
  73.5 10.8 %collective-permute-start.15 = (f32[9,32,128]{2,1,0:T(8,128)S(1)}, f32[9,32,128]{2,1,0:T(8,128)S(1)}, u32[]{:S(2)}, u32[]{:S(2)}) collective-permute-start(f32[9,32,128]{2,1,0:T(8,128)S(1)} %get-tuple-element.248), channel_id=1, source_target_pairs={{0,32},{1,33},{2,34},{3,35},{4,36},{5,37},{6,38},{7,39},{8,40},{9,... | collective-permute-start | bytes 442376 | tf_op jit(solution)/shard_map/ppermute | solution.py:507
  74.9 9.4 %collective-permute-start.16 = (f32[9,32,128]{2,1,0:T(8,128)S(1)}, f32[9,32,128]{2,1,0:T(8,128)S(1)}, u32[]{:S(2)}, u32[]{:S(2)}) collective-permute-start(f32[9,32,128]{2,1,0:T(8,128)S(1)} %get-tuple-element.249), channel_id=1, source_target_pairs={{0,64},{1,65},{2,66},{3,67},{4,68},{5,69},{6,70},{7,71},{8,72},{9,... | collective-permute-start | bytes 442376 | tf_op jit(solution)/shard_map/ppermute | solution.py:507
  77.3 9.3 %collective-permute-start.17 = (f32[9,32,128]{2,1,0:T(8,128)S(1)}, f32[9,32,128]{2,1,0:T(8,128)S(1)}, u32[]{:S(2)}, u32[]{:S(2)}) collective-permute-start(f32[9,32,128]{2,1,0:T(8,128)S(1)} %get-tuple-element.250), channel_id=1, source_target_pairs={{0,96},{1,97},{2,98},{3,99},{4,100},{5,101},{6,102},{7,103},{8,104... | collective-permute-start | bytes 442376 | tf_op jit(solution)/shard_map/ppermute | solution.py:507
